TPU v7x, 32 devices: a whole 2x2x4 slice. The times are simulated.
32 devices in a mesh: groups: 1, leaf: 32 (over z, y, x, core).
Axes of the slice: x: 2, y: 2, z: 4, core: 2. Of those that a mesh axis runs over, the one named last changes fastest.
Arguments:
- embeddings: bfloat16 [768, 65536], P(None, ('groups', 'leaf')), may hold values from -4 to 4
- probes: bfloat16 [32, 65536], P(None, ('groups', 'leaf')), may hold values from -1.75 to 1.75
- order: int32 [32, 2048], P(('groups', 'leaf')), may hold values from 0 to 2047, each once within a row
- near_list: int32 [256, 7], P(('groups', 'leaf')), may hold values from 0 to 255, as said below
- near_count: int32 [32, 8], P(('groups', 'leaf')), may hold values from 1 to 7, 32 in all within a row
- skeleton: int32 [30, 64], P('groups'), may hold values from 0 to 65535, as said below
- core: float32 [30, 64, 64], P('groups'), may hold values from -8 to 8
Outputs:
- values: float32 [32, 65536], P(None, ('groups', 'leaf'))
Inputs may be any that keep to these rules, and one draw needn't show every extreme that they name: `near_list`: slot 0 of leaf t holds t; every slot of leaf t holds a leaf within 3 of t. `near_count`: each row sums to 32, and its largest entry is 7. `skeleton`: entry r of node n lies among the examples of node n, in the r-th of 64 equal parts of them. `order`: each row is a permutation.
All inputs are finite; a program needn't handle non-finite values.
Results may differ from a plain program's by a relative error of at most 0.0042.
Values may be sent and summed in bfloat16 or wider, within the bound.
No kernel may reach another device: no remote copies, remote signals or barrier semaphores. Data moves between devices by JAX's collectives and lax.ppermute only.
A program may use at most 128 MiB of HBM per device.

v0:
```python
import jax
import jax.numpy as jnp
from jax import lax
from jax.sharding import PartitionSpec as P

LEAF = 256
R = 64
LEVELS = 4
W = 3
NEAR = 7


def with_halo(block, sides, width):
    for axis, dim in sides:
        count = lax.axis_size(axis)
        forward = [(i, i + 1) for i in range(count - 1)]
        backward = [(target, source) for source, target in forward]
        low = lax.ppermute(
            lax.slice_in_dim(block, block.shape[dim] - width, None, axis=dim), axis, forward
        )
        high = lax.ppermute(lax.slice_in_dim(block, 0, width, axis=dim), axis, backward)
        block = jnp.concatenate([low, block, high], axis=dim)
    return block


def kernel_matrix(left_emb, left_norm, right_emb, right_norm):
    inner = lax.dot_general(
        left_emb, right_emb, (((0,), (0,)), ((), ())), preferred_element_type=jnp.float32
    )
    distance = left_norm[:, None] + right_norm[None, :] - 2.0 * inner
    return jnp.exp(-0.5 * distance).astype(jnp.bfloat16)


def leaf_kernels(source_emb, source_norm, target_emb, target_norm):
    inner = jnp.einsum("eia,eib->iab", source_emb, target_emb, preferred_element_type=jnp.float32)
    distance = source_norm[:, :, None] + target_norm[:, None, :] - 2.0 * inner
    return jnp.exp(-0.5 * distance).astype(jnp.bfloat16)


def column_norms(columns):
    return jnp.sum(jnp.square(columns.astype(jnp.float32)), axis=0)


def body(embeddings, probes, order, near_list, near_count, skeleton, core):
    axis_devices = lax.axis_size("leaf")
    tree_bits = axis_devices.bit_length() - 1
    position = lax.axis_index("leaf")
    width_e = embeddings.shape[0]
    dev_points = embeddings.shape[1]
    dev_leaves = dev_points // LEAF
    x_tree = probes[:, order[0]]
    probe_cols = x_tree.shape[0]
    norms = column_norms(embeddings)
    stacked = jnp.concatenate([embeddings, x_tree], axis=0)
    padded = with_halo(stacked, (("leaf", 1),), W * LEAF)
    pad_blocks = padded.reshape(padded.shape[0], dev_leaves + 2 * W, LEAF)
    pad_emb = pad_blocks[:width_e]
    pad_x = pad_blocks[width_e:]
    pad_norm = jnp.sum(jnp.square(pad_emb.astype(jnp.float32)), axis=0)
    own_emb = embeddings.reshape(width_e, dev_leaves, LEAF)
    own_norm = norms.reshape(dev_leaves, LEAF)
    local_pos = near_list - position * dev_leaves + W
    counts = near_count[0]
    near_sum = jnp.zeros((probe_cols, dev_leaves, LEAF), jnp.float32)
    for slot_id in range(NEAR):
        sources = local_pos[:, slot_id]
        kernel_vals = leaf_kernels(
            jnp.take(pad_emb, sources, axis=1),
            jnp.take(pad_norm, sources, axis=0),
            own_emb,
            own_norm,
        )
        terms = jnp.einsum(
            "pia,iab->pib",
            jnp.take(pad_x, sources, axis=1),
            kernel_vals,
            preferred_element_type=jnp.float32,
        )
        near_sum = near_sum + jnp.where((slot_id < counts)[None, :, None], terms, 0.0)
    level_bits = [tree_bits - 1 - level_id for level_id in range(LEVELS)]
    own_nodes = [
        2 ** (level_id + 1) - 2 + jnp.right_shift(position, level_bits[level_id])
        for level_id in range(LEVELS)
    ]
    partner_nodes = [
        2 ** (level_id + 1)
        - 2
        + jnp.bitwise_xor(jnp.right_shift(position, level_bits[level_id]), 1)
        for level_id in range(LEVELS)
    ]
    start_point = position * dev_points
    slot_counts = [R * 2 ** (level_id + 1) // axis_devices for level_id in range(LEVELS)]
    slot_starts = [sum(slot_counts[:level_id]) for level_id in range(LEVELS)]
    picks = []
    for level_id in range(LEVELS):
        node_row = lax.dynamic_index_in_dim(skeleton, own_nodes[level_id], 0, keepdims=False)
        within = jnp.bitwise_and(position, (1 << level_bits[level_id]) - 1)
        point_ids = lax.dynamic_slice_in_dim(
            node_row, within * slot_counts[level_id], slot_counts[level_id]
        )
        picks.append(jnp.take(embeddings, point_ids - start_point, axis=1))
    owned = jnp.concatenate(picks, axis=1)
    gathered = lax.all_gather(owned, "leaf", axis=1, tiled=True)
    gathered = gathered.reshape(width_e, axis_devices, owned.shape[1])
    own_parts = []
    part_parts = []
    for level_id in range(LEVELS):
        first_node = 2 ** (level_id + 1) - 2
        level_cols = gathered[
            :, :, slot_starts[level_id] : slot_starts[level_id] + slot_counts[level_id]
        ]
        level_cols = level_cols.reshape(width_e, axis_devices * slot_counts[level_id])
        own_parts.append(
            lax.dynamic_slice_in_dim(level_cols, (own_nodes[level_id] - first_node) * R, R, axis=1)
        )
        part_parts.append(
            lax.dynamic_slice_in_dim(
                level_cols, (partner_nodes[level_id] - first_node) * R, R, axis=1
            )
        )
    own_cols = jnp.concatenate(own_parts, axis=1)
    part_cols = jnp.concatenate(part_parts, axis=1)
    own_sums = jnp.dot(
        x_tree,
        kernel_matrix(embeddings, norms, own_cols, column_norms(own_cols)),
        preferred_element_type=jnp.float32,
    )
    node_terms = jnp.zeros((probe_cols, skeleton.shape[0] * R), jnp.float32)
    for level_id in range(LEVELS):
        node_terms = lax.dynamic_update_slice_in_dim(
            node_terms,
            own_sums[:, level_id * R : (level_id + 1) * R],
            own_nodes[level_id] * R,
            axis=1,
        )
    node_totals = lax.psum(node_terms, "leaf")
    partner_sums = [
        lax.dynamic_slice_in_dim(node_totals, partner_nodes[level_id] * R, R, axis=1)
        for level_id in range(LEVELS)
    ]
    weights = []
    for level_id in range(LEVELS):
        core_part = lax.dynamic_index_in_dim(core, partner_nodes[level_id], 0, keepdims=False)
        weights.append(
            jnp.dot(partner_sums[level_id], core_part, precision=lax.Precision.HIGHEST).astype(
                jnp.bfloat16
            )
        )
    far_kernel = kernel_matrix(part_cols, column_norms(part_cols), embeddings, norms)
    far_sum = jnp.dot(
        jnp.concatenate(weights, axis=1), far_kernel, preferred_element_type=jnp.float32
    )
    tree_values = near_sum.reshape(probe_cols, dev_points) + far_sum
    return jnp.zeros_like(tree_values).at[:, order[0]].set(tree_values)


def solution(mesh):
    return jax.shard_map(
        body,
        mesh=mesh,
        in_specs=(
            P(None, ("groups", "leaf")),
            P(None, ("groups", "leaf")),
            P(("groups", "leaf"), None),
            P(("groups", "leaf"), None),
            P(("groups", "leaf"), None),
            P("groups", None),
            P("groups", None, None),
        ),
        out_specs=P(None, ("groups", "leaf")),
        check_vma=False,
    )
```

profile of v0, /device:TPU:24, one launch (start us, length us, event | category | flops | bytes accessed | tf_op | source)
XLA Modules:
  0.0 335.2 jit_solution(11105078149921155437)
XLA Ops:
  10.7 4.6 %copy.41 = bf16[768,2048]{0,1:T(8,128)(2,1)} copy(bf16[768,2048]{1,0:T(8,128)(2,1)} %param.13) | data formatting | bytes 6291456 | tf_op args[0]
  15.4 2.9 gather_fusion.1
  18.3 2.9 gather_fusion.2
  21.2 2.9 gather_fusion.3
  24.1 2.9 gather_fusion.4
  28.4 6.2 %gather_fusion = bf16[2048,32]{1,0:T(8,128)(2,1)S(1)} fusion(bf16[32,2048]{0,1:T(8,128)(2,1)S(1)} %copy.40, s32[2048]{0:T(1024)S(1)} %broadcast_clamp_fusion), kind=kCustom, calls=%fused_computation.21 | custom fusion | bytes 270336 | tf_op jit(solution)/shard_map/gather | solution.py:51
  34.6 3.0 pad_maximum_fusion.4
  37.6 2.5 copy.43
  40.1 3.8 %collective-permute-start.1 = (bf16[800,768]{1,0:T(8,128)(2,1)}, bf16[800,768]{1,0:T(8,128)(2,1)}, u32[]{:S(2)}, u32[]{:S(2)}) collective-permute-start(bf16[800,768]{1,0:T(8,128)(2,1)} %copy.43), channel_id=1, source_target_pairs={{1,0},{2,1},{3,2},{4,3},{5,4},{6,5},{7,6},{8,7},{9,8},{10,9},{11,1... | collective-permute-start | bytes 3686408 | tf_op jit(solution)/shard_map/ppermute | solution.py:21
  43.9 1.5 copy.42
  45.4 2.1 collective-permute-start
  47.6 2.6 multiply_reduce_fusion.1
  50.5 10.8 %collective-permute-done.1 = bf16[800,768]{1,0:T(8,128)(2,1)} collective-permute-done((bf16[800,768]{1,0:T(8,128)(2,1)}, bf16[800,768]{1,0:T(8,128)(2,1)}, u32[]{:S(2)}, u32[]{:S(2)}) %collective-permute-start.1) | collective-permute-done | bytes 1228832 | tf_op jit(solution)/shard_map/ppermute | solution.py:21
  61.3 1.8 copy.45
  63.0 6.9 %collective-permute-done = bf16[800,768]{1,0:T(8,128)(2,1)} collective-permute-done((bf16[800,768]{1,0:T(8,128)(2,1)}, bf16[800,768]{1,0:T(8,128)(2,1)}, u32[]{:S(2)}, u32[]{:S(2)}) %collective-permute-start) | collective-permute-done | bytes 1228832 | tf_op jit(solution)/shard_map/ppermute | solution.py:18
  69.9 2.5 copy.44
  72.4 6.6 %multiply_reduce_fusion = (f32[3584]{0:T(1024)S(1)}, bf16[768,3584]{0,1:T(8,128)(2,1)}) fusion(bf16[800,768]{0,1:T(8,128)(2,1)S(1)} %copy.45, bf16[32,2048]{0,1:T(8,128)(2,1)S(1)} %bitcast.279, bf16[768,2048]{0,1:T(8,128)(2,1)} %copy.41, bf16[800,768]{0,1:T(8,128)(2,1)} %copy.44), kind=kLoop, calls=%fused_computation.27 | loop fusion | flops 30274048 | bytes 11253760 | tf_op jit(solution)/shard_map/reduce_sum | solution.py:59
  79.0 2.1 pad_maximum_fusion.5
  81.1 1.5 copy.50
  90.5 8.2 %copy.46 = bf16[768,14,256]{2,0,1:T(8,128)(2,1)} copy(bf16[768,14,256]{0,2,1:T(8,128)(2,1)} %bitcast.269) | data formatting | bytes 11010048 | tf_op jit(solution)/shard_map/slice | solution.py:57
  98.7 5.1 %gather_fusion.6 = bf16[8,768,256]{2,1,0:T(8,128)(2,1)} fusion(bf16[768,14,256]{2,0,1:T(8,128)(2,1)} %copy.46, s32[1024]{0:T(1024)S(1)} %pad_clamp_fusion.10), kind=kCustom, calls=%fused_computation.1.clone | custom fusion | bytes 6291488 | tf_op jit(solution)/shard_map/jit(_take)/gather | solution.py:68
  103.7 4.9 %gather_fusion.9 = bf16[8,768,256]{2,1,0:T(8,128)(2,1)} fusion(bf16[768,14,256]{2,0,1:T(8,128)(2,1)} %copy.46, s32[1024]{0:T(1024)S(1)} %pad_clamp_fusion.9), kind=kCustom, calls=%fused_computation.9.clone | custom fusion | bytes 6291488 | tf_op jit(solution)/shard_map/jit(_take)/gather | solution.py:68
  108.7 4.9 %gather_fusion.12 = bf16[8,768,256]{2,1,0:T(8,128)(2,1)} fusion(bf16[768,14,256]{2,0,1:T(8,128)(2,1)} %copy.46, s32[1024]{0:T(1024)S(1)} %pad_clamp_fusion.8), kind=kCustom, calls=%fused_computation.10.clone | custom fusion | bytes 6291488 | tf_op jit(solution)/shard_map/jit(_take)/gather | solution.py:68
  113.6 5.0 %gather_fusion.15 = bf16[8,768,256]{2,1,0:T(8,128)(2,1)} fusion(bf16[768,14,256]{2,0,1:T(8,128)(2,1)} %copy.46, s32[1024]{0:T(1024)S(1)} %pad_clamp_fusion.7), kind=kCustom, calls=%fused_computation.11.clone | custom fusion | bytes 6291488 | tf_op jit(solution)/shard_map/jit(_take)/gather | solution.py:68
  118.6 5.0 %gather_fusion.18 = bf16[8,768,256]{2,1,0:T(8,128)(2,1)} fusion(bf16[768,14,256]{2,0,1:T(8,128)(2,1)} %copy.46, s32[1024]{0:T(1024)S(1)} %pad_clamp_fusion.6), kind=kCustom, calls=%fused_computation.12.clone | custom fusion | bytes 6291488 | tf_op jit(solution)/shard_map/jit(_take)/gather | solution.py:68
  123.6 5.1 %gather_fusion.21 = bf16[8,768,256]{2,1,0:T(8,128)(2,1)} fusion(bf16[768,14,256]{2,0,1:T(8,128)(2,1)} %copy.46, s32[1024]{0:T(1024)S(1)} %pad_clamp_fusion.5), kind=kCustom, calls=%fused_computation.13.clone | custom fusion | bytes 6291488 | tf_op jit(solution)/shard_map/jit(_take)/gather | solution.py:68
  128.7 5.0 %gather_fusion.24 = bf16[8,768,256]{2,1,0:T(8,128)(2,1)} fusion(bf16[768,14,256]{2,0,1:T(8,128)(2,1)} %copy.46, s32[1024]{0:T(1024)S(1)} %pad_clamp_fusion.4), kind=kCustom, calls=%fused_computation.14.clone | custom fusion | bytes 6291488 | tf_op jit(solution)/shard_map/jit(_take)/gather | solution.py:68
  134.2 3.9 %fusion.181 = f32[8,256,32]{1,2,0:T(8,128)S(1)} fusion(bf16[8,768,256]{2,1,0:T(8,128)(2,1)} %gather_fusion.6, pred[8]{0:T(512)(128)(4,1)S(1)} %get-tuple-element.58, f32[8,256]{1,0:T(8,128)S(1)} %add.373, f32[8,256]{1,0:T(8,128)S(1)} %broadcast_select_fusion.6, bf16[96,8,8,256]{3,2,1,0:T(8,128)(2,1)} %bitcast.270, ...), kind=kOutput, calls=%fused_computation.117 | convolution fusion | flops 843186176 | bytes 6701072 | tf_op jit(solution)/shard_map/pia,iab->pib/dot_general | solution.py:73
  138.1 3.9 %fusion.176 = f32[8,256,32]{1,2,0:T(8,128)S(1)} fusion(f32[8,256,32]{1,2,0:T(8,128)S(1)} %fusion.181, bf16[8,768,256]{2,1,0:T(8,128)(2,1)} %gather_fusion.9, pred[8]{0:T(512)(128)(4,1)S(1)} %get-tuple-element.57, f32[8,256]{1,0:T(8,128)S(1)} %broadcast_select_fusion.5, f32[8,256]{1,0:T(8,128)S(1)} %add.373, bf16[96,8,8,256]{3,2,1,0:T(8,128)(2,1)} %bitcast.271, ...), kind=kOutput, calls=%fused_computation.116 | convolution fusion | flops 843251712 | bytes 6963216 | tf_op jit(solution)/shard_map/pia,iab->pib/dot_general | solution.py:73
  142.0 3.9 %fusion.166 = f32[8,256,32]{1,2,0:T(8,128)S(1)} fusion(f32[8,256,32]{1,2,0:T(8,128)S(1)} %fusion.176, bf16[8,768,256]{2,1,0:T(8,128)(2,1)} %gather_fusion.12, pred[8]{0:T(512)(128)(4,1)S(1)} %get-tuple-element.56, f32[8,256]{1,0:T(8,128)S(1)} %broadcast_select_fusion.4, f32[8,256]{1,0:T(8,128)S(1)} %add.373, bf16[96,8,8,256]{3,2,1,0:T(8,128)(2,1)} %bitcast.272, ...), kind=kOutput, calls=%fused_computation.114 | convolution fusion | flops 843251712 | bytes 6963216 | tf_op jit(solution)/shard_map/pia,iab->pib/dot_general | solution.py:73
  145.9 3.9 %fusion.156 = f32[8,256,32]{1,2,0:T(8,128)S(1)} fusion(f32[8,256,32]{1,2,0:T(8,128)S(1)} %fusion.166, bf16[8,768,256]{2,1,0:T(8,128)(2,1)} %gather_fusion.15, pred[8]{0:T(512)(128)(4,1)S(1)} %get-tuple-element.55, f32[8,256]{1,0:T(8,128)S(1)} %broadcast_select_fusion.3, f32[8,256]{1,0:T(8,128)S(1)} %add.373, bf16[96,8,8,256]{3,2,1,0:T(8,128)(2,1)} %bitcast.273, ...), kind=kOutput, calls=%fused_computation.112 | convolution fusion | flops 843251712 | bytes 6963216 | tf_op jit(solution)/shard_map/pia,iab->pib/dot_general | solution.py:73
  149.8 3.9 %fusion.146 = f32[8,256,32]{1,2,0:T(8,128)S(1)} fusion(f32[8,256,32]{1,2,0:T(8,128)S(1)} %fusion.156, bf16[8,768,256]{2,1,0:T(8,128)(2,1)} %gather_fusion.18, pred[8]{0:T(512)(128)(4,1)S(1)} %get-tuple-element.54, f32[8,256]{1,0:T(8,128)S(1)} %broadcast_select_fusion.2, f32[8,256]{1,0:T(8,128)S(1)} %add.373, bf16[96,8,8,256]{3,2,1,0:T(8,128)(2,1)} %bitcast.274, ...), kind=kOutput, calls=%fused_computation.110 | convolution fusion | flops 843251712 | bytes 6963216 | tf_op jit(solution)/shard_map/pia,iab->pib/dot_general | solution.py:73
  153.7 5.2 %fusion.136 = f32[8,256,32]{1,2,0:T(8,128)} fusion(f32[8,256,32]{1,2,0:T(8,128)S(1)} %fusion.146, bf16[8,768,256]{2,1,0:T(8,128)(2,1)} %gather_fusion.21, pred[8]{0:T(512)(128)(4,1)S(1)} %get-tuple-element.53, f32[8,256]{1,0:T(8,128)S(1)} %broadcast_select_fusion.1, f32[8,256]{1,0:T(8,128)S(1)} %add.373, bf16[96,8,8,256]{3,2,1,0:T(8,128)(2,1)} %bitcast.275, ...), kind=kOutput, calls=%fused_computation.108 | convolution fusion | flops 843251712 | bytes 6963216 | tf_op jit(solution)/shard_map/pia,iab->pib/dot_general | solution.py:73
  158.9 5.3 %reshape.494 = bf16[1920,768]{1,0:T(8,128)(2,1)} reshape(bf16[32,60,768]{2,1,0:T(8,128)(2,1)} %all-gather.3.cloned.1.call-done) | data formatting | bytes 5898240
  164.2 5.3 %reshape.251 = bf16[768,32,60]{0,2,1:T(8,128)(2,1)} reshape(bf16[768,1920]{0,1:T(8,128)(2,1)} %bitcast.277) | data formatting | bytes 5898240 | tf_op jit(solution)/shard_map/reshape | solution.py:104
  169.5 1.0 slice.136
  170.5 1.3 slice_bitcast_fusion
  171.8 1.5 slice.138
  173.3 3.4 %slice.139 = bf16[768,32,32]{0,2,1:T(8,128)(2,1)} slice(bf16[768,32,60]{0,2,1:T(8,128)(2,1)} %reshape.251), slice={[0:768], [0:32], [28:60]} | slice | bytes 3145728 | tf_op jit(solution)/shard_map/slice | solution.py:109
  176.9 1.0 constant_dynamic-slice_fusion.4
  178.1 3.3 fusion.52
  183.9 3.9 %fusion.126 = f32[8,4,8,256]{3,2,1,0:T(8,128)S(1)} fusion(f32[8,256,32]{1,2,0:T(8,128)S(1)} %copy-done.5, bf16[8,768,256]{2,1,0:T(8,128)(2,1)} %gather_fusion.24, pred[8]{0:T(512)(128)(4,1)S(1)} %get-tuple-element.52, f32[8,256]{1,0:T(8,128)S(1)} %broadcast_select_fusion, f32[8,256]{1,0:T(8,128)S(1)} %add.373, bf16[96,8,8,256]{3,2,1,0:T(8,128)(2,1)} %bitcast.276, ...), kind=kOutput, calls=%fused_computation.106 | convolution fusion | flops 843251712 | bytes 6963216 | tf_op jit(solution)/shard_map/pia,iab->pib/dot_general | solution.py:73
  187.9 126.2 %all-reduce.2.cloned.1.call-done = f32[32,1920]{1,0:T(8,128)} async-done(((f32[32,1920]{1,0:T(8,128)}), f32[32,1920]{1,0:T(8,128)}) %all-reduce.2.cloned.1.call-update) | async-done | bytes 245776 | tf_op jit(solution)/shard_map/psum | solution.py:136
  315.0 1.0 convolution_convert_fusion.1
  316.0 0.9 convolution_convert_fusion.2
  317.9 3.2 fusion.44
  321.5 5.8 %scatter_custom_fusion = f32[32,2048]{0,1:T(8,128)S(1)} fusion(s32[2048]{0:T(1024)S(1)} %bitcast.286, f32[2048,32]{1,0:T(8,128)S(1)} %copy.80, f32[]{:T(128)} %constant.201.clone.1), kind=kCustom, calls=%fused_computation.168 | custom fusion | bytes 262148 | tf_op jit(solution)/shard_map/scatter | solution.py:154
  327.3 1.0 copy.81
  (93 shorter events, 19.0 us)
Async XLA Ops:
  6.5 307.6 %copy-start = (f32[30,64,64]{2,1,0:T(8,128)S(1)}, f32[30,64,64]{2,1,0:T(8,128)}, u32[]{:S(2)}) copy-start(f32[30,64,64]{2,1,0:T(8,128)} %param.19) | copy-start | bytes 1474564
  6.5 152.4 %all-gather.3.cloned.1.call-start = ((), (), s32[]{:S(2)}) async-start(), calls=%async_computation.1 | async-start | bytes 3244032 | tf_op jit(solution)/shard_map/all_gather | solution.py:103
  18.2 9.8 %copy-start.3 = (s32[1,2048]{1,0:T(1,128)S(1)}, s32[1,2048]{1,0:T(1,128)}, u32[]{:S(2)}) copy-start(s32[1,2048]{1,0:T(1,128)} %param.15) | copy-start | bytes 24580
  18.3 9.9 %copy-start.2 = (bf16[32,2048]{1,0:T(8,128)(2,1)S(1)}, bf16[32,2048]{1,0:T(8,128)(2,1)}, u32[]{:S(2)}) copy-start(bf16[32,2048]{1,0:T(8,128)(2,1)} %param.14) | copy-start | bytes 393220
  28.0 286.1 %all-reduce.2.cloned.1.call-start = ((), (), s32[]{:S(2)}) async-start(), calls=%async_computation | async-start | bytes 491520 | tf_op jit(solution)/shard_map/psum | solution.py:136
  40.1 10.3 %copy-start.4 = (s32[1,8]{1,0:T(1,128)S(1)}, s32[1,8]{1,0:T(1,128)}, u32[]{:S(2)}) copy-start(s32[1,8]{1,0:T(1,128)} %param.17) | copy-start | bytes 100
  40.1 21.2 %collective-permute-start.1 = (bf16[800,768]{1,0:T(8,128)(2,1)}, bf16[800,768]{1,0:T(8,128)(2,1)}, u32[]{:S(2)}, u32[]{:S(2)}) collective-permute-start(bf16[800,768]{1,0:T(8,128)(2,1)} %copy.43), channel_id=1, source_target_pairs={{1,0},{2,1},{3,2},{4,3},{5,4},{6,5},{7,6},{8,7},{9,8},{10,9},{11,1... | collective-permute-start | bytes 3686408 | tf_op jit(solution)/shard_map/ppermute | solution.py:21
  45.4 24.5 %collective-permute-start = (bf16[800,768]{1,0:T(8,128)(2,1)}, bf16[800,768]{1,0:T(8,128)(2,1)}, u32[]{:S(2)}, u32[]{:S(2)}) collective-permute-start(bf16[800,768]{1,0:T(8,128)(2,1)} %copy.42), channel_id=1, source_target_pairs={{0,1},{1,2},{2,3},{3,4},{4,5},{5,6},{6,7},{7,8},{8,9},{9,10},{10,1... | collective-permute-start | bytes 3686408 | tf_op jit(solution)/shard_map/ppermute | solution.py:18
  178.1 5.8 %copy-start.5 = (f32[8,256,32]{1,2,0:T(8,128)S(1)}, f32[8,256,32]{1,2,0:T(8,128)}, u32[]{:S(2)}) copy-start(f32[8,256,32]{1,2,0:T(8,128)} %fusion.136) | copy-start | bytes 786436
  183.1 0.7 copy-start.1
Sparse Core Ops, SparseCore 0:
  28.2 65.5 all-gather.2
  184.0 130.0 all-reduce.1
where the time goes:
time: 339 us; the launch traced here: 335 us
  waiting for transfers between devices  144 us (42%)
  local copies, waits for them, and re-layouts  112 us (33%)
  matrix products  38.9 us (11%)
  other arithmetic  20.1 us (6%)
  between operations  14.1 us (4%)
  starting transfers between devices  5.94 us (2%)
    psum x1, waiting for transfers between devices, body(): node_totals = lax.psum(node_terms, 'leaf')  126 us
    gather x7, local copies, waits for them, and re-layouts, body(): jnp.take(pad_emb, sources, axis=1)  35 us
    dot_general x7, matrix products, body(): jnp.einsum('pia,iab->pib', jnp.take(pad_x, sources, axis=1), kernel_vals,...  28.6 us
    gather x4, local copies, waits for them, and re-layouts, body(): picks.append(jnp.take(embeddings, point_ids - start_point, axis=1))  11.6 us
    unnamed x15, local copies, waits for them, and re-layouts  10.9 us
    ppermute x1, waiting for transfers between devices, with_halo(): lax.ppermute(lax.slice_in_dim(block, 0, width, axis=dim), axis, backward)  10.8 us
    slice x1, local copies, waits for them, and re-layouts, body(): pad_emb = pad_blocks[:width_e]  8.18 us
    scatter x2, local copies, waits for them, and re-layouts, body(): return jnp.zeros_like(tree_values).at[:, order[0]].set(tree_values)  6.86 us
  transfers between devices with their start and end apart: 4, of which 3 were waited for; matrix products, arithmetic and copies ran while one was open for 33% of the time, Pallas kernels for 0%

commit v1 on v0

v1 whole, which is shorter than its diff:
```python
import jax
import jax.numpy as jnp
from jax import lax
from jax.experimental import pallas as pl
from jax.experimental.pallas import tpu as pltpu
from jax.sharding import PartitionSpec as P

LEAF = 256
R = 64
LEVELS = 4
W = 3
F32 = jnp.float32
BF16 = jnp.bfloat16
VMEM_LIMIT = 48 * 1024 * 1024


def dot(a, b):
    return jnp.dot(a, b, preferred_element_type=F32)


def dot_nt(a, b):
    return lax.dot_general(a, b, (((1,), (1,)), ((), ())), preferred_element_type=F32)


def dot_tn(a, b):
    return lax.dot_general(a, b, (((0,), (0,)), ((), ())), preferred_element_type=F32)


def half_norm_row(emb):
    e = emb.astype(F32)
    return 0.5 * jnp.sum(e * e, axis=0, keepdims=True)


def half_norm_col(rows):
    e = rows.astype(F32)
    return 0.5 * jnp.sum(e * e, axis=1, keepdims=True)


def call(kernel, outs, *args, scratch=(), smem=(), flops=0, nbytes=0, name=None):
    single = not isinstance(outs, (list, tuple))
    vm = pl.BlockSpec(memory_space=pltpu.VMEM)
    sm = pl.BlockSpec(memory_space=pltpu.SMEM)
    res = pl.pallas_call(
        kernel,
        out_shape=outs,
        in_specs=[sm if i in smem else vm for i in range(len(args))],
        out_specs=vm if single else [vm] * len(outs),
        scratch_shapes=list(scratch),
        compiler_params=pltpu.CompilerParams(vmem_limit_bytes=VMEM_LIMIT),
        cost_estimate=pl.CostEstimate(flops=flops, bytes_accessed=nbytes, transcendentals=0),
        name=name,
    )(*args)
    return res


class Plan:
    def __init__(self, n):
        self.n = n
        self.bits = n.bit_length() - 1
        self.slots = [R * 2 ** (l + 1) // n for l in range(LEVELS)]
        self.padded = [-(-s // 8) * 8 for s in self.slots]
        self.starts = [sum(self.padded[:l]) for l in range(LEVELS)]
        self.rows = sum(self.padded)
        self.shift = [self.bits - 1 - l for l in range(LEVELS)]
        entries, size = [], 0
        for bit in reversed(range(self.bits)):
            level = self.bits - 1 - bit
            if level < LEVELS:
                entries.append((level, 0, size))
                size += self.padded[level]
            entries += [(lev, off ^ (1 << bit), row + size) for lev, off, row in entries]
            size *= 2
        self.entries, self.size = entries, size


def body(embeddings, probes, order, near_list, near_count, skeleton, core):
    n = lax.axis_size("leaf")
    plan = Plan(n)
    pos = lax.axis_index("leaf")
    width, points = embeddings.shape
    cols = probes.shape[0]
    leaves = points // LEAF
    halo = W * LEAF

    def pick_kernel(skel_ref, emb_ref, g_ref, row_ref):
        me = lax.axis_index("leaf")
        lane = lax.broadcasted_iota(jnp.int32, (1, 128), 1)
        idx = jnp.full((1, 128), -1, jnp.int32)
        row_ref[...] = jnp.zeros_like(row_ref)
        for l in range(LEVELS):
            node = 2 ** (l + 1) - 2 + jnp.right_shift(me, plan.shift[l])
            row_ref[0:1, 0:R] = skel_ref[pl.ds(node, 1), :]
            within = jnp.bitwise_and(me, (1 << plan.shift[l]) - 1)
            shift = jnp.bitwise_and(plan.starts[l] - within * plan.slots[l] + 128, 127)
            rolled = pltpu.roll(row_ref[...], shift, 1)[0:1, :]
            mine = (lane >= plan.starts[l]) & (lane < plan.starts[l] + plan.slots[l])
            idx = jnp.where(mine, rolled - me * points, idx)
        acc = jnp.zeros((width, 128), F32)
        for c in range(points // LEAF):
            at = lax.broadcasted_iota(jnp.int32, (LEAF, 128), 0) + c * LEAF
            hot = jnp.where(at == idx, 1.0, 0.0).astype(BF16)
            acc = acc + dot(emb_ref[:, c * LEAF : (c + 1) * LEAF], hot)
        g_ref[...] = jnp.transpose(acc)[: plan.rows].astype(BF16)

    owned = call(
        pick_kernel,
        jax.ShapeDtypeStruct((plan.rows, width), BF16),
        skeleton,
        embeddings,
        scratch=[pltpu.VMEM((8, 128), jnp.int32)],
        name="pick",
    )

    def tree_kernel(order_ref, probes_ref, emb_ref, x_ref, inv_ref, a_ref, b_ref):
        me = lax.axis_index("leaf")
        inv = jnp.zeros((8, points), F32)
        sub = lax.broadcasted_iota(jnp.int32, (8, LEAF), 0)
        at = lax.broadcasted_iota(jnp.int32, (points, LEAF), 0)
        for c in range(leaves):
            sl = slice(c * LEAF, (c + 1) * LEAF)
            hot = jnp.where(at == order_ref[0:1, sl], 1.0, 0.0).astype(BF16)
            x_ref[:, sl] = dot(probes_ref[...], hot).astype(BF16)
            k = lax.broadcasted_iota(jnp.int32, (8, LEAF), 1) + c * LEAF
            parts = jnp.where(sub == 0, jnp.right_shift(k, 4), jnp.bitwise_and(k, 15))
            inv = inv + dot_nt(parts.astype(F32).astype(BF16), hot)
        inv_ref[...] = (inv[0:1] * 16.0 + inv[1:2]).astype(jnp.int32)
        first, last = slice(0, halo), slice(points - halo, points)

        def put(ref, sl):
            ref[0:width, :] = emb_ref[:, sl]
            ref[width : width + cols, :] = x_ref[:, sl]

        odd = jnp.bitwise_and(me, 1)

        @pl.when(odd == 0)
        def _():
            put(a_ref, last)
            put(b_ref, first)

        @pl.when(odd == 1)
        def _():
            put(a_ref, first)
            put(b_ref, last)

    send = jax.ShapeDtypeStruct((width + cols, halo), BF16)
    x_tree, inv, send_a, send_b = call(
        tree_kernel,
        [
            jax.ShapeDtypeStruct((cols, points), BF16),
            jax.ShapeDtypeStruct((1, points), jnp.int32),
            send,
            send,
        ],
        order,
        probes,
        embeddings,
        name="tree",
    )
    pairs_a = [(i, i ^ 1) for i in range(n)]
    pairs_b = [(i, i + 1) for i in range(1, n - 1, 2)] + [(i + 1, i) for i in range(1, n - 1, 2)]
    recv_a = lax.ppermute(send_a, "leaf", pairs_a)
    recv_b = lax.ppermute(send_b, "leaf", pairs_b)

    reach = jnp.arange(-W, W + 1, dtype=jnp.int32)
    target = pos * leaves + jnp.arange(leaves, dtype=jnp.int32)
    live = jnp.arange(near_list.shape[1], dtype=jnp.int32)[None, :] < near_count[0][:, None]
    same = near_list[:, :, None] == target[:, None, None] + reach[None, None, :]
    mult = jnp.sum(jnp.where(same & live[:, :, None], 1.0, 0.0), axis=1).astype(F32)

    def near_kernel(rows, mult_ref, emb_ref, x_ref, near_ref):
        near_ref[...] = jnp.zeros_like(near_ref)
        hn = half_norm_row(emb_ref[...])
        for i in rows:
            si = slice(i * LEAF, (i + 1) * LEAF)
            ei = jnp.transpose(emb_ref[:, si])
            hi = half_norm_col(ei)
            for j in range(i, min(i + W + 1, leaves)):
                sj = slice(j * LEAF, (j + 1) * LEAF)
                k = jnp.exp(dot(ei, emb_ref[:, sj]) - (hi + hn[:, sj])).astype(BF16)
                near_ref[:, sj] += mult_ref[j, i - j + W] * dot(x_ref[:, si], k)
                if j > i:
                    near_ref[:, si] += mult_ref[i, j - i + W] * dot_nt(x_ref[:, sj], k)

    parts = []
    for rows in ((0, 1), (2, 3), (4, 5, 6, 7)):
        parts.append(
            call(
                lambda *refs, rows=rows: near_kernel(rows, *refs),
                jax.ShapeDtypeStruct((cols, points), F32),
                mult,
                embeddings,
                x_tree,
                smem=(0,),
                flops=10 * 5 * 2 * 256**3,
                nbytes=6 << 20,
                name="near%d" % rows[0],
            )
        )

    block = None
    for bit in reversed(range(plan.bits)):
        level = plan.bits - 1 - bit
        if level < LEVELS:
            own = lax.slice_in_dim(
                owned, plan.starts[level], plan.starts[level] + plan.padded[level], axis=0
            )
            block = own if block is None else jnp.concatenate([block, own], axis=0)
        other = lax.ppermute(block, "leaf", [(i, i ^ (1 << bit)) for i in range(n)])
        block = jnp.concatenate([block, other], axis=0)

    offs, base, mask, slot, ok = [], [], [], [], []
    side = []
    for lev, off, row in sorted(plan.entries, key=lambda e: e[2]):
        for i in range(plan.padded[lev]):
            offs.append(off)
            side.append((off >> plan.shift[lev]) & 1)
            base.append(lev * R + i)
            mask.append((1 << plan.shift[lev]) - 1)
            slot.append(plan.slots[lev])
            ok.append(1 if i < plan.slots[lev] else 0)
    table = jnp.array([offs, side, base, mask, slot, ok], jnp.int32)
    own_w = LEVELS * R
    dest = table[1] * own_w + table[2] + jnp.bitwise_and(pos ^ table[0], table[3]) * table[4]
    dest = jnp.where(table[5] == 1, dest, -1)[None, :]

    def own_kernel(block_ref, dest_ref, emb_ref, x_ref, z_ref, part_ref):
        at = lax.broadcasted_iota(jnp.int32, (2 * own_w, plan.size), 0)
        hot = jnp.where(at == dest_ref[...], 1.0, 0.0).astype(BF16)
        sk = dot(hot, block_ref[...]).astype(BF16)
        part_ref[...] = sk[own_w:]
        hs = half_norm_col(sk[:own_w])
        z = jnp.zeros((cols, own_w), F32)
        for c in range(leaves):
            sl = slice(c * LEAF, (c + 1) * LEAF)
            e = emb_ref[:, sl]
            k = jnp.exp(dot(sk[:own_w], e) - (hs + half_norm_row(e))).astype(BF16)
            z = z + dot_nt(x_ref[:, sl], k)
        z_ref[...] = z

    z, part = call(
        own_kernel,
        [jax.ShapeDtypeStruct((cols, own_w), F32), jax.ShapeDtypeStruct((own_w, width), BF16)],
        block,
        dest,
        embeddings,
        x_tree,
        flops=30 * 2 * 256**3,
        nbytes=4 << 20,
        name="own",
    )

    level_of = lax.broadcasted_iota(jnp.int32, (1, own_w), 1) // R
    for bit in range(plan.bits):
        other = lax.ppermute(z, "leaf", [(i, i ^ (1 << bit)) for i in range(n)])
        swap = level_of == plan.bits - 1 - bit
        add = level_of < plan.bits - 1 - bit
        z = jnp.where(add, z + other, jnp.where(swap, other, z))

    def far_kernel(part_ref, emb_ref, inv_ref, out_ref, k_ref):
        hs = half_norm_col(part_ref[...])
        for c in range(leaves):
            sl = slice(c * LEAF, (c + 1) * LEAF)
            e = emb_ref[:, sl]
            k_ref[:, sl] = jnp.exp(dot(part_ref[...], e) - (hs + half_norm_row(e))).astype(BF16)
        at = lax.broadcasted_iota(jnp.int32, (points, LEAF), 0)
        for c in range(leaves):
            sl = slice(c * LEAF, (c + 1) * LEAF)
            hot = jnp.where(at == inv_ref[0:1, sl], 1.0, 0.0).astype(BF16)
            out_ref[:, sl] = dot(k_ref[...], hot).astype(BF16)

    far_k = call(
        far_kernel,
        jax.ShapeDtypeStruct((own_w, points), BF16),
        part,
        embeddings,
        inv,
        scratch=[pltpu.VMEM((own_w, points), BF16)],
        flops=90 * 2 * 256**3,
        nbytes=4 << 20,
        name="far",
    )

    def edge_kernel(mult_ref, emb_ref, x_ref, a_ref, b_ref, inv_ref, *rest):
        part_refs, (out_ref, near_ref) = rest[:-2], rest[-2:]
        near = part_refs[0][...]
        for ref in part_refs[1:]:
            near = near + ref[...]
        near_ref[...] = near
        odd = jnp.bitwise_and(lax.axis_index("leaf"), 1)

        def edges(low_ref, high_ref):
            for t in range(W):
                st = slice(t * LEAF, (t + 1) * LEAF)
                et = emb_ref[:, st]
                ht = half_norm_row(et)
                for q in range(t, W):
                    sq = slice(q * LEAF, (q + 1) * LEAF)
                    es = jnp.transpose(low_ref[0:width, sq])
                    k = jnp.exp(dot(es, et) - (half_norm_col(es) + ht)).astype(BF16)
                    near_ref[:, st] += mult_ref[t, q - t] * dot(
                        low_ref[width : width + cols, sq], k
                    )
            for back in range(W):
                t = leaves - 1 - back
                st = slice(t * LEAF, (t + 1) * LEAF)
                et = emb_ref[:, st]
                ht = half_norm_row(et)
                for q in range(W - back):
                    sq = slice(q * LEAF, (q + 1) * LEAF)
                    es = jnp.transpose(high_ref[0:width, sq])
                    k = jnp.exp(dot(es, et) - (half_norm_col(es) + ht)).astype(BF16)
                    near_ref[:, st] += mult_ref[t, back + 1 + q + W] * dot(
                        high_ref[width : width + cols, sq], k
                    )

        @pl.when(odd == 1)
        def _():
            edges(a_ref, b_ref)

        @pl.when(odd == 0)
        def _():
            edges(b_ref, a_ref)

        full = near_ref[...]
        high = full.astype(BF16)
        rest_1 = full - high.astype(F32)
        mid = rest_1.astype(BF16)
        low = (rest_1 - mid.astype(F32)).astype(BF16)
        both = jnp.concatenate([high, mid, low], axis=0)
        at = lax.broadcasted_iota(jnp.int32, (points, LEAF), 0)
        for c in range(leaves):
            sl = slice(c * LEAF, (c + 1) * LEAF)
            hot = jnp.where(at == inv_ref[0:1, sl], 1.0, 0.0).astype(BF16)
            res = dot(both, hot)
            out_ref[:, sl] = res[:cols] + res[cols : 2 * cols] + res[2 * cols :]

    near = call(
        edge_kernel,
        jax.ShapeDtypeStruct((cols, points), F32),
        mult,
        embeddings,
        x_tree,
        recv_a,
        recv_b,
        inv,
        *parts,
        scratch=[pltpu.VMEM((cols, points), F32)],
        smem=(0,),
        flops=70 * 2 * 256**3,
        nbytes=6 << 20,
        name="edge",
    )

    def last_kernel(z_ref, core_ref, far_ref, near_ref, out_ref):
        me = lax.axis_index("leaf")
        weights = []
        for l in range(LEVELS):
            node = 2 ** (l + 1) - 2 + (jnp.right_shift(me, plan.shift[l]) ^ 1)
            weights.append(
                jnp.dot(
                    z_ref[:, l * R : (l + 1) * R],
                    core_ref[node],
                    precision=lax.Precision.HIGHEST,
                    preferred_element_type=F32,
                ).astype(BF16)
            )
        w = jnp.concatenate(weights, axis=1)
        for c in range(leaves):
            sl = slice(c * LEAF, (c + 1) * LEAF)
            out_ref[:, sl] = near_ref[:, sl] + dot(w, far_ref[:, sl])

    return call(
        last_kernel,
        jax.ShapeDtypeStruct((cols, points), F32),
        z,
        core,
        far_k,
        near,
        flops=8 * 2 * 256**3,
        nbytes=2 << 20,
        name="last",
    )


def solution(mesh):
    return jax.shard_map(
        body,
        mesh=mesh,
        in_specs=(
            P(None, ("groups", "leaf")),
            P(None, ("groups", "leaf")),
            P(("groups", "leaf"), None),
            P(("groups", "leaf"), None),
            P(("groups", "leaf"), None),
            P("groups", None),
            P("groups", None, None),
        ),
        out_specs=P(None, ("groups", "leaf")),
        check_vma=False,
    )
```

time: 339 us -> 87.1 us (0.26)
  the two profiles are of different devices: /device:TPU:24 before, /device:TPU:0 now
where the time goes in v1:
time: 87.1 us; the launch traced here: 86.9 us
  Pallas kernels  34.9 us (40%)
  waiting for transfers between devices  30.5 us (35%)
  starting transfers between devices  13.8 us (16%)
  local copies, waits for them, and re-layouts  7.18 us (8%)
    pallas_call x9, Pallas kernels, call(): pl.pallas_call(kernel, out_shape=outs, in_specs=[sm if i in smem else vm...  34.9 us
    ppermute x5, waiting for transfers between devices, body(): other = lax.ppermute(block, 'leaf', [(i, i ^ 1 << bit) for i in range(n)])  19.7 us
    ppermute x5, waiting for transfers between devices, body(): other = lax.ppermute(z, 'leaf', [(i, i ^ 1 << bit) for i in range(n)])  10.8 us
    ppermute x5, starting transfers between devices, body(): other = lax.ppermute(block, 'leaf', [(i, i ^ 1 << bit) for i in range(n)])  8.55 us
    unnamed x38, local copies, waits for them, and re-layouts  7.11 us
    ppermute x5, starting transfers between devices, body(): other = lax.ppermute(z, 'leaf', [(i, i ^ 1 << bit) for i in range(n)])  3.53 us
  transfers between devices with their start and end apart: 12, of which 8 were waited for; matrix products, arithmetic and copies ran while one was open for 5% of the time, Pallas kernels for 27%

profile of v1, /device:TPU:0, one launch (start us, length us, event | category | flops | bytes accessed | tf_op | source)
XLA Modules:
  0.0 86.9 jit_solution(9249890404289429840)
XLA Ops:
  0.0 1.9 %copy-done = bf16[768,2048]{1,0:T(8,128)(2,1)S(1)} copy-done((bf16[768,2048]{1,0:T(8,128)(2,1)S(1)}, bf16[768,2048]{1,0:T(8,128)(2,1)}, u32[]{:S(2)}) %copy-start) | copy-done | bytes 3145752
  1.9 0.7 copy-done.4
  2.6 1.1 %pick.1 = bf16[64,768]{1,0:T(8,128)(2,1)S(1)} custom-call(s32[30,64]{1,0:T(8,128)S(1)} %copy-done.4, bf16[768,2048]{1,0:T(8,128)(2,1)S(1)} %copy-done), custom_call_target="tpu_custom_call" | custom-call | tf_op jit(solution)/shard_map/pick/pallas_call | solution.py:43
  3.7 0.6 constant_dynamic-update-slice_fusion.19
  4.4 4.0 %collective-permute-start = (bf16[8,768]{1,0:T(8,128)(2,1)S(1)}, bf16[8,768]{1,0:T(8,128)(2,1)S(1)}, u32[]{:S(2)}, u32[]{:S(2)}) collective-permute-start(bf16[8,768]{1,0:T(8,128)(2,1)S(1)} %get-tuple-element.35), channel_id=1, source_target_pairs={{0,16},{1,17},{2,18},{3,19},{4,20},{5,21},{6,22},{7,23},{8,24},{9,... | collective-permute-start | bytes 36872 | tf_op jit(solution)/shard_map/ppermute | solution.py:208
  8.4 5.4 %tree.1 = (bf16[32,2048]{1,0:T(8,128)(2,1)S(1)}, s32[1,2048]{1,0:T(1,128)S(1)}, bf16[800,768]{1,0:T(8,128)(2,1)}, bf16[800,768]{1,0:T(8,128)(2,1)}) custom-call(s32[1,2048]{1,0:T(1,128)S(1)} %copy-done.5, bf16[32,2048]{1,0:T(8,128)(2,1)S(1)} %copy-done.3, bf16[768,2048]{1,0:T(8,128)(2,1)S(1)} %copy-done.1), custom_call_target="tpu_custom_call" | custom-call | tf_op jit(solution)/shard_map/tree/pallas_call | solution.py:43
  13.8 1.7 %collective-permute-start.11 = (bf16[800,768]{1,0:T(8,128)(2,1)}, bf16[800,768]{1,0:T(8,128)(2,1)}, u32[]{:S(2)}, u32[]{:S(2)}) collective-permute-start(bf16[800,768]{1,0:T(8,128)(2,1)} %get-tuple-element.16), channel_id=1, source_target_pairs={{1,2},{3,4},{5,6},{7,8},{9,10},{11,12},{13,14},{15,16},{17,18},{19... | collective-permute-start | bytes 3686408 | tf_op jit(solution)/shard_map/ppermute | solution.py:162
  15.5 0.1 broadcast_add_fusion
  15.6 0.1 copy.9
  15.6 0.0 collective-permute-done
  15.6 0.6 constant_dynamic-update-slice_fusion.18
  16.3 0.6 constant_dynamic-update-slice_fusion.17
  16.9 4.4 %collective-permute-start.1 = (bf16[24,768]{1,0:T(8,128)(2,1)S(1)}, bf16[24,768]{1,0:T(8,128)(2,1)S(1)}, u32[]{:S(2)}, u32[]{:S(2)}) collective-permute-start(bf16[24,768]{1,0:T(8,128)(2,1)S(1)} %pad_maximum_fusion), channel_id=1, source_target_pairs={{0,8},{1,9},{2,10},{3,11},{4,12},{5,13},{6,14},{7,15},{8,0},{9,1},... | collective-permute-start | bytes 110600 | tf_op jit(solution)/shard_map/ppermute | solution.py:208
  21.3 14.1 %collective-permute-done.1 = bf16[24,768]{1,0:T(8,128)(2,1)S(1)} collective-permute-done((bf16[24,768]{1,0:T(8,128)(2,1)S(1)}, bf16[24,768]{1,0:T(8,128)(2,1)S(1)}, u32[]{:S(2)}, u32[]{:S(2)}) %collective-permute-start.1) | collective-permute-done | bytes 36896 | tf_op jit(solution)/shard_map/ppermute | solution.py:208
  35.4 0.6 constant_dynamic-update-slice_fusion.16
  36.1 0.6 constant_dynamic-update-slice_fusion.15
  36.7 0.0 collective-permute-start.2
  36.7 0.1 select_reduce_fusion.refs_0_.mult_ref
  36.8 4.5 %collective-permute-done.2 = bf16[64,768]{1,0:T(8,128)(2,1)S(1)} collective-permute-done((bf16[64,768]{1,0:T(8,128)(2,1)S(1)}, bf16[64,768]{1,0:T(8,128)(2,1)S(1)}, u32[]{:S(2)}, u32[]{:S(2)}) %collective-permute-start.2) | collective-permute-done | bytes 98336 | tf_op jit(solution)/shard_map/ppermute | solution.py:208
  41.3 0.7 constant_dynamic-update-slice_fusion.14
  41.9 0.6 constant_dynamic-update-slice_fusion.13
  42.6 0.0 collective-permute-start.3
  42.6 3.7 %near0.1.rest_0_ = f32[32,2048]{1,0:T(8,128)S(1)} custom-call(f32[8,7]{1,0:T(8,128)S(1)} %select_reduce_fusion.refs_0_.mult_ref, bf16[768,2048]{1,0:T(8,128)(2,1)S(1)} %copy-done.1, bf16[32,2048]{1,0:T(8,128)(2,1)S(1)} %get-tuple-element.11.x_ref.refs_2_), custom_call_target="tpu_custom_call" | custom-call | flops 1677721600 | bytes 6291456 | tf_op jit(solution)/shard_map/near0/pallas_call | solution.py:43
  46.3 3.8 %near2.1.rest_1_ = f32[32,2048]{1,0:T(8,128)S(1)} custom-call(f32[8,7]{1,0:T(8,128)S(1)} %select_reduce_fusion.refs_0_.mult_ref, bf16[768,2048]{1,0:T(8,128)(2,1)S(1)} %copy-done.1, bf16[32,2048]{1,0:T(8,128)(2,1)S(1)} %get-tuple-element.11.x_ref.refs_2_), custom_call_target="tpu_custom_call" | custom-call | flops 1677721600 | bytes 6291456 | tf_op jit(solution)/shard_map/near2/pallas_call | solution.py:43
  50.1 1.1 %collective-permute-done.3 = bf16[160,768]{1,0:T(8,128)(2,1)S(1)} collective-permute-done((bf16[160,768]{1,0:T(8,128)(2,1)S(1)}, bf16[160,768]{1,0:T(8,128)(2,1)S(1)}, u32[]{:S(2)}, u32[]{:S(2)}) %collective-permute-start.3) | collective-permute-done | bytes 245792 | tf_op jit(solution)/shard_map/ppermute | solution.py:208
  51.2 0.1 collective-permute-start.4
  51.3 0.0 copy-start.7
  51.3 0.0 copy-start.8
  51.3 0.0 copy-start.9
  51.3 0.0 copy-start.10
  51.3 0.0 copy-start.11
  51.3 4.5 %near4.1.rest_2_ = f32[32,2048]{1,0:T(8,128)S(1)} custom-call(f32[8,7]{1,0:T(8,128)S(1)} %select_reduce_fusion.refs_0_.mult_ref, bf16[768,2048]{1,0:T(8,128)(2,1)S(1)} %copy-done.1, bf16[32,2048]{1,0:T(8,128)(2,1)S(1)} %get-tuple-element.11.x_ref.refs_2_), custom_call_target="tpu_custom_call" | custom-call | flops 1677721600 | bytes 6291456 | tf_op jit(solution)/shard_map/near4/pallas_call | solution.py:43
  56.0 2.6 %own.1 = (f32[32,256]{1,0:T(8,128)S(1)}, bf16[256,768]{1,0:T(8,128)(2,1)S(1)}) custom-call(bf16[640,768]{1,0:T(8,128)(2,1)S(1)} %constant_dynamic-update-slice_fusion.20.block_ref, s32[1,640]{1,0:T(1,128)S(1)} %add_select_fusion.dest_ref, bf16[768,2048]{1,0:T(8,128)(2,1)S(1)} %copy-done.1, bf16[32,2048]{1,0:T(8,128)(2,1)S(1)} %get-tuple-element.11.x_ref.refs_2_), custom_call_target="tpu_custom_call" | custom-call | flops 1006632960 | bytes 4194304 | tf_op jit(solution)/shard_map/own/pallas_call | solution.py:43
  58.5 0.5 collective-permute-start.5
  59.0 0.9 collective-permute-done.5
  59.9 1.1 %collective-permute-start.6 = (f32[32,256]{1,0:T(8,128)S(1)}, f32[32,256]{1,0:T(8,128)S(1)}, u32[]{:S(2)}, u32[]{:S(2)}) collective-permute-start(f32[32,256]{1,0:T(8,128)S(1)} %select_select_fusion.4), channel_id=1, source_target_pairs={{0,2},{1,3},{2,0},{3,1},{4,6},{5,7},{6,4},{7,5},{8,10},{9,11},{10,... | collective-permute-start | bytes 98312 | tf_op jit(solution)/shard_map/ppermute | solution.py:254
  61.0 2.9 %collective-permute-done.6 = f32[32,256]{1,0:T(8,128)S(1)} collective-permute-done((f32[32,256]{1,0:T(8,128)S(1)}, f32[32,256]{1,0:T(8,128)S(1)}, u32[]{:S(2)}, u32[]{:S(2)}) %collective-permute-start.6) | collective-permute-done | bytes 32800 | tf_op jit(solution)/shard_map/ppermute | solution.py:254
  63.9 0.4 collective-permute-start.7
  64.3 3.6 %collective-permute-done.7 = f32[32,256]{1,0:T(8,128)S(1)} collective-permute-done((f32[32,256]{1,0:T(8,128)S(1)}, f32[32,256]{1,0:T(8,128)S(1)}, u32[]{:S(2)}, u32[]{:S(2)}) %collective-permute-start.7) | collective-permute-done | bytes 32800 | tf_op jit(solution)/shard_map/ppermute | solution.py:254
  67.9 1.4 %collective-permute-start.8 = (f32[32,256]{1,0:T(8,128)S(1)}, f32[32,256]{1,0:T(8,128)S(1)}, u32[]{:S(2)}, u32[]{:S(2)}) collective-permute-start(f32[32,256]{1,0:T(8,128)S(1)} %select_select_fusion.2), channel_id=1, source_target_pairs={{0,8},{1,9},{2,10},{3,11},{4,12},{5,13},{6,14},{7,15},{8,0},{9,1},... | collective-permute-start | bytes 98312 | tf_op jit(solution)/shard_map/ppermute | solution.py:254
  69.2 2.6 %collective-permute-done.8 = f32[32,256]{1,0:T(8,128)S(1)} collective-permute-done((f32[32,256]{1,0:T(8,128)S(1)}, f32[32,256]{1,0:T(8,128)S(1)}, u32[]{:S(2)}, u32[]{:S(2)}) %collective-permute-start.8) | collective-permute-done | bytes 32800 | tf_op jit(solution)/shard_map/ppermute | solution.py:254
  71.9 0.2 collective-permute-start.9
  72.1 3.8 %far.1.far_ref = bf16[256,2048]{1,0:T(8,128)(2,1)S(1)} custom-call(bf16[256,768]{1,0:T(8,128)(2,1)S(1)} %get-tuple-element.13.part_ref, bf16[768,2048]{1,0:T(8,128)(2,1)S(1)} %copy-done.1, s32[1,2048]{1,0:T(1,128)S(1)} %get-tuple-element.14.inv_ref), custom_call_target="tpu_custom_call" | custom-call | flops 3019898880 | bytes 4194304 | tf_op jit(solution)/shard_map/far/pallas_call | solution.py:43
  75.9 0.9 %collective-permute-done.9 = f32[32,256]{1,0:T(8,128)S(1)} collective-permute-done((f32[32,256]{1,0:T(8,128)S(1)}, f32[32,256]{1,0:T(8,128)S(1)}, u32[]{:S(2)}, u32[]{:S(2)}) %collective-permute-start.9) | collective-permute-done | bytes 32800 | tf_op jit(solution)/shard_map/ppermute | solution.py:254
  76.7 0.0 copy-start.2
  76.8 8.7 %edge.1.near_ref = f32[32,2048]{1,0:T(8,128)S(1)} custom-call(f32[8,7]{1,0:T(8,128)S(1)} %select_reduce_fusion.refs_0_.mult_ref, bf16[768,2048]{1,0:T(8,128)(2,1)} %emb_ref.9, bf16[32,2048]{1,0:T(8,128)(2,1)S(1)} %get-tuple-element.11.x_ref.refs_2_, bf16[800,768]{1,0:T(8,128)(2,1)} %collective-permute-done.10.a_ref, ...), custom_call_target="tpu_custom_call" | custom-call | flops 2348810240 | bytes 6291456 | tf_op jit(solution)/shard_map/edge/pallas_call | solution.py:43
  85.5 0.0 copy-done.2
  85.5 1.3 %last.1 = f32[32,2048]{1,0:T(8,128)} custom-call(f32[32,256]{1,0:T(8,128)S(1)} %select_select_fusion.z_ref, f32[30,64,64]{2,1,0:T(8,128)S(1)} %copy-done.2, bf16[256,2048]{1,0:T(8,128)(2,1)S(1)} %far.1.far_ref, f32[32,2048]{1,0:T(8,128)S(1)} %edge.1.near_ref), custom_call_target="tpu_custom_call" | custom-call | flops 268435456 | bytes 2097152 | tf_op jit(solution)/shard_map/last/pallas_call | solution.py:43
  (42 shorter events, 0.2 us)
Async XLA Ops:
  0.0 1.9 %copy-start = (bf16[768,2048]{1,0:T(8,128)(2,1)S(1)}, bf16[768,2048]{1,0:T(8,128)(2,1)}, u32[]{:S(2)}) copy-start(bf16[768,2048]{1,0:T(8,128)(2,1)} %emb_ref.9) | copy-start | bytes 9437188
  1.9 0.7 copy-start.4
  2.6 5.8 %copy-start.1 = (bf16[768,2048]{1,0:T(8,128)(2,1)S(1)}, bf16[768,2048]{1,0:T(8,128)(2,1)}, u32[]{:S(2)}) copy-start(bf16[768,2048]{1,0:T(8,128)(2,1)} %emb_ref.9) | copy-start | bytes 9437188
  2.6 5.8 %copy-start.3 = (bf16[32,2048]{1,0:T(8,128)(2,1)S(1)}, bf16[32,2048]{1,0:T(8,128)(2,1)}, u32[]{:S(2)}) copy-start(bf16[32,2048]{1,0:T(8,128)(2,1)} %probes_ref.1) | copy-start | bytes 393220
  2.6 5.8 %copy-start.5 = (s32[1,2048]{1,0:T(1,128)S(1)}, s32[1,2048]{1,0:T(1,128)}, u32[]{:S(2)}) copy-start(s32[1,2048]{1,0:T(1,128)} %order_ref.1) | copy-start | bytes 24580
  4.4 11.2 %copy-start.13 = (s32[1,8]{1,0:T(1,128)S(1)}, s32[1,8]{1,0:T(1,128)}, u32[]{:S(2)}) copy-start(s32[1,8]{1,0:T(1,128)} %param.12) | copy-start | bytes 100
  4.4 11.2 %copy-start.6 = (s32[8,7]{1,0:T(8,128)S(1)}, s32[8,7]{1,0:T(8,128)}, u32[]{:S(2)}) copy-start(s32[8,7]{1,0:T(8,128)} %param.11) | copy-start | bytes 676
  4.4 11.3 %collective-permute-start = (bf16[8,768]{1,0:T(8,128)(2,1)S(1)}, bf16[8,768]{1,0:T(8,128)(2,1)S(1)}, u32[]{:S(2)}, u32[]{:S(2)}) collective-permute-start(bf16[8,768]{1,0:T(8,128)(2,1)S(1)} %get-tuple-element.35), channel_id=1, source_target_pairs={{0,16},{1,17},{2,18},{3,19},{4,20},{5,21},{6,22},{7,23},{8,24},{9,... | collective-permute-start | bytes 36872 | tf_op jit(solution)/shard_map/ppermute | solution.py:208
  13.8 63.0 %collective-permute-start.10 = (bf16[800,768]{1,0:T(8,128)(2,1)}, bf16[800,768]{1,0:T(8,128)(2,1)}, u32[]{:S(2)}, u32[]{:S(2)}) collective-permute-start(bf16[800,768]{1,0:T(8,128)(2,1)} %get-tuple-element.15), channel_id=1, source_target_pairs={{0,1},{1,0},{2,3},{3,2},{4,5},{5,4},{6,7},{7,6},{8,9},{9,8},{10,11... | collective-permute-start | bytes 3686408 | tf_op jit(solution)/shard_map/ppermute | solution.py:161
  13.8 63.0 %collective-permute-start.11 = (bf16[800,768]{1,0:T(8,128)(2,1)}, bf16[800,768]{1,0:T(8,128)(2,1)}, u32[]{:S(2)}, u32[]{:S(2)}) collective-permute-start(bf16[800,768]{1,0:T(8,128)(2,1)} %get-tuple-element.16), channel_id=1, source_target_pairs={{1,2},{3,4},{5,6},{7,8},{9,10},{11,12},{13,14},{15,16},{17,18},{19... | collective-permute-start | bytes 3686408 | tf_op jit(solution)/shard_map/ppermute | solution.py:162
  16.9 18.6 %collective-permute-start.1 = (bf16[24,768]{1,0:T(8,128)(2,1)S(1)}, bf16[24,768]{1,0:T(8,128)(2,1)S(1)}, u32[]{:S(2)}, u32[]{:S(2)}) collective-permute-start(bf16[24,768]{1,0:T(8,128)(2,1)S(1)} %pad_maximum_fusion), channel_id=1, source_target_pairs={{0,8},{1,9},{2,10},{3,11},{4,12},{5,13},{6,14},{7,15},{8,0},{9,1},... | collective-permute-start | bytes 110600 | tf_op jit(solution)/shard_map/ppermute | solution.py:208
  36.7 4.6 %collective-permute-start.2 = (bf16[64,768]{1,0:T(8,128)(2,1)S(1)}, bf16[64,768]{1,0:T(8,128)(2,1)S(1)}, u32[]{:S(2)}, u32[]{:S(2)}) collective-permute-start(bf16[64,768]{1,0:T(8,128)(2,1)S(1)} %get-tuple-element.28), channel_id=1, source_target_pairs={{0,4},{1,5},{2,6},{3,7},{4,0},{5,1},{6,2},{7,3},{8,12},{9,13},{10,... | collective-permute-start | bytes 294920 | tf_op jit(solution)/shard_map/ppermute | solution.py:208
  42.6 8.6 %collective-permute-start.3 = (bf16[160,768]{1,0:T(8,128)(2,1)S(1)}, bf16[160,768]{1,0:T(8,128)(2,1)S(1)}, u32[]{:S(2)}, u32[]{:S(2)}) collective-permute-start(bf16[160,768]{1,0:T(8,128)(2,1)S(1)} %get-tuple-element.21), channel_id=1, source_target_pairs={{0,2},{1,3},{2,0},{3,1},{4,6},{5,7},{6,4},{7,5},{8,10},{9,11},{10,... | collective-permute-start | bytes 737288 | tf_op jit(solution)/shard_map/ppermute | solution.py:208
  46.3 4.8 %copy-start.12 = (bf16[320,768]{1,0:T(8,128)(2,1)S(1)}, bf16[320,768]{1,0:T(8,128)(2,1)}, u32[]{:S(2)}) copy-start(bf16[320,768]{1,0:T(8,128)(2,1)} %get-tuple-element.19) | copy-start | bytes 1474564
  51.2 4.7 %collective-permute-start.4 = (bf16[320,768]{1,0:T(8,128)(2,1)S(1)}, bf16[320,768]{1,0:T(8,128)(2,1)S(1)}, u32[]{:S(2)}, u32[]{:S(2)}) collective-permute-start(bf16[320,768]{1,0:T(8,128)(2,1)S(1)} %get-tuple-element.17), channel_id=1, source_target_pairs={{0,1},{1,0},{2,3},{3,2},{4,5},{5,4},{6,7},{7,6},{8,9},{9,8},{10,11... | collective-permute-start | bytes 1474568 | tf_op jit(solution)/shard_map/ppermute | solution.py:208
  51.3 4.6 %copy-start.7 = (pred[1,640]{1,0:T(4,128)(4,1)S(1)}, pred[1,640]{1,0:T(4,128)(4,1)}, u32[]{:S(2)}) copy-start(pred[1,640]{1,0:T(4,128)(4,1)} %constant.67) | copy-start | bytes 1924
  51.3 4.6 %copy-start.8 = (s32[1,640]{1,0:T(1,128)S(1)}, s32[1,640]{1,0:T(1,128)}, u32[]{:S(2)}) copy-start(s32[1,640]{1,0:T(1,128)} %constant.71) | copy-start | bytes 7684
  51.3 4.6 %copy-start.9 = (s32[1,640]{1,0:T(1,128)S(1)}, s32[1,640]{1,0:T(1,128)}, u32[]{:S(2)}) copy-start(s32[1,640]{1,0:T(1,128)} %constant.74) | copy-start | bytes 7684
  51.3 4.6 %copy-start.10 = (s32[1,640]{1,0:T(1,128)S(1)}, s32[1,640]{1,0:T(1,128)}, u32[]{:S(2)}) copy-start(s32[1,640]{1,0:T(1,128)} %constant.73) | copy-start | bytes 7684
  51.3 4.6 %copy-start.11 = (s32[1,640]{1,0:T(1,128)S(1)}, s32[1,640]{1,0:T(1,128)}, u32[]{:S(2)}) copy-start(s32[1,640]{1,0:T(1,128)} %constant.72) | copy-start | bytes 7684
  58.5 1.4 %collective-permute-start.5 = (f32[32,256]{1,0:T(8,128)S(1)}, f32[32,256]{1,0:T(8,128)S(1)}, u32[]{:S(2)}, u32[]{:S(2)}) collective-permute-start(f32[32,256]{1,0:T(8,128)S(1)} %get-tuple-element.12), channel_id=1, source_target_pairs={{0,1},{1,0},{2,3},{3,2},{4,5},{5,4},{6,7},{7,6},{8,9},{9,8},{10,11... | collective-permute-start | bytes 98312 | tf_op jit(solution)/shard_map/ppermute | solution.py:254
  59.9 4.0 %collective-permute-start.6 = (f32[32,256]{1,0:T(8,128)S(1)}, f32[32,256]{1,0:T(8,128)S(1)}, u32[]{:S(2)}, u32[]{:S(2)}) collective-permute-start(f32[32,256]{1,0:T(8,128)S(1)} %select_select_fusion.4), channel_id=1, source_target_pairs={{0,2},{1,3},{2,0},{3,1},{4,6},{5,7},{6,4},{7,5},{8,10},{9,11},{10,... | collective-permute-start | bytes 98312 | tf_op jit(solution)/shard_map/ppermute | solution.py:254
  63.9 4.0 %collective-permute-start.7 = (f32[32,256]{1,0:T(8,128)S(1)}, f32[32,256]{1,0:T(8,128)S(1)}, u32[]{:S(2)}, u32[]{:S(2)}) collective-permute-start(f32[32,256]{1,0:T(8,128)S(1)} %select_select_fusion.3), channel_id=1, source_target_pairs={{0,4},{1,5},{2,6},{3,7},{4,0},{5,1},{6,2},{7,3},{8,12},{9,13},{10,... | collective-permute-start | bytes 98312 | tf_op jit(solution)/shard_map/ppermute | solution.py:254
  67.9 4.0 %collective-permute-start.8 = (f32[32,256]{1,0:T(8,128)S(1)}, f32[32,256]{1,0:T(8,128)S(1)}, u32[]{:S(2)}, u32[]{:S(2)}) collective-permute-start(f32[32,256]{1,0:T(8,128)S(1)} %select_select_fusion.2), channel_id=1, source_target_pairs={{0,8},{1,9},{2,10},{3,11},{4,12},{5,13},{6,14},{7,15},{8,0},{9,1},... | collective-permute-start | bytes 98312 | tf_op jit(solution)/shard_map/ppermute | solution.py:254
  71.9 4.9 %collective-permute-start.9 = (f32[32,256]{1,0:T(8,128)S(1)}, f32[32,256]{1,0:T(8,128)S(1)}, u32[]{:S(2)}, u32[]{:S(2)}) collective-permute-start(f32[32,256]{1,0:T(8,128)S(1)} %select_select_fusion.1), channel_id=1, source_target_pairs={{0,16},{1,17},{2,18},{3,19},{4,20},{5,21},{6,22},{7,23},{8,24},{9,... | collective-permute-start | bytes 98312 | tf_op jit(solution)/shard_map/ppermute | solution.py:254
  76.7 8.8 %copy-start.2 = (f32[30,64,64]{2,1,0:T(8,128)S(1)}, f32[30,64,64]{2,1,0:T(8,128)}, u32[]{:S(2)}) copy-start(f32[30,64,64]{2,1,0:T(8,128)} %core_ref.1) | copy-start | bytes 1474564

commit v2 on v1

v2 whole, which is shorter than its diff:
```python
import jax
import jax.numpy as jnp
from jax import lax
from jax.experimental import pallas as pl
from jax.experimental.pallas import tpu as pltpu
from jax.sharding import PartitionSpec as P

LEAF = 256
R = 64
LEVELS = 4
W = 3
F32 = jnp.float32
BF16 = jnp.bfloat16
VMEM_LIMIT = 14 * 1024 * 1024
LANES = 128
UP, DOWN = 2, 1


def dot(a, b):
    return jnp.dot(a, b, preferred_element_type=F32)


def dot_nt(a, b):
    return lax.dot_general(a, b, (((1,), (1,)), ((), ())), preferred_element_type=F32)


def dot_tn(a, b):
    return lax.dot_general(a, b, (((0,), (0,)), ((), ())), preferred_element_type=F32)


def half_norm_row(emb):
    e = emb.astype(F32)
    return 0.5 * jnp.sum(e * e, axis=0, keepdims=True)


def half_norm_col(rows):
    e = rows.astype(F32)
    return 0.5 * jnp.sum(e * e, axis=1, keepdims=True)


def col_of(row):
    return jnp.transpose(jnp.broadcast_to(row, (8, row.shape[1])))[:, 0:1]


def call(kernel, outs, *args, scratch=(), smem=(), hbm=(), flops=0, nbytes=0, name=None, vmem=VMEM_LIMIT):
    single = not isinstance(outs, (list, tuple))
    vm = pl.BlockSpec(memory_space=pltpu.VMEM)
    sm = pl.BlockSpec(memory_space=pltpu.SMEM)
    hb = pl.BlockSpec(memory_space=pltpu.HBM)
    return pl.pallas_call(
        kernel,
        out_shape=outs,
        in_specs=[sm if i in smem else hb if i in hbm else vm for i in range(len(args))],
        out_specs=vm if single else [vm] * len(outs),
        scratch_shapes=list(scratch),
        compiler_params=pltpu.CompilerParams(vmem_limit_bytes=vmem),
        cost_estimate=pl.CostEstimate(flops=flops, bytes_accessed=nbytes, transcendentals=0),
        name=name,
    )(*args)


class Plan:
    def __init__(self, n):
        self.n = n
        self.bits = n.bit_length() - 1
        self.slots = [R * 2 ** (l + 1) // n for l in range(LEVELS)]
        self.padded = [-(-s // 8) * 8 for s in self.slots]
        self.starts = [sum(self.padded[:l]) for l in range(LEVELS)]
        self.rows = sum(self.padded)
        self.shift = [self.bits - 1 - l for l in range(LEVELS)]
        entries, size = [], 0
        for bit in reversed(range(self.bits)):
            level = self.bits - 1 - bit
            if level < LEVELS:
                entries.append((level, 0, size))
                size += self.padded[level]
            entries += [(lev, off ^ (1 << bit), row + size) for lev, off, row in entries]
            size *= 2
        self.entries, self.size = entries, size


def body(embeddings, probes, order, near_list, near_count, skeleton, core):
    n = lax.axis_size("leaf")
    plan = Plan(n)
    pos = lax.axis_index("leaf")
    width, points = embeddings.shape
    cols = probes.shape[0]
    leaves = points // LEAF
    halo = W * LEAF

    groups = points // LANES

    last = points - halo
    extra = 16

    def pick_kernel(skel_ref, emb_ref, *rest):
        g_refs, row_ref = rest[:-1], rest[-1]
        me = lax.axis_index("leaf")
        lane = lax.broadcasted_iota(jnp.int32, (1, LANES), 1)
        idx = jnp.full((1, LANES), -1, jnp.int32)
        row_ref[...] = jnp.zeros_like(row_ref)
        for l in range(LEVELS):
            node = 2 ** (l + 1) - 2 + jnp.right_shift(me, plan.shift[l])
            row_ref[0:1, 0:R] = skel_ref[pl.ds(node, 1), :]
            within = jnp.bitwise_and(me, (1 << plan.shift[l]) - 1)
            shift = jnp.bitwise_and(plan.starts[l] - within * plan.slots[l] + LANES, LANES - 1)
            rolled = pltpu.roll(row_ref[...], shift, 1)[0:1, :]
            mine = (lane >= plan.starts[l]) & (lane < plan.starts[l] + plan.slots[l])
            idx = jnp.where(mine, rolled, idx)
        acc = jnp.zeros((width, LANES), F32)
        for c in range(leaves):
            at = lax.broadcasted_iota(jnp.int32, (LEAF, LANES), 0) + c * LEAF
            pick = jnp.where(at == idx, 1.0, 0.0).astype(BF16)
            acc = acc + dot(emb_ref[:, c * LEAF : (c + 1) * LEAF], pick)
        picked = jnp.transpose(acc)
        for l in range(LEVELS):
            g_refs[l][...] = picked[plan.starts[l] : plan.starts[l] + plan.padded[l]].astype(BF16)

    owned = call(
        pick_kernel,
        [jax.ShapeDtypeStruct((p, width), BF16) for p in plan.padded],
        skeleton - pos * points,
        embeddings,
        scratch=[pltpu.VMEM((8, LANES), jnp.int32)],
        flops=10 * 2 * 256**3,
        nbytes=6 << 20,
        name="pick",
    )

    def cut_kernel(emb_ref, up_ref, down_ref, a_ref, sems):
        odd = jnp.bitwise_and(lax.axis_index("leaf"), 1)
        copies = []
        for i, (ref, at) in enumerate(
            ((up_ref, points - UP * LEAF), (down_ref, 0), (a_ref, (1 - odd) * last))
        ):
            at = pl.multiple_of(at, LEAF)
            copies.append(
                pltpu.make_async_copy(emb_ref.at[:, pl.ds(at, ref.shape[1])], ref, sems.at[i])
            )
        for copy in copies:
            copy.start()
        for copy in copies:
            copy.wait()

    emb = embeddings
    send_up, send_down, send_a = call(
        cut_kernel,
        [jax.ShapeDtypeStruct((width, w * LEAF), BF16) for w in (UP, DOWN, W)],
        emb,
        scratch=[pltpu.SemaphoreType.DMA((3,))],
        nbytes=3 << 20,
        name="cut",
    )

    reach = jnp.arange(-W, W + 1, dtype=jnp.int32)
    target = pos * leaves + jnp.arange(leaves, dtype=jnp.int32)
    live = jnp.arange(near_list.shape[1], dtype=jnp.int32)[None, :] < near_count[0][:, None]
    same = near_list[:, :, None] == target[:, None, None] + reach[None, None, :]
    mult = jnp.sum(jnp.where(same & live[:, :, None], 1.0, 0.0), axis=1).astype(F32)

    def tree_kernel(order_ref, probes_ref, emb_ref, mult_ref, x_ref, inv_ref, hn_ref, a_ref, b_ref):
        odd = jnp.bitwise_and(lax.axis_index("leaf"), 1)

        order_row = order_ref[...]
        low = jnp.bitwise_and(order_row, LANES - 1)
        high = jnp.right_shift(order_row, LANES.bit_length() - 1)
        hot = jnp.where(
            lax.broadcasted_iota(jnp.int32, (LANES, points), 0) == low, 1.0, 0.0
        ).astype(BF16)
        stack = jnp.concatenate(
            [probes_ref[:, h * LANES : (h + 1) * LANES] for h in range(groups)], axis=0
        )
        for c in range(leaves):
            sl = slice(c * LEAF, (c + 1) * LEAF)
            y = dot(stack, hot[:, sl])
            x = jnp.zeros((cols, LEAF), F32)
            for h in range(groups):
                x = x + jnp.where(high[:, sl] == h, y[h * cols : (h + 1) * cols], 0.0)
            x_ref[:, sl] = x.astype(BF16)
            hn_ref[:, sl] = half_norm_row(emb_ref[:, sl])

        k = lax.broadcasted_iota(jnp.int32, (8, points), 1)
        sub = lax.broadcasted_iota(jnp.int32, (8, points), 0)
        digits = jnp.where(sub == 0, jnp.right_shift(k, 4), jnp.bitwise_and(k, 15)).astype(F32)
        spread = jnp.concatenate(
            [jnp.where(high == h, digits, 0.0) for h in range(groups)], axis=0
        ).astype(BF16)
        found = dot_nt(spread, hot)
        for h in range(groups):
            inv_ref[:, h * LANES : (h + 1) * LANES] = (
                found[8 * h : 8 * h + 1] * 16.0 + found[8 * h + 1 : 8 * h + 2]
            ).astype(jnp.int32)

        def tell(pairs):
            rows = [jnp.full((1, halo), mult_ref[t, o + W], F32) for t, o in pairs]
            rows.append(jnp.zeros((extra - len(rows), halo), F32))
            b_ref[cols:, :] = jnp.concatenate(rows, axis=0).astype(BF16)

        @pl.when(odd == 0)
        def _():
            a_ref[...] = x_ref[:, last:]
            b_ref[0:cols, :] = x_ref[:, :halo]
            tell([(0, -1 - q) for q in range(W)])

        @pl.when(odd == 1)
        def _():
            a_ref[...] = x_ref[:, :halo]
            b_ref[0:cols, :] = x_ref[:, last:]
            tell([(leaves - 1, 2), (leaves - 1, 3), (leaves - 2, 3)])

    x_send = jax.ShapeDtypeStruct((cols, halo), BF16)
    x_tree, inv, hn, x_a, x_b = call(
        tree_kernel,
        [
            jax.ShapeDtypeStruct((cols, points), BF16),
            jax.ShapeDtypeStruct((1, points), jnp.int32),
            jax.ShapeDtypeStruct((1, points), F32),
            x_send,
            jax.ShapeDtypeStruct((cols + extra, halo), BF16),
        ],
        order,
        probes,
        emb,
        mult,
        smem=(3,),
        flops=40 * 2 * 256**3,
        nbytes=1 << 20,
        name="tree",
    )

    pairs_a = [(i, i ^ 1) for i in range(n)]
    pairs_up = [(i, i + 1) for i in range(1, n - 1, 2)]
    pairs_down = [(j, i) for i, j in pairs_up]

    def near_kernel(rows, mult_ref, emb_ref, x_ref, hn_ref, near_ref):
        acc = [None] * leaves

        def add(j, value):
            acc[j] = value if acc[j] is None else acc[j] + value

        def make(i):
            w = min(W + 1, leaves - i)
            si, sp = slice(i * LEAF, (i + 1) * LEAF), slice(i * LEAF, (i + w) * LEAF)
            g = dot(jnp.transpose(emb_ref[:, si]), emb_ref[:, sp])
            return jnp.exp(g - (col_of(hn_ref[:, si]) + hn_ref[:, sp])).astype(BF16)

        def use(i, k):
            y = dot(x_ref[:, i * LEAF : (i + 1) * LEAF], k)
            for q in range(k.shape[1] // LEAF):
                j = i + q
                sq = slice(q * LEAF, (q + 1) * LEAF)
                add(j, mult_ref[j, W - q] * y[:, sq])
                if q:
                    sj = slice(j * LEAF, (j + 1) * LEAF)
                    add(i, mult_ref[i, W + q] * dot_nt(x_ref[:, sj], k[:, sq]))

        held = None
        for i in rows:
            k = make(i)
            if held is not None:
                use(*held)
            held = (i, k)
        use(*held)
        for j in range(leaves):
            sj = slice(j * LEAF, (j + 1) * LEAF)
            near_ref[:, sj] = jnp.zeros((cols, LEAF), F32) if acc[j] is None else acc[j]

    def near_part(rows, emb, x_tree, hn):
        return call(
            lambda *refs: near_kernel(rows, *refs),
            jax.ShapeDtypeStruct((cols, points), F32),
            mult,
            emb,
            x_tree,
            hn,
            smem=(0,),
            flops=60 * 2 * 256**3,
            nbytes=6 << 20,
            name="near%d" % rows[0],
        )

    def join_kernel(*refs):
        row = 0
        for ref in refs[:-1]:
            refs[-1][row : row + ref.shape[0], :] = ref[...]
            row += ref.shape[0]

    def join(*blocks):
        rows = sum(v.shape[0] for v in blocks)
        return call(
            join_kernel, jax.ShapeDtypeStruct((rows, width), BF16), *blocks, nbytes=1 << 18, name="join"
        )

    after = lax.optimization_barrier
    parts = []
    block = owned[0]
    for bit in reversed(range(plan.bits)):
        level = plan.bits - bit
        stage = level - 1
        partner = lax.ppermute(block, "leaf", [(i, i ^ (1 << bit)) for i in range(n)])
        if stage == 0:
            recv_up = lax.ppermute(send_up, "leaf", pairs_up)
            recv_down = lax.ppermute(send_down, "leaf", pairs_down)
            partner, x_tree = after((partner, x_tree))
        if stage == 1:
            recv_a = lax.ppermute(send_a, "leaf", pairs_a)
            recv_xa = lax.ppermute(x_a, "leaf", pairs_a)
            parts.append(near_part((0, 1), emb, x_tree, hn))
            partner, parts[-1] = after((partner, parts[-1]))
        if stage == 2:
            recv_xb = lax.ppermute(x_b, "leaf", pairs_up + pairs_down)
            parts.append(near_part((2, 3), emb, x_tree, hn))
            partner, parts[-1], recv_up, recv_down = after(
                (partner, parts[-1], recv_up, recv_down)
            )
        if stage == 3:
            parts.append(near_part(tuple(range(4, leaves)), emb, x_tree, hn))
            partner, parts[-1], recv_a, recv_xa, recv_xb = after(
                (partner, parts[-1], recv_a, recv_xa, recv_xb)
            )
        if bit:
            block = join(block, partner, *([owned[level]] if level < LEVELS else []))
            block, x_tree, send_a, x_b = after((block, x_tree, send_a, x_b))

    table = []
    for lev, off, row in sorted(plan.entries, key=lambda e: e[2]):
        for i in range(plan.padded[lev]):
            side = (off >> plan.shift[lev]) & 1
            table.append(
                (
                    off,
                    (side * LEVELS + lev) * R + i,
                    (1 << plan.shift[lev]) - 1,
                    plan.slots[lev],
                    i < plan.slots[lev],
                )
            )
    table = jnp.array(table, jnp.int32).T
    own_w = LEVELS * R
    dest = table[1] + jnp.bitwise_and(pos ^ table[0], table[2]) * table[3]
    dest = jnp.where(table[4] == 1, dest, -1)[None, :]

    half = plan.size // 2

    def sorted_rows(first, dest_ref, *refs):
        at = lax.broadcasted_iota(jnp.int32, (own_w, half), 0)
        total = None
        for i, ref in enumerate(refs):
            d = dest_ref[:, i * half : (i + 1) * half] - first
            term = dot(jnp.where(at == d, 1.0, 0.0).astype(BF16), ref[...])
            total = term if total is None else total + term
        return total.astype(BF16)

    def own_kernel(block_ref, other_ref, dest_ref, emb_ref, x_ref, hn_ref, z_ref):
        sk = sorted_rows(0, dest_ref, block_ref, other_ref)
        hs = half_norm_col(sk)
        z = jnp.zeros((cols, own_w), F32)
        held = None
        for c in range(0, leaves, 2):
            sl = slice(c * LEAF, (c + 2) * LEAF)
            k = jnp.exp(dot(sk, emb_ref[:, sl]) - (hs + hn_ref[:, sl])).astype(BF16)
            if held is not None:
                z = z + dot_nt(x_ref[:, held[0]], held[1])
            held = (sl, k)
        z_ref[...] = z + dot_nt(x_ref[:, held[0]], held[1])

    z = call(
        own_kernel,
        jax.ShapeDtypeStruct((cols, own_w), F32),
        block,
        partner,
        dest,
        emb,
        x_tree,
        hn,
        flops=50 * 2 * 256**3,
        nbytes=4 << 20,
        name="own",
    )

    def far_kernel(block_ref, other_ref, dest_ref, emb_ref, hn_ref, out_ref):
        sk = sorted_rows(own_w, dest_ref, block_ref, other_ref)
        hs = half_norm_col(sk)
        for c in range(0, leaves, 2):
            sl = slice(c * LEAF, (c + 2) * LEAF)
            g = dot(sk, emb_ref[:, sl])
            out_ref[:, sl] = jnp.exp(g - (hs + hn_ref[:, sl])).astype(BF16)

    def far_part(block, partner, emb, hn):
        return call(
            far_kernel,
            jax.ShapeDtypeStruct((own_w, points), BF16),
            block,
            partner,
            dest,
            emb,
            hn,
            flops=30 * 2 * 256**3,
            nbytes=4 << 20,
            name="far",
        )

    def low_edge(mult_ref, emb_ref, hn_ref, src_ref, xs_ref, near_ref):
        acc = [jnp.zeros((cols, LEAF), F32)] * W
        for q in range(W):
            sq, sp = slice(q * LEAF, (q + 1) * LEAF), slice(0, (q + 1) * LEAF)
            es = src_ref[:, sq]
            g = dot(jnp.transpose(es), emb_ref[:, sp])
            k = jnp.exp(g - (col_of(half_norm_row(es)) + hn_ref[:, sp])).astype(BF16)
            y = dot(xs_ref[:, sq], k)
            for t in range(q + 1):
                acc[t] = acc[t] + mult_ref[t, q - t] * y[:, t * LEAF : (t + 1) * LEAF]
        near_ref[:, 0:halo] = jnp.concatenate(acc, axis=1)
        near_ref[:, halo:] = jnp.zeros((cols, points - halo), F32)

    def high_edge(mult_ref, emb_ref, hn_ref, src_ref, xs_ref, near_ref):
        acc = [jnp.zeros((cols, LEAF), F32)] * W
        for q in range(W):
            sq, sp = slice(q * LEAF, (q + 1) * LEAF), slice((leaves - W + q) * LEAF, points)
            es = src_ref[:, sq]
            g = dot(jnp.transpose(es), emb_ref[:, sp])
            k = jnp.exp(g - (col_of(half_norm_row(es)) + hn_ref[:, sp])).astype(BF16)
            y = dot(xs_ref[:, sq], k)
            for i in range(W - q):
                t = leaves - W + q + i
                acc[q + i] = acc[q + i] + (
                    mult_ref[t, leaves + q - t + W] * y[:, i * LEAF : (i + 1) * LEAF]
                )
        near_ref[:, 0 : points - halo] = jnp.zeros((cols, points - halo), F32)
        near_ref[:, points - halo :] = jnp.concatenate(acc, axis=1)

    def core_kernel(mult_ref, emb_ref, hn_ref, src_ref, xs_ref, near_ref):
        odd = jnp.bitwise_and(lax.axis_index("leaf"), 1)
        for code, edge in ((1, low_edge), (0, high_edge)):

            @pl.when(odd == code)
            def _():
                edge(mult_ref, emb_ref, hn_ref, src_ref, xs_ref, near_ref)

    def core_part(emb, hn):
        return call(
            core_kernel,
            jax.ShapeDtypeStruct((cols, points), F32),
            mult,
            emb,
            hn,
            recv_a,
            recv_xa,
            smem=(0,),
            flops=30 * 2 * 256**3,
            nbytes=3 << 20,
            name="edge_core",
        )

    def chip_kernel(mult_ref, emb_ref, hn_ref, x_ref, up_ref, down_ref, xs_ref, near_ref, back_ref):
        odd = jnp.bitwise_and(lax.axis_index("leaf"), 1)

        def kernel_of(es, sp):
            g = dot(jnp.transpose(es), emb_ref[:, sp])
            return jnp.exp(g - (col_of(half_norm_row(es)) + hn_ref[:, sp])).astype(BF16)

        def told(row):
            return xs_ref[cols + row : cols + row + 1, 0:LEAF].astype(F32)

        def leaf(q):
            return slice(q * LEAF, (q + 1) * LEAF)

        @pl.when(odd == 1)
        def _():
            k = kernel_of(down_ref[...], slice(last, points))
            y = dot(xs_ref[0:cols, 0:LEAF], k)
            back = jnp.zeros((cols, LEAF), F32)
            for q in range(W):
                t = leaves - W + q
                near_ref[:, leaf(t)] = mult_ref[t, 2 * W - q] * y[:, leaf(q)]
                back = back + told(W - 1 - q) * dot_nt(x_ref[:, leaf(t)], k[:, leaf(q)])
            near_ref[:, 0:last] = jnp.zeros((cols, last), F32)
            back_ref[:, leaf(0)] = back
            back_ref[:, leaf(1)] = jnp.zeros((cols, LEAF), F32)

        @pl.when(odd == 0)
        def _():
            k3 = kernel_of(up_ref[:, leaf(1)], slice(LEAF, 3 * LEAF))
            k2 = kernel_of(up_ref[:, leaf(0)], leaf(1))
            y3 = dot(xs_ref[0:cols, leaf(2)], k3)
            y2 = dot(xs_ref[0:cols, leaf(1)], k2)
            near_ref[:, leaf(0)] = jnp.zeros((cols, LEAF), F32)
            near_ref[:, leaf(1)] = mult_ref[1, 1] * y3[:, leaf(0)] + mult_ref[1, 0] * y2
            near_ref[:, leaf(2)] = mult_ref[2, 0] * y3[:, leaf(1)]
            near_ref[:, halo:] = jnp.zeros((cols, last), F32)
            back_ref[:, leaf(1)] = told(0) * dot_nt(x_ref[:, leaf(1)], k3[:, leaf(0)]) + told(
                1
            ) * dot_nt(x_ref[:, leaf(2)], k3[:, leaf(1)])
            back_ref[:, leaf(0)] = told(2) * dot_nt(x_ref[:, leaf(1)], k2)

    def chip_part(emb, hn):
        return call(
            chip_kernel,
            [
                jax.ShapeDtypeStruct((cols, points), F32),
                jax.ShapeDtypeStruct((cols, UP * LEAF), F32),
            ],
            mult,
            emb,
            hn,
            x_tree,
            recv_up,
            recv_down,
            recv_xb,
            smem=(0,),
            flops=30 * 2 * 256**3,
            nbytes=4 << 20,
            name="edge_chip",
        )

    level_of = lax.broadcasted_iota(jnp.int32, (1, own_w), 1) // R
    for stage, bit in enumerate(range(plan.bits)):
        heard = lax.ppermute(z, "leaf", [(i, i ^ (1 << bit)) for i in range(n)])
        if stage == 1:
            chip_near, back = chip_part(emb, hn)
            heard, chip_near, back = after((heard, chip_near, back))
        if stage == 2:
            back = lax.ppermute(back, "leaf", pairs_up + pairs_down)
            far_k = far_part(block, partner, emb, hn)
            heard, far_k = after((heard, far_k))
        if stage == 3:
            parts += [core_part(emb, hn), chip_near]
            heard, parts[-2] = after((heard, parts[-2]))
        swap = level_of == plan.bits - 1 - bit
        add = level_of < plan.bits - 1 - bit
        z = jnp.where(add, z + heard, jnp.where(swap, heard, z))
        z, emb = after((z, emb))

    def last_kernel(z_ref, core_ref, far_ref, back_ref, inv_ref, *rest):
        part_refs, out_ref = rest[:-1], rest[-1]
        me = lax.axis_index("leaf")
        weights = []
        for l in range(LEVELS):
            node = 2 ** (l + 1) - 2 + (jnp.right_shift(me, plan.shift[l]) ^ 1)
            weights.append(
                jnp.dot(
                    z_ref[:, l * R : (l + 1) * R],
                    core_ref[node],
                    precision=lax.Precision.HIGHEST,
                    preferred_element_type=F32,
                ).astype(BF16)
            )
        w = jnp.concatenate(weights, axis=1)
        tree = dot(w, far_ref[...])
        for ref in part_refs:
            tree = tree + ref[...]
        even = jnp.bitwise_and(me, 1) == 0
        low_back = jnp.where(even, back_ref[:, 0:LEAF], 0.0)
        high_back = jnp.where(even, 0.0, back_ref[...])
        tree = tree + jnp.concatenate(
            [low_back, jnp.zeros((cols, points - (1 + UP) * LEAF), F32), high_back], axis=1
        )
        top = tree.astype(BF16)
        rest = (tree - top.astype(F32)).astype(BF16)
        stack = jnp.concatenate(
            [
                jnp.concatenate([v[:, h * LANES : (h + 1) * LANES] for v in (top, rest)], axis=1)
                for h in range(groups)
            ],
            axis=0,
        )
        low = jnp.bitwise_and(inv_ref[...], LANES - 1)
        high = jnp.right_shift(inv_ref[...], LANES.bit_length() - 1)
        hot = jnp.where(
            lax.broadcasted_iota(jnp.int32, (LANES, points), 0) == low, 1.0, 0.0
        ).astype(BF16)
        for c in range(leaves):
            sl = slice(c * LEAF, (c + 1) * LEAF)
            y = dot(stack, jnp.concatenate([hot[:, sl]] * 2, axis=0))
            out = jnp.zeros((cols, LEAF), F32)
            for h in range(groups):
                out = out + jnp.where(high[:, sl] == h, y[h * cols : (h + 1) * cols], 0.0)
            out_ref[:, sl] = out

    return call(
        last_kernel,
        jax.ShapeDtypeStruct((cols, points), F32),
        z,
        core,
        far_k,
        back,
        inv,
        *parts,
        flops=30 * 2 * 256**3,
        nbytes=2 << 20,
        name="last",
    )


def solution(mesh):
    return jax.shard_map(
        body,
        mesh=mesh,
        in_specs=(
            P(None, ("groups", "leaf")),
            P(None, ("groups", "leaf")),
            P(("groups", "leaf"), None),
            P(("groups", "leaf"), None),
            P(("groups", "leaf"), None),
            P("groups", None),
            P("groups", None, None),
        ),
        out_specs=P(None, ("groups", "leaf")),
        check_vma=False,
    )
```

time: 87.1 us -> 65.1 us (0.75)
  the two profiles are of different devices: /device:TPU:0 before, /device:TPU:24 now
where the time goes in v2:
time: 65.1 us; the launch traced here: 63.9 us
  starting transfers between devices  24 us (37%)
  Pallas kernels  19.2 us (29%)
  waiting for transfers between devices  16.4 us (25%)
  local copies, waits for them, and re-layouts  3.03 us (5%)
  other arithmetic  0.97 us (1%)
    pallas_call x15, Pallas kernels, call(): pl.pallas_call(kernel, out_shape=outs, in_specs=[sm if i in smem else hb...  19.2 us
    ppermute x5, waiting for transfers between devices, body(): partner = lax.ppermute(block, 'leaf', [(i, i ^ 1 << bit) for i in range(n)])  8.47 us
    ppermute x5, starting transfers between devices, body(): heard = lax.ppermute(z, 'leaf', [(i, i ^ 1 << bit) for i in range(n)])  6.87 us
    ppermute x1, starting transfers between devices, body(): recv_down = lax.ppermute(send_down, 'leaf', pairs_down)  6.13 us
    ppermute x1, starting transfers between devices, body(): recv_xb = lax.ppermute(x_b, 'leaf', pairs_up + pairs_down)  4.94 us
    ppermute x1, waiting for transfers between devices, body(): back = lax.ppermute(back, 'leaf', pairs_up + pairs_down)  4.15 us
    ppermute x5, waiting for transfers between devices, body(): heard = lax.ppermute(z, 'leaf', [(i, i ^ 1 << bit) for i in range(n)])  3.55 us
    unnamed x25, local copies, waits for them, and re-layouts  3.03 us
  transfers between devices with their start and end apart: 16, of which 11 were waited for; matrix products, arithmetic and copies ran while one was open for 0% of the time, Pallas kernels for 22%

profile of v2, /device:TPU:24, one launch (start us, length us, event | category | flops | bytes accessed | tf_op | source)
XLA Modules:
  0.0 63.9 jit_solution(18078449011601636185)
XLA Ops:
  0.0 0.7 %broadcast_subtract_fusion.skel_ref = s32[30,64]{1,0:T(8,128)S(1)} fusion(s32[30,64]{1,0:T(8,128)} %param.13, s32[]{:T(128)S(6)} %mul.10), kind=kLoop, calls=%fused_computation.6 | loop fusion | flops 1920 | bytes 15364 | tf_op jit(solution)/shard_map/sub | solution.py:122
  0.7 1.9 %copy-done = bf16[768,2048]{1,0:T(8,128)(2,1)S(1)} copy-done((bf16[768,2048]{1,0:T(8,128)(2,1)S(1)}, bf16[768,2048]{1,0:T(8,128)(2,1)}, u32[]{:S(2)}) %copy-start) | copy-done | bytes 3145752
  2.6 1.1 %pick.1 = (bf16[8,768]{1,0:T(8,128)(2,1)S(1)}, bf16[8,768]{1,0:T(8,128)(2,1)S(1)}, bf16[16,768]{1,0:T(8,128)(2,1)S(1)}, bf16[32,768]{1,0:T(8,128)(2,1)S(1)}) custom-call(s32[30,64]{1,0:T(8,128)S(1)} %broadcast_subtract_fusion.skel_ref, bf16[768,2048]{1,0:T(8,128)(2,1)S(1)} %copy-done), custom_call_target="tpu_custom_call" | custom-call | flops 335544320 | bytes 6291456 | tf_op jit(solution)/shard_map/pick/pallas_call | solution.py:50
  3.8 0.4 collective-permute-start
  4.2 0.1 copy.9
  4.3 0.1 broadcast_add_fusion
  4.3 0.1 select_reduce_fusion.mult_ref.refs_0_
  4.4 0.1 copy-done.1
  4.5 0.9 %copy-done.3 = bf16[32,2048]{1,0:T(8,128)(2,1)S(1)} copy-done((bf16[32,2048]{1,0:T(8,128)(2,1)S(1)}, bf16[32,2048]{1,0:T(8,128)(2,1)}, u32[]{:S(2)}) %copy-start.3) | copy-done | bytes 131096
  5.4 1.6 %tree.1 = (bf16[32,2048]{1,0:T(8,128)(2,1)S(1)}, s32[1,2048]{1,0:T(1,128)S(1)}, f32[1,2048]{1,0:T(1,128)S(1)}, bf16[32,768]{1,0:T(8,128)(2,1)S(1)}, bf16[48,768]{1,0:T(8,128)(2,1)S(1)}) custom-call(s32[1,2048]{1,0:T(1,128)S(1)} %copy-done.4, bf16[32,2048]{1,0:T(8,128)(2,1)S(1)} %copy-done.3, bf16[768,2048]{1,0:T(8,128)(2,1)S(1)} %copy-done.1, ...), custom_call_target="tpu_custom_call" | custom-call | flops 1342177280 | bytes 1048576 | tf_op jit(solution)/shard_map/tree/pallas_call | solution.py:50
  7.0 0.4 cut.1
  7.4 1.0 %collective-permute-done.refs_1_ = bf16[8,768]{1,0:T(8,128)(2,1)S(1)} collective-permute-done((bf16[8,768]{1,0:T(8,128)(2,1)S(1)}, bf16[8,768]{1,0:T(8,128)(2,1)S(1)}, u32[]{:S(2)}, u32[]{:S(2)}) %collective-permute-start) | collective-permute-done | bytes 12320 | tf_op jit(solution)/shard_map/ppermute | solution.py:300
  8.4 1.3 %collective-permute-start.3 = (bf16[768,512]{1,0:T(8,128)(2,1)S(1)}, bf16[768,512]{1,0:T(8,128)(2,1)S(1)}, u32[]{:S(2)}, u32[]{:S(2)}) collective-permute-start(bf16[768,512]{1,0:T(8,128)(2,1)S(1)} %get-tuple-element.73), channel_id=1, source_target_pairs={{1,2},{3,4},{5,6},{7,8},{9,10},{11,12},{13,14},{15,16},{17,18},{19... | collective-permute-start | bytes 2359304 | tf_op jit(solution)/shard_map/ppermute | solution.py:302
  9.7 6.1 %collective-permute-start.4 = (bf16[768,256]{1,0:T(8,128)(2,1)S(1)}, bf16[768,256]{1,0:T(8,128)(2,1)S(1)}, u32[]{:S(2)}, u32[]{:S(2)}) collective-permute-start(bf16[768,256]{1,0:T(8,128)(2,1)S(1)} %get-tuple-element.74), channel_id=1, source_target_pairs={{2,1},{4,3},{6,5},{8,7},{10,9},{12,11},{14,13},{16,15},{18,17},{20... | collective-permute-start | bytes 1179656 | tf_op jit(solution)/shard_map/ppermute | solution.py:303
  15.9 0.5 collective-permute-start.1
  16.4 2.0 %near0.1.rest_0_ = f32[32,2048]{1,0:T(8,128)S(1)} custom-call(f32[8,7]{1,0:T(8,128)S(1)} %select_reduce_fusion.mult_ref.refs_0_, bf16[768,2048]{1,0:T(8,128)(2,1)S(1)} %copy-done.1, bf16[32,2048]{1,0:T(8,128)(2,1)S(1)} %get-tuple-element.83.refs_2_.x_ref, f32[1,2048]{1,0:T(1,128)S(1)} %get-tuple-element.66.refs_3_.hn_ref), custom_call_target="tpu_custom_call" | custom-call | flops 2013265920 | bytes 6291456 | tf_op jit(solution)/shard_map/near0/pallas_call | solution.py:50
  18.4 3.2 %collective-permute-done.1.refs_1_ = bf16[24,768]{1,0:T(8,128)(2,1)S(1)} collective-permute-done((bf16[24,768]{1,0:T(8,128)(2,1)S(1)}, bf16[24,768]{1,0:T(8,128)(2,1)S(1)}, u32[]{:S(2)}, u32[]{:S(2)}) %collective-permute-start.1) | collective-permute-done | bytes 36896 | tf_op jit(solution)/shard_map/ppermute | solution.py:300
  21.6 2.0 %near2.1.rest_1_ = f32[32,2048]{1,0:T(8,128)S(1)} custom-call(f32[8,7]{1,0:T(8,128)S(1)} %select_reduce_fusion.mult_ref.refs_0_, bf16[768,2048]{1,0:T(8,128)(2,1)S(1)} %copy-done.1, bf16[32,2048]{1,0:T(8,128)(2,1)S(1)} %get-tuple-element.83.refs_2_.x_ref, f32[1,2048]{1,0:T(1,128)S(1)} %get-tuple-element.66.refs_3_.hn_ref), custom_call_target="tpu_custom_call" | custom-call | flops 2013265920 | bytes 6291456 | tf_op jit(solution)/shard_map/near2/pallas_call | solution.py:50
  23.6 2.6 %collective-permute-done.2.refs_1_ = bf16[64,768]{1,0:T(8,128)(2,1)S(1)} collective-permute-done((bf16[64,768]{1,0:T(8,128)(2,1)S(1)}, bf16[64,768]{1,0:T(8,128)(2,1)S(1)}, u32[]{:S(2)}, u32[]{:S(2)}) %collective-permute-start.2) | collective-permute-done | bytes 98336 | tf_op jit(solution)/shard_map/ppermute | solution.py:300
  26.2 0.1 collective-permute-start.5
  26.3 0.0 copy-start.6
  26.3 0.0 copy-start.7
  26.3 0.0 copy-start.8
  26.3 0.0 copy-start.9
  26.4 0.0 copy-start.10
  26.4 1.6 %collective-permute-start.7 = (bf16[32,768]{1,0:T(8,128)(2,1)S(1)}, bf16[32,768]{1,0:T(8,128)(2,1)S(1)}, u32[]{:S(2)}, u32[]{:S(2)}) collective-permute-start(bf16[32,768]{1,0:T(8,128)(2,1)S(1)} %get-tuple-element.80), channel_id=1, source_target_pairs={{0,1},{1,0},{2,3},{3,2},{4,5},{5,4},{6,7},{7,6},{8,9},{9,8},{10,11... | collective-permute-start | bytes 147464 | tf_op jit(solution)/shard_map/ppermute | solution.py:307
  28.0 4.9 %collective-permute-start.8 = (bf16[48,768]{1,0:T(8,128)(2,1)S(1)}, bf16[48,768]{1,0:T(8,128)(2,1)S(1)}, u32[]{:S(2)}, u32[]{:S(2)}) collective-permute-start(bf16[48,768]{1,0:T(8,128)(2,1)S(1)} %get-tuple-element.77), channel_id=1, source_target_pairs={{1,2},{3,4},{5,6},{7,8},{9,10},{11,12},{13,14},{15,16},{17,18},{19... | collective-permute-start | bytes 221192 | tf_op jit(solution)/shard_map/ppermute | solution.py:311
  33.0 2.4 %near4.1.rest_2_ = f32[32,2048]{1,0:T(8,128)S(1)} custom-call(f32[8,7]{1,0:T(8,128)S(1)} %select_reduce_fusion.mult_ref.refs_0_, bf16[768,2048]{1,0:T(8,128)(2,1)S(1)} %copy-done.1, bf16[32,2048]{1,0:T(8,128)(2,1)S(1)} %get-tuple-element.83.refs_2_.x_ref, f32[1,2048]{1,0:T(1,128)S(1)} %get-tuple-element.66.refs_3_.hn_ref), custom_call_target="tpu_custom_call" | custom-call | flops 2013265920 | bytes 6291456 | tf_op jit(solution)/shard_map/near4/pallas_call | solution.py:50
  35.3 0.2 collective-permute-done.8.xs_ref
  35.6 0.2 collective-permute-start.9
  35.9 1.6 %collective-permute-done.9.other_ref = bf16[320,768]{1,0:T(8,128)(2,1)S(1)} collective-permute-done((bf16[320,768]{1,0:T(8,128)(2,1)S(1)}, bf16[320,768]{1,0:T(8,128)(2,1)S(1)}, u32[]{:S(2)}, u32[]{:S(2)}) %collective-permute-start.9) | collective-permute-done | bytes 491552 | tf_op jit(solution)/shard_map/ppermute | solution.py:300
  37.6 2.0 %own.1 = f32[32,256]{1,0:T(8,128)S(1)} custom-call(bf16[320,768]{1,0:T(8,128)(2,1)S(1)} %join.7.block_ref, bf16[320,768]{1,0:T(8,128)(2,1)S(1)} %collective-permute-done.9.other_ref, s32[1,640]{1,0:T(1,128)S(1)} %add_select_fusion.dest_ref, bf16[768,2048]{1,0:T(8,128)(2,1)S(1)} %copy-done.1, bf16[32,2048]{1,0:T(8,128)(2,1)S(1)} %get-tuple-element.83.refs_2_.x_ref, ...), custom_call_target="tpu_custom_call" | custom-call | flops 1677721600 | bytes 4194304 | tf_op jit(solution)/shard_map/own/pallas_call | solution.py:50
  39.5 0.2 collective-permute-start.10
  39.7 1.1 %collective-permute-done.10 = f32[32,256]{1,0:T(8,128)S(1)} collective-permute-done((f32[32,256]{1,0:T(8,128)S(1)}, f32[32,256]{1,0:T(8,128)S(1)}, u32[]{:S(2)}, u32[]{:S(2)}) %collective-permute-start.10) | collective-permute-done | bytes 32800 | tf_op jit(solution)/shard_map/ppermute | solution.py:518
  40.8 2.1 %collective-permute-start.11 = (f32[32,256]{1,0:T(8,128)S(1)}, f32[32,256]{1,0:T(8,128)S(1)}, u32[]{:S(2)}, u32[]{:S(2)}) collective-permute-start(f32[32,256]{1,0:T(8,128)S(1)} %select_select_fusion.4), channel_id=1, source_target_pairs={{0,2},{1,3},{2,0},{3,1},{4,6},{5,7},{6,4},{7,5},{8,10},{9,11},{10,... | collective-permute-start | bytes 98312 | tf_op jit(solution)/shard_map/ppermute | solution.py:518
  42.8 1.6 %edge_chip.1 = (f32[32,2048]{1,0:T(8,128)S(1)}, f32[32,512]{1,0:T(8,128)S(1)}) custom-call(f32[8,7]{1,0:T(8,128)S(1)} %select_reduce_fusion.mult_ref.refs_0_, bf16[768,2048]{1,0:T(8,128)(2,1)S(1)} %copy-done.1, f32[1,2048]{1,0:T(1,128)S(1)} %get-tuple-element.66.refs_3_.hn_ref, bf16[32,2048]{1,0:T(8,128)(2,1)S(1)} %get-tuple-element.83.refs_2_.x_ref, ...), custom_call_target="tpu_custom_call" | custom-call | flops 1006632960 | bytes 4194304 | tf_op jit(solution)/shard_map/edge_chip/pallas_call | solution.py:50
  44.4 0.4 collective-permute-done.11
  44.8 1.9 %collective-permute-start.12 = (f32[32,256]{1,0:T(8,128)S(1)}, f32[32,256]{1,0:T(8,128)S(1)}, u32[]{:S(2)}, u32[]{:S(2)}) collective-permute-start(f32[32,256]{1,0:T(8,128)S(1)} %select_select_fusion.3), channel_id=1, source_target_pairs={{0,4},{1,5},{2,6},{3,7},{4,0},{5,1},{6,2},{7,3},{8,12},{9,13},{10,... | collective-permute-start | bytes 98312 | tf_op jit(solution)/shard_map/ppermute | solution.py:518
  46.7 1.7 %far.1.far_ref = bf16[256,2048]{1,0:T(8,128)(2,1)S(1)} custom-call(bf16[320,768]{1,0:T(8,128)(2,1)S(1)} %join.7.block_ref, bf16[320,768]{1,0:T(8,128)(2,1)S(1)} %collective-permute-done.9.other_ref, s32[1,640]{1,0:T(1,128)S(1)} %add_select_fusion.dest_ref, bf16[768,2048]{1,0:T(8,128)(2,1)S(1)} %copy-done.1, f32[1,2048]{1,0:T(1,128)S(1)} %get-tuple-element.66.refs_3_.hn_ref), custom_call_target="tpu_custom_call" | custom-call | flops 1006632960 | bytes 4194304 | tf_op jit(solution)/shard_map/far/pallas_call | solution.py:50
  48.4 0.3 collective-permute-done.12
  48.8 1.1 %collective-permute-start.13 = (f32[32,256]{1,0:T(8,128)S(1)}, f32[32,256]{1,0:T(8,128)S(1)}, u32[]{:S(2)}, u32[]{:S(2)}) collective-permute-start(f32[32,256]{1,0:T(8,128)S(1)} %select_select_fusion.2), channel_id=1, source_target_pairs={{0,8},{1,9},{2,10},{3,11},{4,12},{5,13},{6,14},{7,15},{8,0},{9,1},... | collective-permute-start | bytes 98312 | tf_op jit(solution)/shard_map/ppermute | solution.py:518
  49.8 2.4 %edge_core.1.rest_3_ = f32[32,2048]{1,0:T(8,128)S(1)} custom-call(f32[8,7]{1,0:T(8,128)S(1)} %select_reduce_fusion.mult_ref.refs_0_, bf16[768,2048]{1,0:T(8,128)(2,1)S(1)} %copy-done.1, f32[1,2048]{1,0:T(1,128)S(1)} %get-tuple-element.66.refs_3_.hn_ref, bf16[768,768]{1,0:T(8,128)(2,1)S(1)} %collective-permute-done.6.src_ref, ...), custom_call_target="tpu_custom_call" | custom-call | flops 1006632960 | bytes 3145728 | tf_op jit(solution)/shard_map/edge_core/pallas_call | solution.py:50
  52.2 0.5 collective-permute-done.13
  52.8 1.7 %collective-permute-start.14 = (f32[32,256]{1,0:T(8,128)S(1)}, f32[32,256]{1,0:T(8,128)S(1)}, u32[]{:S(2)}, u32[]{:S(2)}) collective-permute-start(f32[32,256]{1,0:T(8,128)S(1)} %select_select_fusion.1), channel_id=1, source_target_pairs={{0,16},{1,17},{2,18},{3,19},{4,20},{5,21},{6,22},{7,23},{8,24},{9,... | collective-permute-start | bytes 98312 | tf_op jit(solution)/shard_map/ppermute | solution.py:518
  54.4 1.9 %collective-permute-start.15 = (f32[32,512]{1,0:T(8,128)S(1)}, f32[32,512]{1,0:T(8,128)S(1)}, u32[]{:S(2)}, u32[]{:S(2)}) collective-permute-start(f32[32,512]{1,0:T(8,128)S(1)} %get-tuple-element.102), channel_id=1, source_target_pairs={{1,2},{3,4},{5,6},{7,8},{9,10},{11,12},{13,14},{15,16},{17,18},{19... | collective-permute-start | bytes 196616 | tf_op jit(solution)/shard_map/ppermute | solution.py:523
  56.3 1.3 %collective-permute-done.14 = f32[32,256]{1,0:T(8,128)S(1)} collective-permute-done((f32[32,256]{1,0:T(8,128)S(1)}, f32[32,256]{1,0:T(8,128)S(1)}, u32[]{:S(2)}, u32[]{:S(2)}) %collective-permute-start.14) | collective-permute-done | bytes 32800 | tf_op jit(solution)/shard_map/ppermute | solution.py:518
  57.6 4.1 %collective-permute-done.15.back_ref = f32[32,512]{1,0:T(8,128)S(1)} collective-permute-done((f32[32,512]{1,0:T(8,128)S(1)}, f32[32,512]{1,0:T(8,128)S(1)}, u32[]{:S(2)}, u32[]{:S(2)}) %collective-permute-start.15) | collective-permute-done | bytes 65568 | tf_op jit(solution)/shard_map/ppermute | solution.py:523
  61.8 2.1 %last.1 = f32[32,2048]{1,0:T(8,128)} custom-call(f32[32,256]{1,0:T(8,128)S(1)} %select_select_fusion.z_ref, f32[30,64,64]{2,1,0:T(8,128)S(1)} %copy-done.2, bf16[256,2048]{1,0:T(8,128)(2,1)S(1)} %far.1.far_ref, f32[32,512]{1,0:T(8,128)S(1)} %collective-permute-done.15.back_ref, s32[1,2048]{1,0:T(1,128)S(1)} %get-tuple-element.103.inv_ref, ...), custom_call_target="tpu_custom_call" | custom-call | flops 1006632960 | bytes 2097152 | tf_op jit(solution)/shard_map/last/pallas_call | solution.py:50
  (41 shorter events, 0.2 us)
Async XLA Ops:
  0.7 1.9 %copy-start = (bf16[768,2048]{1,0:T(8,128)(2,1)S(1)}, bf16[768,2048]{1,0:T(8,128)(2,1)}, u32[]{:S(2)}) copy-start(bf16[768,2048]{1,0:T(8,128)(2,1)} %emb_ref.10) | copy-start | bytes 9437188
  2.6 1.6 %copy-start.5 = (s32[8,7]{1,0:T(8,128)S(1)}, s32[8,7]{1,0:T(8,128)}, u32[]{:S(2)}) copy-start(s32[8,7]{1,0:T(8,128)} %param.11) | copy-start | bytes 676
  2.6 1.6 %copy-start.11 = (s32[1,8]{1,0:T(1,128)S(1)}, s32[1,8]{1,0:T(1,128)}, u32[]{:S(2)}) copy-start(s32[1,8]{1,0:T(1,128)} %param.12) | copy-start | bytes 100
  2.6 1.9 %copy-start.1 = (bf16[768,2048]{1,0:T(8,128)(2,1)S(1)}, bf16[768,2048]{1,0:T(8,128)(2,1)}, u32[]{:S(2)}) copy-start(bf16[768,2048]{1,0:T(8,128)(2,1)} %emb_ref.10) | copy-start | bytes 9437188
  2.6 1.9 %copy-start.4 = (s32[1,2048]{1,0:T(1,128)S(1)}, s32[1,2048]{1,0:T(1,128)}, u32[]{:S(2)}) copy-start(s32[1,2048]{1,0:T(1,128)} %order_ref.1) | copy-start | bytes 24580
  3.8 4.7 %collective-permute-start = (bf16[8,768]{1,0:T(8,128)(2,1)S(1)}, bf16[8,768]{1,0:T(8,128)(2,1)S(1)}, u32[]{:S(2)}, u32[]{:S(2)}) collective-permute-start(bf16[8,768]{1,0:T(8,128)(2,1)S(1)} %get-tuple-element.57.refs_0_), channel_id=1, source_target_pairs={{0,16},{1,17},{2,18},{3,19},{4,20},{5,21},{6,22},{7,23},{8,24},{9,... | collective-permute-start | bytes 36872 | tf_op jit(solution)/shard_map/ppermute | solution.py:300
  4.5 0.9 %copy-start.3 = (bf16[32,2048]{1,0:T(8,128)(2,1)S(1)}, bf16[32,2048]{1,0:T(8,128)(2,1)}, u32[]{:S(2)}) copy-start(bf16[32,2048]{1,0:T(8,128)(2,1)} %probes_ref.1) | copy-start | bytes 393220
  8.4 27.1 %collective-permute-start.6 = (bf16[768,768]{1,0:T(8,128)(2,1)S(1)}, bf16[768,768]{1,0:T(8,128)(2,1)S(1)}, u32[]{:S(2)}, u32[]{:S(2)}) collective-permute-start(bf16[768,768]{1,0:T(8,128)(2,1)S(1)} %get-tuple-element.69), channel_id=1, source_target_pairs={{0,1},{1,0},{2,3},{3,2},{4,5},{5,4},{6,7},{7,6},{8,9},{9,8},{10,11... | collective-permute-start | bytes 3538952 | tf_op jit(solution)/shard_map/ppermute | solution.py:306
  8.4 17.8 %collective-permute-start.3 = (bf16[768,512]{1,0:T(8,128)(2,1)S(1)}, bf16[768,512]{1,0:T(8,128)(2,1)S(1)}, u32[]{:S(2)}, u32[]{:S(2)}) collective-permute-start(bf16[768,512]{1,0:T(8,128)(2,1)S(1)} %get-tuple-element.73), channel_id=1, source_target_pairs={{1,2},{3,4},{5,6},{7,8},{9,10},{11,12},{13,14},{15,16},{17,18},{19... | collective-permute-start | bytes 2359304 | tf_op jit(solution)/shard_map/ppermute | solution.py:302
  9.7 16.5 %collective-permute-start.4 = (bf16[768,256]{1,0:T(8,128)(2,1)S(1)}, bf16[768,256]{1,0:T(8,128)(2,1)S(1)}, u32[]{:S(2)}, u32[]{:S(2)}) collective-permute-start(bf16[768,256]{1,0:T(8,128)(2,1)S(1)} %get-tuple-element.74), channel_id=1, source_target_pairs={{2,1},{4,3},{6,5},{8,7},{10,9},{12,11},{14,13},{16,15},{18,17},{20... | collective-permute-start | bytes 1179656 | tf_op jit(solution)/shard_map/ppermute | solution.py:303
  15.9 5.7 %collective-permute-start.1 = (bf16[24,768]{1,0:T(8,128)(2,1)S(1)}, bf16[24,768]{1,0:T(8,128)(2,1)S(1)}, u32[]{:S(2)}, u32[]{:S(2)}) collective-permute-start(bf16[24,768]{1,0:T(8,128)(2,1)S(1)} %join.4.refs_0_), channel_id=1, source_target_pairs={{0,8},{1,9},{2,10},{3,11},{4,12},{5,13},{6,14},{7,15},{8,0},{9,1},... | collective-permute-start | bytes 110600 | tf_op jit(solution)/shard_map/ppermute | solution.py:300
  21.6 4.6 %collective-permute-start.2 = (bf16[64,768]{1,0:T(8,128)(2,1)S(1)}, bf16[64,768]{1,0:T(8,128)(2,1)S(1)}, u32[]{:S(2)}, u32[]{:S(2)}) collective-permute-start(bf16[64,768]{1,0:T(8,128)(2,1)S(1)} %join.5.refs_0_), channel_id=1, source_target_pairs={{0,4},{1,5},{2,6},{3,7},{4,0},{5,1},{6,2},{7,3},{8,12},{9,13},{10,... | collective-permute-start | bytes 294920 | tf_op jit(solution)/shard_map/ppermute | solution.py:300
  26.2 9.4 %collective-permute-start.5 = (bf16[160,768]{1,0:T(8,128)(2,1)S(1)}, bf16[160,768]{1,0:T(8,128)(2,1)S(1)}, u32[]{:S(2)}, u32[]{:S(2)}) collective-permute-start(bf16[160,768]{1,0:T(8,128)(2,1)S(1)} %join.6.refs_0_), channel_id=1, source_target_pairs={{0,2},{1,3},{2,0},{3,1},{4,6},{5,7},{6,4},{7,5},{8,10},{9,11},{10,... | collective-permute-start | bytes 737288 | tf_op jit(solution)/shard_map/ppermute | solution.py:300
  26.3 9.6 %copy-start.6 = (pred[1,640]{1,0:T(4,128)(4,1)S(1)}, pred[1,640]{1,0:T(4,128)(4,1)}, u32[]{:S(2)}) copy-start(pred[1,640]{1,0:T(4,128)(4,1)} %constant.68) | copy-start | bytes 1924
  26.3 9.6 %copy-start.7 = (s32[1,640]{1,0:T(1,128)S(1)}, s32[1,640]{1,0:T(1,128)}, u32[]{:S(2)}) copy-start(s32[1,640]{1,0:T(1,128)} %constant.69) | copy-start | bytes 7684
  26.3 9.6 %copy-start.8 = (s32[1,640]{1,0:T(1,128)S(1)}, s32[1,640]{1,0:T(1,128)}, u32[]{:S(2)}) copy-start(s32[1,640]{1,0:T(1,128)} %constant.70) | copy-start | bytes 7684
  26.3 9.5 %copy-start.9 = (s32[1,640]{1,0:T(1,128)S(1)}, s32[1,640]{1,0:T(1,128)}, u32[]{:S(2)}) copy-start(s32[1,640]{1,0:T(1,128)} %constant.71) | copy-start | bytes 7684
  26.4 9.5 %copy-start.10 = (s32[1,640]{1,0:T(1,128)S(1)}, s32[1,640]{1,0:T(1,128)}, u32[]{:S(2)}) copy-start(s32[1,640]{1,0:T(1,128)} %constant.72) | copy-start | bytes 7684
  26.4 9.0 %collective-permute-start.7 = (bf16[32,768]{1,0:T(8,128)(2,1)S(1)}, bf16[32,768]{1,0:T(8,128)(2,1)S(1)}, u32[]{:S(2)}, u32[]{:S(2)}) collective-permute-start(bf16[32,768]{1,0:T(8,128)(2,1)S(1)} %get-tuple-element.80), channel_id=1, source_target_pairs={{0,1},{1,0},{2,3},{3,2},{4,5},{5,4},{6,7},{7,6},{8,9},{9,8},{10,11... | collective-permute-start | bytes 147464 | tf_op jit(solution)/shard_map/ppermute | solution.py:307
  28.0 7.6 %collective-permute-start.8 = (bf16[48,768]{1,0:T(8,128)(2,1)S(1)}, bf16[48,768]{1,0:T(8,128)(2,1)S(1)}, u32[]{:S(2)}, u32[]{:S(2)}) collective-permute-start(bf16[48,768]{1,0:T(8,128)(2,1)S(1)} %get-tuple-element.77), channel_id=1, source_target_pairs={{1,2},{3,4},{5,6},{7,8},{9,10},{11,12},{13,14},{15,16},{17,18},{19... | collective-permute-start | bytes 221192 | tf_op jit(solution)/shard_map/ppermute | solution.py:311
  35.6 1.9 %collective-permute-start.9 = (bf16[320,768]{1,0:T(8,128)(2,1)S(1)}, bf16[320,768]{1,0:T(8,128)(2,1)S(1)}, u32[]{:S(2)}, u32[]{:S(2)}) collective-permute-start(bf16[320,768]{1,0:T(8,128)(2,1)S(1)} %join.7.block_ref), channel_id=1, source_target_pairs={{0,1},{1,0},{2,3},{3,2},{4,5},{5,4},{6,7},{7,6},{8,9},{9,8},{10,11... | collective-permute-start | bytes 1474568 | tf_op jit(solution)/shard_map/ppermute | solution.py:300
  39.5 1.2 %collective-permute-start.10 = (f32[32,256]{1,0:T(8,128)S(1)}, f32[32,256]{1,0:T(8,128)S(1)}, u32[]{:S(2)}, u32[]{:S(2)}) collective-permute-start(f32[32,256]{1,0:T(8,128)S(1)} %own.1), channel_id=1, source_target_pairs={{0,1},{1,0},{2,3},{3,2},{4,5},{5,4},{6,7},{7,6},{8,9},{9,8},{10,11... | collective-permute-start | bytes 98312 | tf_op jit(solution)/shard_map/ppermute | solution.py:518
  40.8 4.0 %collective-permute-start.11 = (f32[32,256]{1,0:T(8,128)S(1)}, f32[32,256]{1,0:T(8,128)S(1)}, u32[]{:S(2)}, u32[]{:S(2)}) collective-permute-start(f32[32,256]{1,0:T(8,128)S(1)} %select_select_fusion.4), channel_id=1, source_target_pairs={{0,2},{1,3},{2,0},{3,1},{4,6},{5,7},{6,4},{7,5},{8,10},{9,11},{10,... | collective-permute-start | bytes 98312 | tf_op jit(solution)/shard_map/ppermute | solution.py:518
  44.8 4.0 %collective-permute-start.12 = (f32[32,256]{1,0:T(8,128)S(1)}, f32[32,256]{1,0:T(8,128)S(1)}, u32[]{:S(2)}, u32[]{:S(2)}) collective-permute-start(f32[32,256]{1,0:T(8,128)S(1)} %select_select_fusion.3), channel_id=1, source_target_pairs={{0,4},{1,5},{2,6},{3,7},{4,0},{5,1},{6,2},{7,3},{8,12},{9,13},{10,... | collective-permute-start | bytes 98312 | tf_op jit(solution)/shard_map/ppermute | solution.py:518
  48.7 13.0 %copy-start.2 = (f32[30,64,64]{2,1,0:T(8,128)S(1)}, f32[30,64,64]{2,1,0:T(8,128)}, u32[]{:S(2)}) copy-start(f32[30,64,64]{2,1,0:T(8,128)} %core_ref.1) | copy-start | bytes 1474564
  48.8 4.0 %collective-permute-start.13 = (f32[32,256]{1,0:T(8,128)S(1)}, f32[32,256]{1,0:T(8,128)S(1)}, u32[]{:S(2)}, u32[]{:S(2)}) collective-permute-start(f32[32,256]{1,0:T(8,128)S(1)} %select_select_fusion.2), channel_id=1, source_target_pairs={{0,8},{1,9},{2,10},{3,11},{4,12},{5,13},{6,14},{7,15},{8,0},{9,1},... | collective-permute-start | bytes 98312 | tf_op jit(solution)/shard_map/ppermute | solution.py:518
  52.8 4.9 %collective-permute-start.14 = (f32[32,256]{1,0:T(8,128)S(1)}, f32[32,256]{1,0:T(8,128)S(1)}, u32[]{:S(2)}, u32[]{:S(2)}) collective-permute-start(f32[32,256]{1,0:T(8,128)S(1)} %select_select_fusion.1), channel_id=1, source_target_pairs={{0,16},{1,17},{2,18},{3,19},{4,20},{5,21},{6,22},{7,23},{8,24},{9,... | collective-permute-start | bytes 98312 | tf_op jit(solution)/shard_map/ppermute | solution.py:518
  54.4 7.4 %collective-permute-start.15 = (f32[32,512]{1,0:T(8,128)S(1)}, f32[32,512]{1,0:T(8,128)S(1)}, u32[]{:S(2)}, u32[]{:S(2)}) collective-permute-start(f32[32,512]{1,0:T(8,128)S(1)} %get-tuple-element.102), channel_id=1, source_target_pairs={{1,2},{3,4},{5,6},{7,8},{9,10},{11,12},{13,14},{15,16},{17,18},{19... | collective-permute-start | bytes 196616 | tf_op jit(solution)/shard_map/ppermute | solution.py:523

commit v3 on v2

v3 whole, which is shorter than its diff:
```python
import jax
import jax.numpy as jnp
from jax import lax
from jax.experimental import pallas as pl
from jax.experimental.pallas import tpu as pltpu
from jax.sharding import PartitionSpec as P

LEAF = 256
R = 64
LEVELS = 4
W = 3
F32 = jnp.float32
BF16 = jnp.bfloat16
VMEM_LIMIT = 14 * 1024 * 1024
LANES = 128
PREP_VMEM = 16 * 1024 * 1024
UP = 2


def dot(a, b):
    return jnp.dot(a, b, preferred_element_type=F32)


def dot_nt(a, b):
    return lax.dot_general(a, b, (((1,), (1,)), ((), ())), preferred_element_type=F32)


def dot_tn(a, b):
    return lax.dot_general(a, b, (((0,), (0,)), ((), ())), preferred_element_type=F32)


def half_norm_row(emb):
    e = emb.astype(F32)
    return 0.5 * jnp.sum(e * e, axis=0, keepdims=True)


def half_norm_col(rows):
    e = rows.astype(F32)
    return 0.5 * jnp.sum(e * e, axis=1, keepdims=True)


def col_of(row):
    return jnp.transpose(jnp.broadcast_to(row, (8, row.shape[1])))[:, 0:1]


def call(kernel, outs, *args, scratch=(), smem=(), hbm=(), flops=0, nbytes=0, name=None, vmem=VMEM_LIMIT):
    single = not isinstance(outs, (list, tuple))
    vm = pl.BlockSpec(memory_space=pltpu.VMEM)
    sm = pl.BlockSpec(memory_space=pltpu.SMEM)
    hb = pl.BlockSpec(memory_space=pltpu.HBM)
    return pl.pallas_call(
        kernel,
        out_shape=outs,
        in_specs=[sm if i in smem else hb if i in hbm else vm for i in range(len(args))],
        out_specs=vm if single else [vm] * len(outs),
        scratch_shapes=list(scratch),
        compiler_params=pltpu.CompilerParams(vmem_limit_bytes=vmem),
        cost_estimate=pl.CostEstimate(flops=0, bytes_accessed=0, transcendentals=0),
        name=name,
    )(*args)


class Plan:
    def __init__(self, n):
        self.n = n
        self.bits = n.bit_length() - 1
        self.slots = [R * 2 ** (l + 1) // n for l in range(LEVELS)]
        self.padded = [-(-s // 8) * 8 for s in self.slots]
        self.starts = [sum(self.padded[:l]) for l in range(LEVELS)]
        self.rows = sum(self.padded)
        self.shift = [self.bits - 1 - l for l in range(LEVELS)]
        entries, size = [], 0
        for bit in reversed(range(self.bits)):
            level = self.bits - 1 - bit
            if level < LEVELS:
                entries.append((level, 0, size))
                size += self.padded[level]
            entries += [(lev, off ^ (1 << bit), row + size) for lev, off, row in entries]
            size *= 2
        self.entries, self.size = entries, size


def body(embeddings, probes, order, near_list, near_count, skeleton, core):
    n = lax.axis_size("leaf")
    plan = Plan(n)
    pos = lax.axis_index("leaf")
    width, points = embeddings.shape
    cols = probes.shape[0]
    leaves = points // LEAF
    halo = W * LEAF

    groups = points // LANES
    last = points - halo
    extra = 16
    slabs = 4
    slab = width // slabs
    reach = 2 * W + 1

    pairs_a = [(i, i ^ 1) for i in range(n)]

    def pairs(*starts):
        up = [(i, i + 1) for at in starts for i in range(at, n - 1, 4)]
        return up + [(j, i) for i, j in up]

    def cut_kernel(emb_ref, x_ref, a_ref, sem):
        odd = jnp.bitwise_and(lax.axis_index("leaf"), 1)
        at = pl.multiple_of((1 - odd) * last, LEAF)
        copy = pltpu.make_async_copy(
            emb_ref.at[:, pl.ds(at, halo)], a_ref.at[pl.ds(0, width), :], sem.at[0]
        )
        copy.start()
        ends = jnp.where(odd == 1, x_ref[:, :halo].astype(F32), x_ref[:, last:].astype(F32))
        a_ref[width:, :] = ends.astype(BF16)
        copy.wait()

    def cut_core(emb, x_tree):
        return call(
            cut_kernel,
            jax.ShapeDtypeStruct((width + cols, halo), BF16),
            emb,
            x_tree,
            scratch=[pltpu.SemaphoreType.DMA((1,))],
            name="cut",
        )

    def fill(b_ref, x_ref, mult_ref):
        odd = jnp.bitwise_and(lax.axis_index("leaf"), 1)

        def tell(pairs):
            rows = [mult_ref[(o + W) * leaves + t : (o + W) * leaves + t + 1, :] for t, o in pairs]
            rows.append(jnp.zeros((extra - len(rows), LANES), F32))
            b_ref[width + cols :, 0:LANES] = jnp.concatenate(rows, axis=0).astype(BF16)
            b_ref[width + cols :, LANES:] = jnp.zeros((extra, UP * LEAF - LANES), BF16)

        @pl.when(odd == 0)
        def _():
            b_ref[width : width + cols, :] = x_ref[:, : UP * LEAF]
            tell([(0, -1 - q) for q in range(W)])

        @pl.when(odd == 1)
        def _():
            b_ref[width : width + cols, :] = x_ref[:, points - UP * LEAF :]
            tell([(leaves - 1, 2), (leaves - 1, 3), (leaves - 2, 3)])

    def cut_chip_kernel(emb_ref, x_ref, mult_ref, b_ref, sem):
        odd = jnp.bitwise_and(lax.axis_index("leaf"), 1)
        at = pl.multiple_of(odd * (points - UP * LEAF), LEAF)
        copy = pltpu.make_async_copy(
            emb_ref.at[:, pl.ds(at, UP * LEAF)], b_ref.at[pl.ds(0, width), :], sem.at[0]
        )
        copy.start()
        fill(b_ref, x_ref, mult_ref)
        copy.wait()

    def cut_chip(emb, x_tree):
        return call(
            cut_chip_kernel,
            jax.ShapeDtypeStruct((width + cols + extra, UP * LEAF), BF16),
            emb,
            x_tree,
            mult,
            scratch=[pltpu.SemaphoreType.DMA((1,))],
            name="cut_chip",
        )

    def prep_kernel(
        skel_hbm, order_hbm, probes_hbm, list_hbm, count_hbm, emb_hbm, *rest
    ):
        g_refs, rest = rest[:LEVELS], rest[LEVELS:]
        x_ref, inv_ref, hn_ref, mult_ref = rest[:4]
        emb_ref, skel_ref, order_ref, probes_ref, list_ref, count_ref, row_ref, sems = rest[4:]
        me = lax.axis_index("leaf")
        small = [
            pltpu.make_async_copy(src, dst, sems.at[i])
            for i, (src, dst) in enumerate(
                (
                    (skel_hbm, skel_ref),
                    (order_hbm, order_ref),
                    (probes_hbm, probes_ref),
                    (list_hbm, list_ref),
                    (count_hbm, count_ref),
                )
            )
        ]
        large = [
            pltpu.make_async_copy(
                emb_hbm.at[pl.ds(r * slab, slab), :], emb_ref.at[pl.ds(r * slab, slab), :], sems.at[5 + r]
            )
            for r in range(slabs)
        ]
        for copy in small + large:
            copy.start()
        for copy in small:
            copy.wait()

        lane = lax.broadcasted_iota(jnp.int32, (1, LANES), 1)
        idx = jnp.full((1, LANES), -1, jnp.int32)
        row_ref[...] = jnp.zeros_like(row_ref)
        for l in range(LEVELS):
            node = 2 ** (l + 1) - 2 + jnp.right_shift(me, plan.shift[l])
            row_ref[0:1, 0:R] = skel_ref[pl.ds(node, 1), :]
            within = jnp.bitwise_and(me, (1 << plan.shift[l]) - 1)
            shift = jnp.bitwise_and(plan.starts[l] - within * plan.slots[l] + LANES, LANES - 1)
            rolled = pltpu.roll(row_ref[...], shift, 1)[0:1, :]
            mine = (lane >= plan.starts[l]) & (lane < plan.starts[l] + plan.slots[l])
            idx = jnp.where(mine, rolled - me * points, idx)
        pick = jnp.where(
            lax.broadcasted_iota(jnp.int32, (points, LANES), 0) == idx, 1.0, 0.0
        ).astype(BF16)

        near = list_ref[...]
        slots = near.shape[1]
        sub = lax.broadcasted_iota(jnp.int32, (leaves, leaves), 0)
        here = sub == lax.broadcasted_iota(jnp.int32, (leaves, leaves), 1)
        count = jnp.sum(jnp.where(here, count_ref[...], 0), axis=1, keepdims=True)
        alive = lax.broadcasted_iota(jnp.int32, (leaves, slots), 1) < count
        offset = near - (me * leaves + lax.broadcasted_iota(jnp.int32, (leaves, slots), 0))
        for o in range(reach):
            hits = jnp.where(alive & (offset == o - W), 1.0, 0.0)
            mult_ref[o * leaves : (o + 1) * leaves, :] = jnp.broadcast_to(
                jnp.sum(hits, axis=1, keepdims=True), (leaves, LANES)
            )

        order_row = order_ref[...]
        low = jnp.bitwise_and(order_row, LANES - 1)
        high = jnp.right_shift(order_row, LANES.bit_length() - 1)
        hot = jnp.where(
            lax.broadcasted_iota(jnp.int32, (LANES, points), 0) == low, 1.0, 0.0
        ).astype(BF16)
        stack = jnp.concatenate(
            [probes_ref[:, h * LANES : (h + 1) * LANES] for h in range(groups)], axis=0
        )
        for c in range(leaves):
            sl = slice(c * LEAF, (c + 1) * LEAF)
            y = dot(stack, hot[:, sl])
            x = jnp.zeros((cols, LEAF), F32)
            for h in range(groups):
                x = x + jnp.where(high[:, sl] == h, y[h * cols : (h + 1) * cols], 0.0)
            x_ref[:, sl] = x.astype(BF16)

        k = lax.broadcasted_iota(jnp.int32, (8, points), 1)
        first = lax.broadcasted_iota(jnp.int32, (8, points), 0) == 0
        digits = jnp.where(first, jnp.right_shift(k, 4), jnp.bitwise_and(k, 15)).astype(F32)
        spread = jnp.concatenate(
            [jnp.where(high == h, digits, 0.0) for h in range(groups)], axis=0
        ).astype(BF16)
        found = dot_nt(spread, hot)
        for h in range(groups):
            inv_ref[:, h * LANES : (h + 1) * LANES] = (
                found[8 * h : 8 * h + 1] * 16.0 + found[8 * h + 1 : 8 * h + 2]
            ).astype(jnp.int32)

        hn = jnp.zeros((1, points), F32)
        for r in range(slabs):
            large[r].wait()
            rows = slice(r * slab, (r + 1) * slab)
            picked = jnp.transpose(dot(emb_ref[rows, :], pick))
            for l in range(LEVELS):
                g_refs[l][:, rows] = picked[
                    plan.starts[l] : plan.starts[l] + plan.padded[l]
                ].astype(BF16)
            hn = hn + half_norm_row(emb_ref[rows, :])
        hn_ref[...] = hn

    *owned, x_tree, inv, hn, mult = call(
        prep_kernel,
        [jax.ShapeDtypeStruct((p, width), BF16) for p in plan.padded]
        + [
            jax.ShapeDtypeStruct((cols, points), BF16),
            jax.ShapeDtypeStruct((1, points), jnp.int32),
            jax.ShapeDtypeStruct((1, points), F32),
            jax.ShapeDtypeStruct((reach * leaves, LANES), F32),
        ],
        *[pltpu.with_memory_space_constraint(v, pltpu.HBM) for v in (skeleton, order, probes, near_list, near_count)],
        pltpu.with_memory_space_constraint(embeddings, pltpu.HBM),
        hbm=tuple(range(6)),
        scratch=[
            pltpu.VMEM((width, points), BF16),
            pltpu.VMEM(skeleton.shape, jnp.int32),
            pltpu.VMEM(order.shape, jnp.int32),
            pltpu.VMEM(probes.shape, BF16),
            pltpu.VMEM(near_list.shape, jnp.int32),
            pltpu.VMEM(near_count.shape, jnp.int32),
            pltpu.VMEM((8, LANES), jnp.int32),
            pltpu.SemaphoreType.DMA((6 + slabs,)),
        ],
        flops=50 * 2 * 256**3,
        nbytes=6 << 20,
        name="prep",
        vmem=PREP_VMEM,
    )

    emb, x_tree = lax.optimization_barrier((embeddings, x_tree))

    def times(mult_ref, t, o, value):
        row = mult_ref[o * leaves + t : o * leaves + t + 1, :]
        return value * jnp.concatenate([row] * (LEAF // LANES), axis=1)

    def near_kernel(rows, mult_ref, emb_ref, x_ref, hn_ref, *rest):
        near_ref = rest[-1]
        acc = [None] * leaves

        def add(j, value):
            acc[j] = value if acc[j] is None else acc[j] + value

        def make(i):
            w = min(W + 1, leaves - i)
            si, sp = slice(i * LEAF, (i + 1) * LEAF), slice(i * LEAF, (i + w) * LEAF)
            g = dot(jnp.transpose(emb_ref[:, si]), emb_ref[:, sp])
            return jnp.exp(g - (col_of(hn_ref[:, si]) + hn_ref[:, sp])).astype(BF16)

        def use(i, k):
            y = dot(x_ref[:, i * LEAF : (i + 1) * LEAF], k)
            for q in range(k.shape[1] // LEAF):
                j = i + q
                sq = slice(q * LEAF, (q + 1) * LEAF)
                add(j, times(mult_ref, j, W - q, y[:, sq]))
                if q:
                    sj = slice(j * LEAF, (j + 1) * LEAF)
                    add(i, times(mult_ref, i, W + q, dot_nt(x_ref[:, sj], k[:, sq])))

        held = None
        for i in rows:
            k = make(i)
            if held is not None:
                use(*held)
            held = (i, k)
        use(*held)
        for j in range(leaves):
            sj = slice(j * LEAF, (j + 1) * LEAF)
            if len(rest) > 1:
                add(j, rest[0][:, sj])
            near_ref[:, sj] = jnp.zeros((cols, LEAF), F32) if acc[j] is None else acc[j]

    def near_part(rows, emb, x_tree, hn, *near):
        return call(
            lambda *refs: near_kernel(rows, *refs),
            jax.ShapeDtypeStruct((cols, points), F32),
            mult,
            emb,
            x_tree,
            hn,
            *near,
            flops=60 * 2 * 256**3,
            nbytes=6 << 20,
            name="near%d" % rows[0],
        )

    def low_edge(mult_ref, emb_ref, hn_ref, src_ref, near_in, near_ref):
        acc = [jnp.zeros((cols, LEAF), F32)] * W
        for q in range(W):
            sq, sp = slice(q * LEAF, (q + 1) * LEAF), slice(0, (q + 1) * LEAF)
            es = src_ref[0:width, sq]
            g = dot(jnp.transpose(es), emb_ref[:, sp])
            k = jnp.exp(g - (col_of(half_norm_row(es)) + hn_ref[:, sp])).astype(BF16)
            y = dot(src_ref[width:, sq], k)
            for t in range(q + 1):
                acc[t] = acc[t] + times(mult_ref, t, q - t, y[:, t * LEAF : (t + 1) * LEAF])
        near_ref[:, 0:halo] = near_in[:, 0:halo] + jnp.concatenate(acc, axis=1)
        near_ref[:, halo:] = near_in[:, halo:]

    def high_edge(mult_ref, emb_ref, hn_ref, src_ref, near_in, near_ref):
        acc = [jnp.zeros((cols, LEAF), F32)] * W
        for q in range(W):
            sq, sp = slice(q * LEAF, (q + 1) * LEAF), slice((leaves - W + q) * LEAF, points)
            es = src_ref[0:width, sq]
            g = dot(jnp.transpose(es), emb_ref[:, sp])
            k = jnp.exp(g - (col_of(half_norm_row(es)) + hn_ref[:, sp])).astype(BF16)
            y = dot(src_ref[width:, sq], k)
            for i in range(W - q):
                t = leaves - W + q + i
                acc[q + i] = acc[q + i] + (
                    times(mult_ref, t, leaves + q - t + W, y[:, i * LEAF : (i + 1) * LEAF])
                )
        near_ref[:, 0:last] = near_in[:, 0:last]
        near_ref[:, last:] = near_in[:, last:] + jnp.concatenate(acc, axis=1)

    def core_kernel(mult_ref, emb_ref, hn_ref, src_ref, near_in, near_ref):
        odd = jnp.bitwise_and(lax.axis_index("leaf"), 1)
        for code, edge in ((1, low_edge), (0, high_edge)):

            @pl.when(odd == code)
            def _():
                edge(mult_ref, emb_ref, hn_ref, src_ref, near_in, near_ref)

    def core_part(emb, hn, recv_a, near):
        return call(
            core_kernel,
            jax.ShapeDtypeStruct((cols, points), F32),
            mult,
            emb,
            hn,
            recv_a,
            near,
            flops=30 * 2 * 256**3,
            nbytes=3 << 20,
            name="edge_core",
        )

    def kernel_of(es, emb_ref, hn_ref, sp):
        g = dot(jnp.transpose(es), emb_ref[:, sp])
        return jnp.exp(g - (col_of(half_norm_row(es)) + hn_ref[:, sp])).astype(BF16)

    def told(src_ref, row, value):
        at = width + cols + row
        count = src_ref[at : at + 1, 0:LANES].astype(F32)
        return value * jnp.concatenate([count] * (LEAF // LANES), axis=1)

    def leaf(q):
        return slice(q * LEAF, (q + 1) * LEAF)

    def upper(mult_ref, emb_ref, hn_ref, x_ref, src_ref, near_ref, back_ref):
        k3 = kernel_of(src_ref[0:width, leaf(1)], emb_ref, hn_ref, slice(LEAF, 3 * LEAF))
        k2 = kernel_of(src_ref[0:width, leaf(0)], emb_ref, hn_ref, leaf(1))
        y3 = dot(src_ref[width : width + cols, leaf(1)], k3)
        y2 = dot(src_ref[width : width + cols, leaf(0)], k2)
        near_ref[:, leaf(1)] += times(mult_ref, 1, 1, y3[:, leaf(0)]) + times(mult_ref, 1, 0, y2)
        near_ref[:, leaf(2)] += times(mult_ref, 2, 0, y3[:, leaf(1)])
        back_ref[:, leaf(0)] = told(src_ref, 2, dot_nt(x_ref[:, leaf(1)], k2))
        back_ref[:, leaf(1)] = told(src_ref, 0, dot_nt(x_ref[:, leaf(1)], k3[:, leaf(0)])) + told(
            src_ref, 1, dot_nt(x_ref[:, leaf(2)], k3[:, leaf(1)])
        )

    def lower(mult_ref, emb_ref, hn_ref, x_ref, src_ref, near_ref, back_ref):
        k = kernel_of(src_ref[0:width, leaf(0)], emb_ref, hn_ref, slice(last, points))
        y = dot(src_ref[width : width + cols, leaf(0)], k)
        back = jnp.zeros((cols, LEAF), F32)
        for q in range(W):
            t = leaves - W + q
            near_ref[:, leaf(t)] += times(mult_ref, t, 2 * W - q, y[:, leaf(q)])
            back = back + told(src_ref, W - 1 - q, dot_nt(x_ref[:, leaf(t)], k[:, leaf(q)]))
        back_ref[:, leaf(0)] = back
        back_ref[:, leaf(1)] = jnp.zeros((cols, LEAF), F32)

    def chip_kernel(mult_ref, emb_ref, hn_ref, x_ref, one_ref, two_ref, near_in, near_ref, back_ref):
        near_ref[...] = near_in[...]
        turn = jnp.bitwise_and(lax.axis_index("leaf"), 3)
        for code, side, src_ref in (
            (1, lower, one_ref),
            (2, upper, one_ref),
            (3, lower, two_ref),
            (0, upper, two_ref),
        ):

            @pl.when(turn == code)
            def _():
                side(mult_ref, emb_ref, hn_ref, x_ref, src_ref, near_ref, back_ref)

    def chip_part(emb, recv_b1, recv_b2, near):
        return call(
            chip_kernel,
            [
                jax.ShapeDtypeStruct((cols, points), F32),
                jax.ShapeDtypeStruct((cols, UP * LEAF), F32),
            ],
            mult,
            emb,
            hn,
            x_tree,
            recv_b1,
            recv_b2,
            near,
            name="edge_chip",
        )

    table = []
    for lev, off, row in sorted(plan.entries, key=lambda e: e[2]):
        for i in range(plan.padded[lev]):
            side = (off >> plan.shift[lev]) & 1
            table.append(
                (
                    off,
                    (side * LEVELS + lev) * R + i,
                    (1 << plan.shift[lev]) - 1,
                    plan.slots[lev],
                    i < plan.slots[lev],
                )
            )
    table = jnp.array(table, jnp.int32).T
    own_w = LEVELS * R
    dest = table[1] + jnp.bitwise_and(pos ^ table[0], table[2]) * table[3]
    dest = jnp.where(table[4] == 1, dest, -1)[None, :]

    def join_kernel(*refs):
        row = 0
        for ref in refs[:-1]:
            refs[-1][row : row + ref.shape[0], :] = ref[...]
            row += ref.shape[0]

    def join(*blocks):
        rows = sum(v.shape[0] for v in blocks)
        return call(
            join_kernel, jax.ShapeDtypeStruct((rows, width), BF16), *blocks, nbytes=1 << 18, name="join"
        )

    after = lax.optimization_barrier
    block = owned[0]
    for bit in reversed(range(plan.bits)):
        level = plan.bits - bit
        stage = level - 1
        partner = lax.ppermute(block, "leaf", [(i, i ^ (1 << bit)) for i in range(n)])
        if stage == 0:
            partner, x_tree, dest = after((partner, x_tree, dest))
        if stage == 1:
            near = near_part((0, 1), emb, x_tree, hn)
            send_a = cut_core(emb, x_tree)
            partner, near, send_a = after((partner, near, send_a))
        if stage == 2:
            recv_a = lax.ppermute(send_a, "leaf", pairs_a)
            near = near_part((2, 3), emb, x_tree, hn, near)
            partner, near = after((partner, near))
        if stage == 3:
            near = near_part(tuple(range(4, leaves)), emb, x_tree, hn, near)
            emb, near = after((emb, near))
            recv_b2 = lax.ppermute(cut_chip(emb, x_tree), "leaf", pairs(3))
            near = core_part(emb, hn, recv_a, near)
            partner, near = after((partner, near))
        if bit:
            block = join(block, partner, *([owned[level]] if level < LEVELS else []))
            block, x_tree, emb = after((block, x_tree, emb))
    half = plan.size // 2

    def sorted_rows(first, dest_ref, *refs):
        at = lax.broadcasted_iota(jnp.int32, (own_w, half), 0)
        total = None
        for i, ref in enumerate(refs):
            d = dest_ref[:, i * half : (i + 1) * half] - first
            term = dot(jnp.where(at == d, 1.0, 0.0).astype(BF16), ref[...])
            total = term if total is None else total + term
        return total.astype(BF16)

    def own_kernel(block_ref, other_ref, dest_ref, emb_ref, x_ref, hn_ref, z_ref):
        sk = sorted_rows(0, dest_ref, block_ref, other_ref)
        hs = half_norm_col(sk)
        z = jnp.zeros((cols, own_w), F32)
        held = None
        for c in range(0, leaves, 2):
            sl = slice(c * LEAF, (c + 2) * LEAF)
            k = jnp.exp(dot(sk, emb_ref[:, sl]) - (hs + hn_ref[:, sl])).astype(BF16)
            if held is not None:
                z = z + dot_nt(x_ref[:, held[0]], held[1])
            held = (sl, k)
        z_ref[...] = z + dot_nt(x_ref[:, held[0]], held[1])

    z = call(
        own_kernel,
        jax.ShapeDtypeStruct((cols, own_w), F32),
        block,
        partner,
        dest,
        emb,
        x_tree,
        hn,
        flops=50 * 2 * 256**3,
        nbytes=4 << 20,
        name="own",
    )

    def far_kernel(block_ref, other_ref, dest_ref, emb_ref, hn_ref, out_ref):
        sk = sorted_rows(own_w, dest_ref, block_ref, other_ref)
        hs = half_norm_col(sk)
        for c in range(0, leaves, 2):
            sl = slice(c * LEAF, (c + 2) * LEAF)
            g = dot(sk, emb_ref[:, sl])
            out_ref[:, sl] = jnp.exp(g - (hs + hn_ref[:, sl])).astype(BF16)

    def far_part(block, partner, emb, hn):
        return call(
            far_kernel,
            jax.ShapeDtypeStruct((own_w, points), BF16),
            block,
            partner,
            dest,
            emb,
            hn,
            flops=30 * 2 * 256**3,
            nbytes=4 << 20,
            name="far",
        )

    level_of = lax.broadcasted_iota(jnp.int32, (1, own_w), 1) // R
    for stage, bit in enumerate([0] + list(range(3, plan.bits)) + [2, 1]):
        heard = lax.ppermute(z, "leaf", [(i, i ^ (1 << bit)) for i in range(n)])
        if stage == 0:
            far_k = far_part(block, partner, emb, hn)
            heard, far_k, recv_b2 = after((heard, far_k, recv_b2))
        if stage == 0:
            recv_b1 = lax.ppermute(cut_chip(emb, x_tree), "leaf", pairs(1))
        if stage == 3:
            near, back = chip_part(emb, recv_b1, recv_b2, near)
            heard, near, back = after((heard, near, back))
        if stage == 4:
            back = lax.ppermute(back, "leaf", pairs(1, 3))
        swap = level_of == plan.bits - 1 - bit
        add = level_of < plan.bits - 1 - bit
        z = jnp.where(add, z + heard, jnp.where(swap, heard, z))
        z, emb = after((z, emb))

    def last_kernel(z_ref, core_ref, far_ref, back_ref, inv_ref, near_ref, out_ref):
        me = lax.axis_index("leaf")
        weights = []
        for l in range(LEVELS):
            node = 2 ** (l + 1) - 2 + (jnp.right_shift(me, plan.shift[l]) ^ 1)
            weights.append(
                jnp.dot(
                    z_ref[:, l * R : (l + 1) * R],
                    core_ref[node],
                    precision=lax.Precision.HIGHEST,
                    preferred_element_type=F32,
                ).astype(BF16)
            )
        w = jnp.concatenate(weights, axis=1)
        tree = near_ref[...] + dot(w, far_ref[...])
        even = jnp.bitwise_and(me, 1) == 0
        low_back = jnp.where(even, back_ref[:, 0:LEAF], 0.0)
        high_back = jnp.where(even, 0.0, back_ref[...])
        tree = tree + jnp.concatenate(
            [low_back, jnp.zeros((cols, points - (1 + UP) * LEAF), F32), high_back], axis=1
        )
        top = tree.astype(BF16)
        rest = (tree - top.astype(F32)).astype(BF16)
        stack = jnp.concatenate(
            [
                jnp.concatenate([v[:, h * LANES : (h + 1) * LANES] for v in (top, rest)], axis=1)
                for h in range(groups)
            ],
            axis=0,
        )
        low = jnp.bitwise_and(inv_ref[...], LANES - 1)
        high = jnp.right_shift(inv_ref[...], LANES.bit_length() - 1)
        hot = jnp.where(
            lax.broadcasted_iota(jnp.int32, (LANES, points), 0) == low, 1.0, 0.0
        ).astype(BF16)
        for c in range(leaves):
            sl = slice(c * LEAF, (c + 1) * LEAF)
            y = dot(stack, jnp.concatenate([hot[:, sl]] * 2, axis=0))
            out = jnp.zeros((cols, LEAF), F32)
            for h in range(groups):
                out = out + jnp.where(high[:, sl] == h, y[h * cols : (h + 1) * cols], 0.0)
            out_ref[:, sl] = out

    return call(
        last_kernel,
        jax.ShapeDtypeStruct((cols, points), F32),
        z,
        core,
        far_k,
        back,
        inv,
        near,
        flops=30 * 2 * 256**3,
        nbytes=2 << 20,
        name="last",
    )


def solution(mesh):
    return jax.shard_map(
        body,
        mesh=mesh,
        in_specs=(
            P(None, ("groups", "leaf")),
            P(None, ("groups", "leaf")),
            P(("groups", "leaf"), None),
            P(("groups", "leaf"), None),
            P(("groups", "leaf"), None),
            P("groups", None),
            P("groups", None, None),
        ),
        out_specs=P(None, ("groups", "leaf")),
        check_vma=False,
    )
```

time: 65.1 us -> 60.3 us (0.926); the launches traced: 63.9 us -> 60.1 us
  waiting for transfers between devices: 16.4 us -> 30.6 us
  starting transfers between devices: 24 us -> 11.4 us
  local copies, waits for them, and re-layouts: 3.03 us -> 0.03 us
  Pallas kernels: 19.2 us -> 17.7 us
  other arithmetic: 0.97 us -> 0.09 us
    ppermute x5 -> x3, starting transfers between devices: 15.9 us -> 5.13 us  [the longest x1 2.31 us: body(): recv_b2 = lax.ppermute(cut_chip(emb, x_tree), 'leaf', pairs(3))]
    ppermute x5, waiting for transfers between devices: 3.55 us -> 11.9 us  [body(): heard = lax.ppermute(z, 'leaf', [(i, i ^ 1 << bit) for i in range(n)])]
    ppermute x5, starting transfers between devices: 6.87 us -> 2.3 us  [body(): heard = lax.ppermute(z, 'leaf', [(i, i ^ 1 << bit) for i in range(n)])]
    ppermute x5 -> x3, waiting for transfers between devices: 4.4 us -> 8.17 us  [the longest x1 4.62 us: body(): recv_b2 = lax.ppermute(cut_chip(emb, x_tree), 'leaf', pairs(3))]
    unnamed x25 -> x14, local copies, waits for them, and re-layouts: 3.03 us -> 0.03 us
    ppermute x5, starting transfers between devices: 1.18 us -> 4 us  [body(): partner = lax.ppermute(block, 'leaf', [(i, i ^ 1 << bit) for i in range(n)])]
    ppermute x5, waiting for transfers between devices: 8.47 us -> 10.5 us  [body(): partner = lax.ppermute(block, 'leaf', [(i, i ^ 1 << bit) for i in range(n)])]
    pallas_call x15 -> x16, Pallas kernels: 19.2 us -> 17.7 us  [call(): pl.pallas_call(kernel, out_shape=outs, in_specs=[sm if i in smem else hb...]
  transfers between devices with their start and end apart: 16 -> 14, of which waited for: 11 -> 11; matrix products, arithmetic and copies ran while one was open for 0% -> 0% of each run, Pallas kernels for 22% -> 19%
where the time goes in v3:
time: 60.3 us; the launch traced here: 60.1 us
  waiting for transfers between devices  30.6 us (51%)
  Pallas kernels  17.7 us (29%)
  starting transfers between devices  11.4 us (19%)
    pallas_call x16, Pallas kernels, call(): pl.pallas_call(kernel, out_shape=outs, in_specs=[sm if i in smem else hb...  17.7 us
    ppermute x5, waiting for transfers between devices, body(): heard = lax.ppermute(z, 'leaf', [(i, i ^ 1 << bit) for i in range(n)])  11.9 us
    ppermute x5, waiting for transfers between devices, body(): partner = lax.ppermute(block, 'leaf', [(i, i ^ 1 << bit) for i in range(n)])  10.5 us
    ppermute x1, waiting for transfers between devices, body(): recv_b2 = lax.ppermute(cut_chip(emb, x_tree), 'leaf', pairs(3))  4.62 us
    ppermute x5, starting transfers between devices, body(): partner = lax.ppermute(block, 'leaf', [(i, i ^ 1 << bit) for i in range(n)])  4 us
    ppermute x1, waiting for transfers between devices, body(): back = lax.ppermute(back, 'leaf', pairs(1, 3))  3.55 us
    ppermute x1, starting transfers between devices, body(): recv_b2 = lax.ppermute(cut_chip(emb, x_tree), 'leaf', pairs(3))  2.31 us
    ppermute x5, starting transfers between devices, body(): heard = lax.ppermute(z, 'leaf', [(i, i ^ 1 << bit) for i in range(n)])  2.3 us
  transfers between devices with their start and end apart: 14, of which 11 were waited for; matrix products, arithmetic and copies ran while one was open for 0% of the time, Pallas kernels for 19%

profile of v3, /device:TPU:24, one launch (start us, length us, event | category | flops | bytes accessed | tf_op | source)
XLA Modules:
  0.0 60.1 jit_solution(214064674308655162)
XLA Ops:
  0.0 0.0 copy-start.5
  0.0 0.0 copy-start.6
  0.0 0.0 copy-start
  0.0 4.3 %prep.1 = (bf16[8,768]{1,0:T(8,128)(2,1)S(1)}, bf16[8,768]{1,0:T(8,128)(2,1)S(1)}, bf16[16,768]{1,0:T(8,128)(2,1)S(1)}, bf16[32,768]{1,0:T(8,128)(2,1)S(1)}, bf1...) custom-call(s32[30,64]{1,0:T(8,128)} %skel_hbm.1, ...), custom_call_target="tpu_custom_call" | custom-call | tf_op jit(solution)/shard_map/prep/pallas_call | solution.py:51
  4.3 0.4 collective-permute-start
  4.7 0.0 copy-done.2
  4.7 0.0 copy-done.3
  4.7 0.0 copy-done.4
  4.7 0.0 copy-done.5
  4.7 0.0 copy-done.6
  4.8 4.2 %collective-permute-done.refs_1_ = bf16[8,768]{1,0:T(8,128)(2,1)S(1)} collective-permute-done((bf16[8,768]{1,0:T(8,128)(2,1)S(1)}, bf16[8,768]{1,0:T(8,128)(2,1)S(1)}, u32[]{:S(2)}, u32[]{:S(2)}) %collective-permute-start) | collective-permute-done | bytes 12320 | tf_op jit(solution)/shard_map/ppermute | solution.py:501
  9.0 0.4 collective-permute-start.1
  9.4 0.2 cut.1
  9.6 1.4 %near0.1.refs_4_ = f32[32,2048]{1,0:T(8,128)S(1)} custom-call(f32[56,128]{1,0:T(8,128)S(1)} %get-tuple-element.62.refs_0_.mult_ref, bf16[768,2048]{1,0:T(8,128)(2,1)S(1)} %copy-done, bf16[32,2048]{1,0:T(8,128)(2,1)S(1)} %get-tuple-element.85.refs_2_.x_ref, f32[1,2048]{1,0:T(1,128)S(1)} %get-tuple-element.65.refs_3_.hn_ref), custom_call_target="tpu_custom_call" | custom-call | tf_op jit(solution)/shard_map/near0/pallas_call | solution.py:51
  11.1 1.9 %collective-permute-done.1.refs_1_ = bf16[24,768]{1,0:T(8,128)(2,1)S(1)} collective-permute-done((bf16[24,768]{1,0:T(8,128)(2,1)S(1)}, bf16[24,768]{1,0:T(8,128)(2,1)S(1)}, u32[]{:S(2)}, u32[]{:S(2)}) %collective-permute-start.1) | collective-permute-done | bytes 36896 | tf_op jit(solution)/shard_map/ppermute | solution.py:501
  13.0 0.0 collective-permute-start.4
  13.0 1.6 %collective-permute-start.2 = (bf16[64,768]{1,0:T(8,128)(2,1)S(1)}, bf16[64,768]{1,0:T(8,128)(2,1)S(1)}, u32[]{:S(2)}, u32[]{:S(2)}) collective-permute-start(bf16[64,768]{1,0:T(8,128)(2,1)S(1)} %join.5.refs_0_), channel_id=1, source_target_pairs={{0,4},{1,5},{2,6},{3,7},{4,0},{5,1},{6,2},{7,3},{8,12},{9,13},{10,... | collective-permute-start | bytes 294920 | tf_op jit(solution)/shard_map/ppermute | solution.py:501
  14.6 1.4 %near2.1.refs_4_ = f32[32,2048]{1,0:T(8,128)S(1)} custom-call(f32[56,128]{1,0:T(8,128)S(1)} %get-tuple-element.62.refs_0_.mult_ref, bf16[768,2048]{1,0:T(8,128)(2,1)S(1)} %copy-done, bf16[32,2048]{1,0:T(8,128)(2,1)S(1)} %get-tuple-element.85.refs_2_.x_ref, f32[1,2048]{1,0:T(1,128)S(1)} %get-tuple-element.65.refs_3_.hn_ref, f32[32,2048]{1,0:T(8,128)S(1)} %near0.1.refs_4_), custom_call_target="tpu_custom_call" | custom-call | tf_op jit(solution)/shard_map/near2/pallas_call | solution.py:51
  16.0 2.3 %collective-permute-done.2.refs_1_ = bf16[64,768]{1,0:T(8,128)(2,1)S(1)} collective-permute-done((bf16[64,768]{1,0:T(8,128)(2,1)S(1)}, bf16[64,768]{1,0:T(8,128)(2,1)S(1)}, u32[]{:S(2)}, u32[]{:S(2)}) %collective-permute-start.2) | collective-permute-done | bytes 98336 | tf_op jit(solution)/shard_map/ppermute | solution.py:501
  18.3 1.5 %collective-permute-start.3 = (bf16[160,768]{1,0:T(8,128)(2,1)S(1)}, bf16[160,768]{1,0:T(8,128)(2,1)S(1)}, u32[]{:S(2)}, u32[]{:S(2)}) collective-permute-start(bf16[160,768]{1,0:T(8,128)(2,1)S(1)} %join.6.refs_0_), channel_id=1, source_target_pairs={{0,2},{1,3},{2,0},{3,1},{4,6},{5,7},{6,4},{7,5},{8,10},{9,11},{10,... | collective-permute-start | bytes 737288 | tf_op jit(solution)/shard_map/ppermute | solution.py:501
  19.8 1.8 %near4.1.near_in = f32[32,2048]{1,0:T(8,128)S(1)} custom-call(f32[56,128]{1,0:T(8,128)S(1)} %get-tuple-element.62.refs_0_.mult_ref, bf16[768,2048]{1,0:T(8,128)(2,1)S(1)} %copy-done, bf16[32,2048]{1,0:T(8,128)(2,1)S(1)} %get-tuple-element.85.refs_2_.x_ref, f32[1,2048]{1,0:T(1,128)S(1)} %get-tuple-element.65.refs_3_.hn_ref, f32[32,2048]{1,0:T(8,128)S(1)} %near2.1.refs_4_), custom_call_target="tpu_custom_call" | custom-call | tf_op jit(solution)/shard_map/near4/pallas_call | solution.py:51
  21.6 0.1 cut_chip.2
  21.7 2.3 %collective-permute-start.7 = (bf16[816,512]{1,0:T(8,128)(2,1)S(1)}, bf16[816,512]{1,0:T(8,128)(2,1)S(1)}, u32[]{:S(2)}, u32[]{:S(2)}) collective-permute-start(bf16[816,512]{1,0:T(8,128)(2,1)S(1)} %cut_chip.2), channel_id=1, source_target_pairs={{3,4},{7,8},{11,12},{15,16},{19,20},{23,24},{27,28},{4,3},{8,7},{1... | collective-permute-start | bytes 2506760 | tf_op jit(solution)/shard_map/ppermute | solution.py:515
  24.0 0.0 collective-permute-done.4.src_ref
  24.0 1.6 %edge_core.1.near_in = f32[32,2048]{1,0:T(8,128)S(1)} custom-call(f32[56,128]{1,0:T(8,128)S(1)} %get-tuple-element.62.refs_0_.mult_ref, bf16[768,2048]{1,0:T(8,128)(2,1)S(1)} %copy-done, f32[1,2048]{1,0:T(1,128)S(1)} %get-tuple-element.65.refs_3_.hn_ref, bf16[800,768]{1,0:T(8,128)(2,1)S(1)} %collective-permute-done.4.src_ref, f32[32,2048]{1,0:T(8,128)S(1)} %near4.1.near_in), custom_call_target="tpu_custom_call" | custom-call | tf_op jit(solution)/shard_map/edge_core/pallas_call | solution.py:51
  25.7 0.2 collective-permute-done.3.refs_1_
  26.0 0.1 collective-permute-start.5
  26.0 1.9 %collective-permute-done.5.other_ref = bf16[320,768]{1,0:T(8,128)(2,1)S(1)} collective-permute-done((bf16[320,768]{1,0:T(8,128)(2,1)S(1)}, bf16[320,768]{1,0:T(8,128)(2,1)S(1)}, u32[]{:S(2)}, u32[]{:S(2)}) %collective-permute-start.5) | collective-permute-done | bytes 491552 | tf_op jit(solution)/shard_map/ppermute | solution.py:501
  27.9 2.0 %own.1 = f32[32,256]{1,0:T(8,128)S(1)} custom-call(bf16[320,768]{1,0:T(8,128)(2,1)S(1)} %join.7.block_ref, bf16[320,768]{1,0:T(8,128)(2,1)S(1)} %collective-permute-done.5.other_ref, s32[1,640]{1,0:T(1,128)S(1)} %add_select_fusion.dest_ref, bf16[768,2048]{1,0:T(8,128)(2,1)S(1)} %copy-done, bf16[32,2048]{1,0:T(8,128)(2,1)S(1)} %get-tuple-element.85.refs_2_.x_ref, ...), custom_call_target="tpu_custom_call" | custom-call | tf_op jit(solution)/shard_map/own/pallas_call | solution.py:51
  29.8 0.2 collective-permute-start.6
  30.0 0.1 cut_chip.3
  30.2 0.9 %collective-permute-start.11 = (bf16[816,512]{1,0:T(8,128)(2,1)S(1)}, bf16[816,512]{1,0:T(8,128)(2,1)S(1)}, u32[]{:S(2)}, u32[]{:S(2)}) collective-permute-start(bf16[816,512]{1,0:T(8,128)(2,1)S(1)} %cut_chip.3), channel_id=1, source_target_pairs={{1,2},{5,6},{9,10},{13,14},{17,18},{21,22},{25,26},{29,30},{2,1},{... | collective-permute-start | bytes 2506760 | tf_op jit(solution)/shard_map/ppermute | solution.py:588
  31.1 1.8 %far.1.far_ref = bf16[256,2048]{1,0:T(8,128)(2,1)S(1)} custom-call(bf16[320,768]{1,0:T(8,128)(2,1)S(1)} %join.7.block_ref, bf16[320,768]{1,0:T(8,128)(2,1)S(1)} %collective-permute-done.5.other_ref, s32[1,640]{1,0:T(1,128)S(1)} %add_select_fusion.dest_ref, bf16[768,2048]{1,0:T(8,128)(2,1)S(1)} %copy-done, f32[1,2048]{1,0:T(1,128)S(1)} %get-tuple-element.65.refs_3_.hn_ref), custom_call_target="tpu_custom_call" | custom-call | tf_op jit(solution)/shard_map/far/pallas_call | solution.py:51
  32.8 4.6 %collective-permute-done.7.two_ref = bf16[816,512]{1,0:T(8,128)(2,1)S(1)} collective-permute-done((bf16[816,512]{1,0:T(8,128)(2,1)S(1)}, bf16[816,512]{1,0:T(8,128)(2,1)S(1)}, u32[]{:S(2)}, u32[]{:S(2)}) %collective-permute-start.7) | collective-permute-done | bytes 835616 | tf_op jit(solution)/shard_map/ppermute | solution.py:515
  37.4 0.0 collective-permute-done.6
  37.5 0.5 collective-permute-start.8
  37.9 3.5 %collective-permute-done.8 = f32[32,256]{1,0:T(8,128)S(1)} collective-permute-done((f32[32,256]{1,0:T(8,128)S(1)}, f32[32,256]{1,0:T(8,128)S(1)}, u32[]{:S(2)}, u32[]{:S(2)}) %collective-permute-start.8) | collective-permute-done | bytes 32800 | tf_op jit(solution)/shard_map/ppermute | solution.py:583
  41.4 0.4 collective-permute-start.9
  41.8 4.7 %collective-permute-done.9 = f32[32,256]{1,0:T(8,128)S(1)} collective-permute-done((f32[32,256]{1,0:T(8,128)S(1)}, f32[32,256]{1,0:T(8,128)S(1)}, u32[]{:S(2)}, u32[]{:S(2)}) %collective-permute-start.9) | collective-permute-done | bytes 32800 | tf_op jit(solution)/shard_map/ppermute | solution.py:583
  46.5 1.2 %collective-permute-start.10 = (f32[32,256]{1,0:T(8,128)S(1)}, f32[32,256]{1,0:T(8,128)S(1)}, u32[]{:S(2)}, u32[]{:S(2)}) collective-permute-start(f32[32,256]{1,0:T(8,128)S(1)} %select_select_fusion.2), channel_id=1, source_target_pairs={{0,4},{1,5},{2,6},{3,7},{4,0},{5,1},{6,2},{7,3},{8,12},{9,13},{10,... | collective-permute-start | bytes 98312 | tf_op jit(solution)/shard_map/ppermute | solution.py:583
  47.8 0.0 collective-permute-done.11.one_ref
  47.8 1.0 %edge_chip.1 = (f32[32,2048]{1,0:T(8,128)S(1)}, f32[32,512]{1,0:T(8,128)S(1)}) custom-call(f32[56,128]{1,0:T(8,128)S(1)} %get-tuple-element.62.refs_0_.mult_ref, bf16[768,2048]{1,0:T(8,128)(2,1)S(1)} %copy-done, f32[1,2048]{1,0:T(1,128)S(1)} %get-tuple-element.65.refs_3_.hn_ref, bf16[32,2048]{1,0:T(8,128)(2,1)S(1)} %get-tuple-element.85.refs_2_.x_ref, ...), custom_call_target="tpu_custom_call" | custom-call | tf_op jit(solution)/shard_map/edge_chip/pallas_call | solution.py:51
  48.7 1.8 %collective-permute-done.10 = f32[32,256]{1,0:T(8,128)S(1)} collective-permute-done((f32[32,256]{1,0:T(8,128)S(1)}, f32[32,256]{1,0:T(8,128)S(1)}, u32[]{:S(2)}, u32[]{:S(2)}) %collective-permute-start.10) | collective-permute-done | bytes 32800 | tf_op jit(solution)/shard_map/ppermute | solution.py:583
  50.5 0.1 collective-permute-start.12
  50.6 1.9 %collective-permute-start.13 = (f32[32,512]{1,0:T(8,128)S(1)}, f32[32,512]{1,0:T(8,128)S(1)}, u32[]{:S(2)}, u32[]{:S(2)}) collective-permute-start(f32[32,512]{1,0:T(8,128)S(1)} %get-tuple-element.100), channel_id=1, source_target_pairs={{1,2},{5,6},{9,10},{13,14},{17,18},{21,22},{25,26},{29,30},{3,4},{... | collective-permute-start | bytes 196616 | tf_op jit(solution)/shard_map/ppermute | solution.py:593
  52.5 2.0 %collective-permute-done.12 = f32[32,256]{1,0:T(8,128)S(1)} collective-permute-done((f32[32,256]{1,0:T(8,128)S(1)}, f32[32,256]{1,0:T(8,128)S(1)}, u32[]{:S(2)}, u32[]{:S(2)}) %collective-permute-start.12) | collective-permute-done | bytes 32800 | tf_op jit(solution)/shard_map/ppermute | solution.py:583
  54.5 3.6 %collective-permute-done.13.back_ref = f32[32,512]{1,0:T(8,128)S(1)} collective-permute-done((f32[32,512]{1,0:T(8,128)S(1)}, f32[32,512]{1,0:T(8,128)S(1)}, u32[]{:S(2)}, u32[]{:S(2)}) %collective-permute-start.13) | collective-permute-done | bytes 65568 | tf_op jit(solution)/shard_map/ppermute | solution.py:593
  58.1 2.0 %last.1 = f32[32,2048]{1,0:T(8,128)} custom-call(f32[32,256]{1,0:T(8,128)S(1)} %select_select_fusion.z_ref, f32[30,64,64]{2,1,0:T(8,128)S(1)} %copy-done.1, bf16[256,2048]{1,0:T(8,128)(2,1)S(1)} %far.1.far_ref, f32[32,512]{1,0:T(8,128)S(1)} %collective-permute-done.13.back_ref, s32[1,2048]{1,0:T(1,128)S(1)} %get-tuple-element.101.inv_ref, ...), custom_call_target="tpu_custom_call" | custom-call | tf_op jit(solution)/shard_map/last/pallas_call | solution.py:51
  (21 shorter events, 0.2 us)
Async XLA Ops:
  0.0 4.7 %copy-start.2 = (pred[1,640]{1,0:T(4,128)(4,1)S(1)}, pred[1,640]{1,0:T(4,128)(4,1)}, u32[]{:S(2)}) copy-start(pred[1,640]{1,0:T(4,128)(4,1)} %constant.58) | copy-start | bytes 1924
  0.0 4.7 %copy-start.3 = (s32[1,640]{1,0:T(1,128)S(1)}, s32[1,640]{1,0:T(1,128)}, u32[]{:S(2)}) copy-start(s32[1,640]{1,0:T(1,128)} %constant.59) | copy-start | bytes 7684
  0.0 4.7 %copy-start.4 = (s32[1,640]{1,0:T(1,128)S(1)}, s32[1,640]{1,0:T(1,128)}, u32[]{:S(2)}) copy-start(s32[1,640]{1,0:T(1,128)} %constant.62) | copy-start | bytes 7684
  0.0 4.7 %copy-start.5 = (s32[1,640]{1,0:T(1,128)S(1)}, s32[1,640]{1,0:T(1,128)}, u32[]{:S(2)}) copy-start(s32[1,640]{1,0:T(1,128)} %constant.61) | copy-start | bytes 7684
  0.0 4.7 %copy-start.6 = (s32[1,640]{1,0:T(1,128)S(1)}, s32[1,640]{1,0:T(1,128)}, u32[]{:S(2)}) copy-start(s32[1,640]{1,0:T(1,128)} %constant.60) | copy-start | bytes 7684
  0.0 9.4 %copy-start = (bf16[768,2048]{1,0:T(8,128)(2,1)S(1)}, bf16[768,2048]{1,0:T(8,128)(2,1)}, u32[]{:S(2)}) copy-start(bf16[768,2048]{1,0:T(8,128)(2,1)} %emb_ref.6) | copy-start | bytes 9437188
  4.3 4.7 %collective-permute-start = (bf16[8,768]{1,0:T(8,128)(2,1)S(1)}, bf16[8,768]{1,0:T(8,128)(2,1)S(1)}, u32[]{:S(2)}, u32[]{:S(2)}) collective-permute-start(bf16[8,768]{1,0:T(8,128)(2,1)S(1)} %get-tuple-element.54.refs_0_), channel_id=1, source_target_pairs={{0,16},{1,17},{2,18},{3,19},{4,20},{5,21},{6,22},{7,23},{8,24},{9,... | collective-permute-start | bytes 36872 | tf_op jit(solution)/shard_map/ppermute | solution.py:501
  9.0 4.0 %collective-permute-start.1 = (bf16[24,768]{1,0:T(8,128)(2,1)S(1)}, bf16[24,768]{1,0:T(8,128)(2,1)S(1)}, u32[]{:S(2)}, u32[]{:S(2)}) collective-permute-start(bf16[24,768]{1,0:T(8,128)(2,1)S(1)} %join.4.refs_0_), channel_id=1, source_target_pairs={{0,8},{1,9},{2,10},{3,11},{4,12},{5,13},{6,14},{7,15},{8,0},{9,1},... | collective-permute-start | bytes 110600 | tf_op jit(solution)/shard_map/ppermute | solution.py:501
  13.0 11.1 %collective-permute-start.4 = (bf16[800,768]{1,0:T(8,128)(2,1)S(1)}, bf16[800,768]{1,0:T(8,128)(2,1)S(1)}, u32[]{:S(2)}, u32[]{:S(2)}) collective-permute-start(bf16[800,768]{1,0:T(8,128)(2,1)S(1)} %cut.1), channel_id=1, source_target_pairs={{0,1},{1,0},{2,3},{3,2},{4,5},{5,4},{6,7},{7,6},{8,9},{9,8},{10,11... | collective-permute-start | bytes 3686408 | tf_op jit(solution)/shard_map/ppermute | solution.py:509
  13.0 5.3 %collective-permute-start.2 = (bf16[64,768]{1,0:T(8,128)(2,1)S(1)}, bf16[64,768]{1,0:T(8,128)(2,1)S(1)}, u32[]{:S(2)}, u32[]{:S(2)}) collective-permute-start(bf16[64,768]{1,0:T(8,128)(2,1)S(1)} %join.5.refs_0_), channel_id=1, source_target_pairs={{0,4},{1,5},{2,6},{3,7},{4,0},{5,1},{6,2},{7,3},{8,12},{9,13},{10,... | collective-permute-start | bytes 294920 | tf_op jit(solution)/shard_map/ppermute | solution.py:501
  18.3 7.6 %collective-permute-start.3 = (bf16[160,768]{1,0:T(8,128)(2,1)S(1)}, bf16[160,768]{1,0:T(8,128)(2,1)S(1)}, u32[]{:S(2)}, u32[]{:S(2)}) collective-permute-start(bf16[160,768]{1,0:T(8,128)(2,1)S(1)} %join.6.refs_0_), channel_id=1, source_target_pairs={{0,2},{1,3},{2,0},{3,1},{4,6},{5,7},{6,4},{7,5},{8,10},{9,11},{10,... | collective-permute-start | bytes 737288 | tf_op jit(solution)/shard_map/ppermute | solution.py:501
  21.7 15.7 %collective-permute-start.7 = (bf16[816,512]{1,0:T(8,128)(2,1)S(1)}, bf16[816,512]{1,0:T(8,128)(2,1)S(1)}, u32[]{:S(2)}, u32[]{:S(2)}) collective-permute-start(bf16[816,512]{1,0:T(8,128)(2,1)S(1)} %cut_chip.2), channel_id=1, source_target_pairs={{3,4},{7,8},{11,12},{15,16},{19,20},{23,24},{27,28},{4,3},{8,7},{1... | collective-permute-start | bytes 2506760 | tf_op jit(solution)/shard_map/ppermute | solution.py:515
  26.0 1.9 %collective-permute-start.5 = (bf16[320,768]{1,0:T(8,128)(2,1)S(1)}, bf16[320,768]{1,0:T(8,128)(2,1)S(1)}, u32[]{:S(2)}, u32[]{:S(2)}) collective-permute-start(bf16[320,768]{1,0:T(8,128)(2,1)S(1)} %join.7.block_ref), channel_id=1, source_target_pairs={{0,1},{1,0},{2,3},{3,2},{4,5},{5,4},{6,7},{7,6},{8,9},{9,8},{10,11... | collective-permute-start | bytes 1474568 | tf_op jit(solution)/shard_map/ppermute | solution.py:501
  29.8 7.6 %collective-permute-start.6 = (f32[32,256]{1,0:T(8,128)S(1)}, f32[32,256]{1,0:T(8,128)S(1)}, u32[]{:S(2)}, u32[]{:S(2)}) collective-permute-start(f32[32,256]{1,0:T(8,128)S(1)} %own.1), channel_id=1, source_target_pairs={{0,1},{1,0},{2,3},{3,2},{4,5},{5,4},{6,7},{7,6},{8,9},{9,8},{10,11... | collective-permute-start | bytes 98312 | tf_op jit(solution)/shard_map/ppermute | solution.py:583
  30.2 17.6 %collective-permute-start.11 = (bf16[816,512]{1,0:T(8,128)(2,1)S(1)}, bf16[816,512]{1,0:T(8,128)(2,1)S(1)}, u32[]{:S(2)}, u32[]{:S(2)}) collective-permute-start(bf16[816,512]{1,0:T(8,128)(2,1)S(1)} %cut_chip.3), channel_id=1, source_target_pairs={{1,2},{5,6},{9,10},{13,14},{17,18},{21,22},{25,26},{29,30},{2,1},{... | collective-permute-start | bytes 2506760 | tf_op jit(solution)/shard_map/ppermute | solution.py:588
  37.5 4.0 %collective-permute-start.8 = (f32[32,256]{1,0:T(8,128)S(1)}, f32[32,256]{1,0:T(8,128)S(1)}, u32[]{:S(2)}, u32[]{:S(2)}) collective-permute-start(f32[32,256]{1,0:T(8,128)S(1)} %select_select_fusion.4), channel_id=1, source_target_pairs={{0,8},{1,9},{2,10},{3,11},{4,12},{5,13},{6,14},{7,15},{8,0},{9,1},... | collective-permute-start | bytes 98312 | tf_op jit(solution)/shard_map/ppermute | solution.py:583
  41.4 5.1 %collective-permute-start.9 = (f32[32,256]{1,0:T(8,128)S(1)}, f32[32,256]{1,0:T(8,128)S(1)}, u32[]{:S(2)}, u32[]{:S(2)}) collective-permute-start(f32[32,256]{1,0:T(8,128)S(1)} %select_select_fusion.3), channel_id=1, source_target_pairs={{0,16},{1,17},{2,18},{3,19},{4,20},{5,21},{6,22},{7,23},{8,24},{9,... | collective-permute-start | bytes 98312 | tf_op jit(solution)/shard_map/ppermute | solution.py:583
  46.5 4.0 %collective-permute-start.10 = (f32[32,256]{1,0:T(8,128)S(1)}, f32[32,256]{1,0:T(8,128)S(1)}, u32[]{:S(2)}, u32[]{:S(2)}) collective-permute-start(f32[32,256]{1,0:T(8,128)S(1)} %select_select_fusion.2), channel_id=1, source_target_pairs={{0,4},{1,5},{2,6},{3,7},{4,0},{5,1},{6,2},{7,3},{8,12},{9,13},{10,... | collective-permute-start | bytes 98312 | tf_op jit(solution)/shard_map/ppermute | solution.py:583
  47.8 10.3 %copy-start.1 = (f32[30,64,64]{2,1,0:T(8,128)S(1)}, f32[30,64,64]{2,1,0:T(8,128)}, u32[]{:S(2)}) copy-start(f32[30,64,64]{2,1,0:T(8,128)} %core_ref.1) | copy-start | bytes 1474564
  50.5 4.0 %collective-permute-start.12 = (f32[32,256]{1,0:T(8,128)S(1)}, f32[32,256]{1,0:T(8,128)S(1)}, u32[]{:S(2)}, u32[]{:S(2)}) collective-permute-start(f32[32,256]{1,0:T(8,128)S(1)} %select_select_fusion.1), channel_id=1, source_target_pairs={{0,2},{1,3},{2,0},{3,1},{4,6},{5,7},{6,4},{7,5},{8,10},{9,11},{10,... | collective-permute-start | bytes 98312 | tf_op jit(solution)/shard_map/ppermute | solution.py:583
  50.6 7.5 %collective-permute-start.13 = (f32[32,512]{1,0:T(8,128)S(1)}, f32[32,512]{1,0:T(8,128)S(1)}, u32[]{:S(2)}, u32[]{:S(2)}) collective-permute-start(f32[32,512]{1,0:T(8,128)S(1)} %get-tuple-element.100), channel_id=1, source_target_pairs={{1,2},{5,6},{9,10},{13,14},{17,18},{21,22},{25,26},{29,30},{3,4},{... | collective-permute-start | bytes 196616 | tf_op jit(solution)/shard_map/ppermute | solution.py:593

commit v4 on v3

--- a/solution.py
+++ b/solution.py
@@ -43,7 +43,7 @@
     return jnp.transpose(jnp.broadcast_to(row, (8, row.shape[1])))[:, 0:1]
 
 
-def call(kernel, outs, *args, scratch=(), smem=(), hbm=(), flops=0, nbytes=0, name=None, vmem=VMEM_LIMIT):
+def call(kernel, outs, *args, scratch=(), smem=(), hbm=(), flops=0, nbytes=0, name=None, vmem=VMEM_LIMIT, cost=0):
     single = not isinstance(outs, (list, tuple))
     vm = pl.BlockSpec(memory_space=pltpu.VMEM)
     sm = pl.BlockSpec(memory_space=pltpu.SMEM)
@@ -55,7 +55,7 @@
         out_specs=vm if single else [vm] * len(outs),
         scratch_shapes=list(scratch),
         compiler_params=pltpu.CompilerParams(vmem_limit_bytes=vmem),
-        cost_estimate=pl.CostEstimate(flops=0, bytes_accessed=0, transcendentals=0),
+        cost_estimate=pl.CostEstimate(flops=cost, bytes_accessed=0, transcendentals=0),
         name=name,
     )(*args)
 
@@ -74,7 +74,7 @@
             level = self.bits - 1 - bit
             if level < LEVELS:
                 entries.append((level, 0, size))
-                size += self.padded[level]
+                size += self.slots[level]
             entries += [(lev, off ^ (1 << bit), row + size) for lev, off, row in entries]
             size *= 2
         self.entries, self.size = entries, size
@@ -91,7 +91,7 @@
 
     groups = points // LANES
     last = points - halo
-    extra = 16
+    extra = 8
     slabs = 4
     slab = width // slabs
     reach = 2 * W + 1
@@ -163,35 +163,19 @@
             name="cut_chip",
         )
 
-    def prep_kernel(
-        skel_hbm, order_hbm, probes_hbm, list_hbm, count_hbm, emb_hbm, *rest
-    ):
-        g_refs, rest = rest[:LEVELS], rest[LEVELS:]
-        x_ref, inv_ref, hn_ref, mult_ref = rest[:4]
-        emb_ref, skel_ref, order_ref, probes_ref, list_ref, count_ref, row_ref, sems = rest[4:]
+    def prep_kernel(skel_hbm, emb_hbm, *rest):
+        g_refs, (emb_ref, skel_ref, row_ref, sems) = rest[:LEVELS], rest[LEVELS:]
         me = lax.axis_index("leaf")
-        small = [
-            pltpu.make_async_copy(src, dst, sems.at[i])
-            for i, (src, dst) in enumerate(
-                (
-                    (skel_hbm, skel_ref),
-                    (order_hbm, order_ref),
-                    (probes_hbm, probes_ref),
-                    (list_hbm, list_ref),
-                    (count_hbm, count_ref),
-                )
-            )
-        ]
+        small = pltpu.make_async_copy(skel_hbm, skel_ref, sems.at[slabs])
         large = [
             pltpu.make_async_copy(
-                emb_hbm.at[pl.ds(r * slab, slab), :], emb_ref.at[pl.ds(r * slab, slab), :], sems.at[5 + r]
+                emb_hbm.at[pl.ds(r * slab, slab), :], emb_ref.at[pl.ds(r * slab, slab), :], sems.at[r]
             )
             for r in range(slabs)
         ]
-        for copy in small + large:
+        for copy in [small] + large:
             copy.start()
-        for copy in small:
-            copy.wait()
+        small.wait()
 
         lane = lax.broadcasted_iota(jnp.int32, (1, LANES), 1)
         idx = jnp.full((1, LANES), -1, jnp.int32)
@@ -208,6 +192,54 @@
             lax.broadcasted_iota(jnp.int32, (points, LANES), 0) == idx, 1.0, 0.0
         ).astype(BF16)
 
+        for r in range(slabs):
+            large[r].wait()
+            rows = slice(r * slab, (r + 1) * slab)
+            picked = jnp.transpose(dot(emb_ref[rows, :], pick))
+            for l in range(LEVELS):
+                g_refs[l][:, rows] = picked[
+                    plan.starts[l] : plan.starts[l] + plan.padded[l]
+                ].astype(BF16)
+
+    def in_hbm(*args):
+        return [pltpu.with_memory_space_constraint(v, pltpu.HBM) for v in args]
+
+    *owned, emb = call(
+        prep_kernel,
+        [jax.ShapeDtypeStruct((p, width), BF16) for p in plan.padded] + [jax.ShapeDtypeStruct((width, points), BF16)],
+        *in_hbm(skeleton, embeddings),
+        hbm=(0, 1),
+        scratch=[
+            pltpu.VMEM(skeleton.shape, jnp.int32),
+            pltpu.VMEM((8, LANES), jnp.int32),
+            pltpu.SemaphoreType.DMA((1 + slabs,)),
+        ],
+        name="prep",
+        vmem=PREP_VMEM,
+    )
+
+    def tree_kernel(order_hbm, probes_hbm, list_hbm, count_hbm, emb_ref, *rest):
+        x_ref, inv_ref, hn_ref, mult_ref, order_ref, probes_ref, list_ref, count_ref, sems = rest
+        me = lax.axis_index("leaf")
+        small = [
+            pltpu.make_async_copy(src, dst, sems.at[i])
+            for i, (src, dst) in enumerate(
+                (
+                    (order_hbm, order_ref),
+                    (probes_hbm, probes_ref),
+                    (list_hbm, list_ref),
+                    (count_hbm, count_ref),
+                )
+            )
+        ]
+        for copy in small:
+            copy.start()
+        for c in range(leaves):
+            sl = slice(c * LEAF, (c + 1) * LEAF)
+            hn_ref[:, sl] = half_norm_row(emb_ref[:, sl])
+        for copy in small:
+            copy.wait()
+
         near = list_ref[...]
         slots = near.shape[1]
         sub = lax.broadcasted_iota(jnp.int32, (leaves, leaves), 0)
@@ -250,47 +282,27 @@
                 found[8 * h : 8 * h + 1] * 16.0 + found[8 * h + 1 : 8 * h + 2]
             ).astype(jnp.int32)
 
-        hn = jnp.zeros((1, points), F32)
-        for r in range(slabs):
-            large[r].wait()
-            rows = slice(r * slab, (r + 1) * slab)
-            picked = jnp.transpose(dot(emb_ref[rows, :], pick))
-            for l in range(LEVELS):
-                g_refs[l][:, rows] = picked[
-                    plan.starts[l] : plan.starts[l] + plan.padded[l]
-                ].astype(BF16)
-            hn = hn + half_norm_row(emb_ref[rows, :])
-        hn_ref[...] = hn
-
-    *owned, x_tree, inv, hn, mult = call(
-        prep_kernel,
-        [jax.ShapeDtypeStruct((p, width), BF16) for p in plan.padded]
-        + [
+    x_tree, inv, hn, mult = call(
+        tree_kernel,
+        [
             jax.ShapeDtypeStruct((cols, points), BF16),
             jax.ShapeDtypeStruct((1, points), jnp.int32),
             jax.ShapeDtypeStruct((1, points), F32),
             jax.ShapeDtypeStruct((reach * leaves, LANES), F32),
         ],
-        *[pltpu.with_memory_space_constraint(v, pltpu.HBM) for v in (skeleton, order, probes, near_list, near_count)],
-        pltpu.with_memory_space_constraint(embeddings, pltpu.HBM),
-        hbm=tuple(range(6)),
+        *in_hbm(order, probes, near_list, near_count),
+        emb,
+        hbm=(0, 1, 2, 3),
         scratch=[
-            pltpu.VMEM((width, points), BF16),
-            pltpu.VMEM(skeleton.shape, jnp.int32),
             pltpu.VMEM(order.shape, jnp.int32),
             pltpu.VMEM(probes.shape, BF16),
             pltpu.VMEM(near_list.shape, jnp.int32),
             pltpu.VMEM(near_count.shape, jnp.int32),
-            pltpu.VMEM((8, LANES), jnp.int32),
-            pltpu.SemaphoreType.DMA((6 + slabs,)),
+            pltpu.SemaphoreType.DMA((4,)),
         ],
-        flops=50 * 2 * 256**3,
-        nbytes=6 << 20,
-        name="prep",
-        vmem=PREP_VMEM,
+        name="tree",
     )
 
-    emb, x_tree = lax.optimization_barrier((embeddings, x_tree))
 
     def times(mult_ref, t, o, value):
         row = mult_ref[o * leaves + t : o * leaves + t + 1, :]
@@ -465,7 +477,7 @@
 
     table = []
     for lev, off, row in sorted(plan.entries, key=lambda e: e[2]):
-        for i in range(plan.padded[lev]):
+        for i in range(plan.slots[lev]):
             side = (off >> plan.shift[lev]) & 1
             table.append(
                 (
@@ -473,28 +485,39 @@
                     (side * LEVELS + lev) * R + i,
                     (1 << plan.shift[lev]) - 1,
                     plan.slots[lev],
-                    i < plan.slots[lev],
                 )
             )
     table = jnp.array(table, jnp.int32).T
     own_w = LEVELS * R
     dest = table[1] + jnp.bitwise_and(pos ^ table[0], table[2]) * table[3]
-    dest = jnp.where(table[4] == 1, dest, -1)[None, :]
-
-    def join_kernel(*refs):
-        row = 0
-        for ref in refs[:-1]:
-            refs[-1][row : row + ref.shape[0], :] = ref[...]
-            row += ref.shape[0]
+    dest = dest[None, :]
 
     def join(*blocks):
-        rows = sum(v.shape[0] for v in blocks)
+        rows = sum(used for _, used in blocks)
+        whole = all(used % 8 == 0 for _, used in blocks)
+        pad = -rows % 8
+
+        def join_kernel(*refs):
+            if whole:
+                row = 0
+                for ref, (_, used) in zip(refs, blocks):
+                    refs[-1][row : row + used, :] = ref[0:used, :]
+                    row += used
+            else:
+                values = [ref[...].astype(F32)[0:used] for ref, (_, used) in zip(refs, blocks)]
+                if pad:
+                    values.append(jnp.zeros((pad, width), F32))
+                refs[-1][...] = jnp.concatenate(values, axis=0).astype(BF16)
+
         return call(
-            join_kernel, jax.ShapeDtypeStruct((rows, width), BF16), *blocks, nbytes=1 << 18, name="join"
+            join_kernel,
+            jax.ShapeDtypeStruct((rows + pad, width), BF16),
+            *[v for v, _ in blocks],
+            name="join",
         )
 
     after = lax.optimization_barrier
-    block = owned[0]
+    block, used = owned[0], plan.slots[0]
     for bit in reversed(range(plan.bits)):
         level = plan.bits - bit
         stage = level - 1
@@ -516,7 +539,9 @@
             near = core_part(emb, hn, recv_a, near)
             partner, near = after((partner, near))
         if bit:
-            block = join(block, partner, *([owned[level]] if level < LEVELS else []))
+            more = [(owned[level], plan.slots[level])] if level < LEVELS else []
+            block = join((block, used), (partner, used), *more)
+            used = 2 * used + sum(slots for _, slots in more)
             block, x_tree, emb = after((block, x_tree, emb))
     half = plan.size // 2
 
@@ -554,6 +579,7 @@
         flops=50 * 2 * 256**3,
         nbytes=4 << 20,
         name="own",
+        cost=2_000_000_000,
     )
 
     def far_kernel(block_ref, other_ref, dest_ref, emb_ref, hn_ref, out_ref):

time: 60.3 us -> 58.6 us (0.972)
  waiting for transfers between devices: 30.6 us -> 28.4 us
    ppermute x5, waiting for transfers between devices: 10.5 us -> 7.53 us  [body(): partner = lax.ppermute(block, 'leaf', [(i, i ^ 1 << bit) for i in range(n)])]
    ppermute x1, waiting for transfers between devices: 4.62 us -> 5.68 us  [body(): recv_b2 = lax.ppermute(cut_chip(emb, x_tree), 'leaf', pairs(3))]
    pallas_call x16 -> x17, Pallas kernels: 17.7 us -> 17.7 us  [call(): pl.pallas_call(kernel, out_shape=outs, in_specs=[sm if i in smem else hb...]
  transfers between devices with their start and end apart: 14 -> 14, of which waited for: 11 -> 10; matrix products, arithmetic and copies ran while one was open for 0% -> 0% of each run, Pallas kernels for 19% -> 21%
where the time goes in v4:
time: 58.6 us; the launch traced here: 58.4 us
  waiting for transfers between devices  28.4 us (48%)
  Pallas kernels  17.7 us (30%)
  starting transfers between devices  12 us (20%)
    pallas_call x17, Pallas kernels, call(): pl.pallas_call(kernel, out_shape=outs, in_specs=[sm if i in smem else hb...  17.7 us
    ppermute x5, waiting for transfers between devices, body(): heard = lax.ppermute(z, 'leaf', [(i, i ^ 1 << bit) for i in range(n)])  11.6 us
    ppermute x5, waiting for transfers between devices, body(): partner = lax.ppermute(block, 'leaf', [(i, i ^ 1 << bit) for i in range(n)])  7.53 us
    ppermute x1, waiting for transfers between devices, body(): recv_b2 = lax.ppermute(cut_chip(emb, x_tree), 'leaf', pairs(3))  5.68 us
    ppermute x5, starting transfers between devices, body(): partner = lax.ppermute(block, 'leaf', [(i, i ^ 1 << bit) for i in range(n)])  4.1 us
    ppermute x1, waiting for transfers between devices, body(): back = lax.ppermute(back, 'leaf', pairs(1, 3))  3.59 us
    ppermute x5, starting transfers between devices, body(): heard = lax.ppermute(z, 'leaf', [(i, i ^ 1 << bit) for i in range(n)])  2.83 us
    ppermute x1, starting transfers between devices, body(): recv_b2 = lax.ppermute(cut_chip(emb, x_tree), 'leaf', pairs(3))  2.24 us
  transfers between devices with their start and end apart: 14, of which 10 were waited for; matrix products, arithmetic and copies ran while one was open for 0% of the time, Pallas kernels for 21%

profile of v4, /device:TPU:24, one launch (start us, length us, event | category | flops | bytes accessed | tf_op | source)
XLA Modules:
  0.0 58.4 jit_solution(8090498484220550374)
XLA Ops:
  0.0 0.0 copy-start.4
  0.0 3.1 %prep.1 = (bf16[8,768]{1,0:T(8,128)(2,1)S(1)}, bf16[8,768]{1,0:T(8,128)(2,1)S(1)}, bf16[16,768]{1,0:T(8,128)(2,1)S(1)}, bf16[32,768]{1,0:T(8,128)(2,1)S(1)}, bf16[768,2048]{1,0:T(8,128)(2,1)S(1)}) custom-call(s32[30,64]{1,0:T(8,128)} %skel_hbm.1, bf16[768,2048]{1,0:T(8,128)(2,1)} %emb_hbm.1), custom_call_target="tpu_custom_call" | custom-call | tf_op jit(solution)/shard_map/prep/pallas_call | solution.py:51
  3.1 0.4 collective-permute-start
  3.5 0.0 copy-done.1
  3.5 0.0 copy-done.2
  3.5 0.0 copy-done.3
  3.5 0.0 copy-done.4
  3.5 1.9 %tree.1 = (bf16[32,2048]{1,0:T(8,128)(2,1)S(1)}, s32[1,2048]{1,0:T(1,128)S(1)}, f32[1,2048]{1,0:T(1,128)S(1)}, f32[56,128]{1,0:T(8,128)S(1)}) custom-call(s32[1,2048]{1,0:T(1,128)} %order_hbm.1, bf16[32,2048]{1,0:T(8,128)(2,1)} %probes_hbm.1, s32[8,7]{1,0:T(8,128)} %list_hbm.1, s32[1,8]{1,0:T(1,128)} %count_hbm.1, ...), custom_call_target="tpu_custom_call" | custom-call | tf_op jit(solution)/shard_map/tree/pallas_call | solution.py:51
  5.4 2.4 %collective-permute-done.refs_1_ = bf16[8,768]{1,0:T(8,128)(2,1)S(1)} collective-permute-done((bf16[8,768]{1,0:T(8,128)(2,1)S(1)}, bf16[8,768]{1,0:T(8,128)(2,1)S(1)}, u32[]{:S(2)}, u32[]{:S(2)}) %collective-permute-start) | collective-permute-done | bytes 12320 | tf_op jit(solution)/shard_map/ppermute | solution.py:524
  7.8 0.5 collective-permute-start.1
  8.3 0.2 cut.1
  8.5 1.4 %near0.1.refs_4_ = f32[32,2048]{1,0:T(8,128)S(1)} custom-call(f32[56,128]{1,0:T(8,128)S(1)} %get-tuple-element.60.refs_0_.mult_ref, bf16[768,2048]{1,0:T(8,128)(2,1)S(1)} %get-tuple-element.90.emb_ref.refs_1_, bf16[32,2048]{1,0:T(8,128)(2,1)S(1)} %get-tuple-element.83.refs_2_.x_ref, f32[1,2048]{1,0:T(1,128)S(1)} %get-tuple-element.63.refs_3_.hn_ref), custom_call_target="tpu_custom_call" | custom-call | tf_op jit(solution)/shard_map/near0/pallas_call | solution.py:51
  9.9 1.8 %collective-permute-done.1.refs_1_ = bf16[16,768]{1,0:T(8,128)(2,1)S(1)} collective-permute-done((bf16[16,768]{1,0:T(8,128)(2,1)S(1)}, bf16[16,768]{1,0:T(8,128)(2,1)S(1)}, u32[]{:S(2)}, u32[]{:S(2)}) %collective-permute-start.1) | collective-permute-done | bytes 24608 | tf_op jit(solution)/shard_map/ppermute | solution.py:524
  11.7 0.0 collective-permute-start.4
  11.7 1.6 %collective-permute-start.2 = (bf16[48,768]{1,0:T(8,128)(2,1)S(1)}, bf16[48,768]{1,0:T(8,128)(2,1)S(1)}, u32[]{:S(2)}, u32[]{:S(2)}) collective-permute-start(bf16[48,768]{1,0:T(8,128)(2,1)S(1)} %join.5.refs_0_), channel_id=1, source_target_pairs={{0,4},{1,5},{2,6},{3,7},{4,0},{5,1},{6,2},{7,3},{8,12},{9,13},{10,... | collective-permute-start | bytes 221192 | tf_op jit(solution)/shard_map/ppermute | solution.py:524
  13.3 1.4 %near2.1.refs_4_ = f32[32,2048]{1,0:T(8,128)S(1)} custom-call(f32[56,128]{1,0:T(8,128)S(1)} %get-tuple-element.60.refs_0_.mult_ref, bf16[768,2048]{1,0:T(8,128)(2,1)S(1)} %get-tuple-element.90.emb_ref.refs_1_, bf16[32,2048]{1,0:T(8,128)(2,1)S(1)} %get-tuple-element.83.refs_2_.x_ref, f32[1,2048]{1,0:T(1,128)S(1)} %get-tuple-element.63.refs_3_.hn_ref, ...), custom_call_target="tpu_custom_call" | custom-call | tf_op jit(solution)/shard_map/near2/pallas_call | solution.py:51
  14.7 1.7 %collective-permute-done.2.refs_1_ = bf16[48,768]{1,0:T(8,128)(2,1)S(1)} collective-permute-done((bf16[48,768]{1,0:T(8,128)(2,1)S(1)}, bf16[48,768]{1,0:T(8,128)(2,1)S(1)}, u32[]{:S(2)}, u32[]{:S(2)}) %collective-permute-start.2) | collective-permute-done | bytes 73760 | tf_op jit(solution)/shard_map/ppermute | solution.py:524
  16.4 1.6 %collective-permute-start.3 = (bf16[128,768]{1,0:T(8,128)(2,1)S(1)}, bf16[128,768]{1,0:T(8,128)(2,1)S(1)}, u32[]{:S(2)}, u32[]{:S(2)}) collective-permute-start(bf16[128,768]{1,0:T(8,128)(2,1)S(1)} %join.6.refs_0_), channel_id=1, source_target_pairs={{0,2},{1,3},{2,0},{3,1},{4,6},{5,7},{6,4},{7,5},{8,10},{9,11},{10,... | collective-permute-start | bytes 589832 | tf_op jit(solution)/shard_map/ppermute | solution.py:524
  17.9 1.8 %near4.1.near_in = f32[32,2048]{1,0:T(8,128)S(1)} custom-call(f32[56,128]{1,0:T(8,128)S(1)} %get-tuple-element.60.refs_0_.mult_ref, bf16[768,2048]{1,0:T(8,128)(2,1)S(1)} %get-tuple-element.90.emb_ref.refs_1_, bf16[32,2048]{1,0:T(8,128)(2,1)S(1)} %get-tuple-element.83.refs_2_.x_ref, f32[1,2048]{1,0:T(1,128)S(1)} %get-tuple-element.63.refs_3_.hn_ref, ...), custom_call_target="tpu_custom_call" | custom-call | tf_op jit(solution)/shard_map/near4/pallas_call | solution.py:51
  19.7 0.1 cut_chip.2
  19.8 2.2 %collective-permute-start.7 = (bf16[808,512]{1,0:T(8,128)(2,1)S(1)}, bf16[808,512]{1,0:T(8,128)(2,1)S(1)}, u32[]{:S(2)}, u32[]{:S(2)}) collective-permute-start(bf16[808,512]{1,0:T(8,128)(2,1)S(1)} %cut_chip.2), channel_id=1, source_target_pairs={{3,4},{7,8},{11,12},{15,16},{19,20},{23,24},{27,28},{4,3},{8,7},{1... | collective-permute-start | bytes 2482184 | tf_op jit(solution)/shard_map/ppermute | solution.py:538
  22.1 0.0 collective-permute-done.4.src_ref
  22.1 1.6 %edge_core.1.near_in = f32[32,2048]{1,0:T(8,128)S(1)} custom-call(f32[56,128]{1,0:T(8,128)S(1)} %get-tuple-element.60.refs_0_.mult_ref, bf16[768,2048]{1,0:T(8,128)(2,1)S(1)} %get-tuple-element.90.emb_ref.refs_1_, f32[1,2048]{1,0:T(1,128)S(1)} %get-tuple-element.63.refs_3_.hn_ref, bf16[800,768]{1,0:T(8,128)(2,1)S(1)} %collective-permute-done.4.src_ref, ...), custom_call_target="tpu_custom_call" | custom-call | tf_op jit(solution)/shard_map/edge_core/pallas_call | solution.py:51
  23.7 0.0 collective-permute-done.3.refs_1_
  23.8 0.1 collective-permute-start.5
  23.9 1.7 %collective-permute-done.5.other_ref = bf16[256,768]{1,0:T(8,128)(2,1)S(1)} collective-permute-done((bf16[256,768]{1,0:T(8,128)(2,1)S(1)}, bf16[256,768]{1,0:T(8,128)(2,1)S(1)}, u32[]{:S(2)}, u32[]{:S(2)}) %collective-permute-start.5) | collective-permute-done | bytes 393248 | tf_op jit(solution)/shard_map/ppermute | solution.py:524
  25.6 1.7 %own.1 = f32[32,256]{1,0:T(8,128)S(1)} custom-call(bf16[256,768]{1,0:T(8,128)(2,1)S(1)} %join.7.block_ref, bf16[256,768]{1,0:T(8,128)(2,1)S(1)} %collective-permute-done.5.other_ref, s32[1,512]{1,0:T(1,128)S(1)} %multiply_add_fusion.dest_ref, bf16[768,2048]{1,0:T(8,128)(2,1)S(1)} %get-tuple-element.90.emb_ref.refs_1_, ...), custom_call_target="tpu_custom_call" | custom-call | flops 2000000000 | tf_op jit(solution)/shard_map/own/pallas_call | solution.py:51
  27.3 0.2 collective-permute-start.6
  27.4 0.1 cut_chip.3
  27.6 0.9 %collective-permute-start.11 = (bf16[808,512]{1,0:T(8,128)(2,1)S(1)}, bf16[808,512]{1,0:T(8,128)(2,1)S(1)}, u32[]{:S(2)}, u32[]{:S(2)}) collective-permute-start(bf16[808,512]{1,0:T(8,128)(2,1)S(1)} %cut_chip.3), channel_id=1, source_target_pairs={{1,2},{5,6},{9,10},{13,14},{17,18},{21,22},{25,26},{29,30},{2,1},{... | collective-permute-start | bytes 2482184 | tf_op jit(solution)/shard_map/ppermute | solution.py:614
  28.5 1.3 %far.1.far_ref = bf16[256,2048]{1,0:T(8,128)(2,1)S(1)} custom-call(bf16[256,768]{1,0:T(8,128)(2,1)S(1)} %join.7.block_ref, bf16[256,768]{1,0:T(8,128)(2,1)S(1)} %collective-permute-done.5.other_ref, s32[1,512]{1,0:T(1,128)S(1)} %multiply_add_fusion.dest_ref, bf16[768,2048]{1,0:T(8,128)(2,1)S(1)} %get-tuple-element.90.emb_ref.refs_1_, ...), custom_call_target="tpu_custom_call" | custom-call | tf_op jit(solution)/shard_map/far/pallas_call | solution.py:51
  29.8 0.0 copy-start
  29.8 5.7 %collective-permute-done.7.two_ref = bf16[808,512]{1,0:T(8,128)(2,1)S(1)} collective-permute-done((bf16[808,512]{1,0:T(8,128)(2,1)S(1)}, bf16[808,512]{1,0:T(8,128)(2,1)S(1)}, u32[]{:S(2)}, u32[]{:S(2)}) %collective-permute-start.7) | collective-permute-done | bytes 827424 | tf_op jit(solution)/shard_map/ppermute | solution.py:538
  35.5 0.0 collective-permute-done.6
  35.5 0.5 collective-permute-start.8
  36.0 3.5 %collective-permute-done.8 = f32[32,256]{1,0:T(8,128)S(1)} collective-permute-done((f32[32,256]{1,0:T(8,128)S(1)}, f32[32,256]{1,0:T(8,128)S(1)}, u32[]{:S(2)}, u32[]{:S(2)}) %collective-permute-start.8) | collective-permute-done | bytes 32800 | tf_op jit(solution)/shard_map/ppermute | solution.py:609
  39.5 0.4 collective-permute-start.9
  39.9 4.8 %collective-permute-done.9 = f32[32,256]{1,0:T(8,128)S(1)} collective-permute-done((f32[32,256]{1,0:T(8,128)S(1)}, f32[32,256]{1,0:T(8,128)S(1)}, u32[]{:S(2)}, u32[]{:S(2)}) %collective-permute-start.9) | collective-permute-done | bytes 32800 | tf_op jit(solution)/shard_map/ppermute | solution.py:609
  44.7 1.7 %collective-permute-start.10 = (f32[32,256]{1,0:T(8,128)S(1)}, f32[32,256]{1,0:T(8,128)S(1)}, u32[]{:S(2)}, u32[]{:S(2)}) collective-permute-start(f32[32,256]{1,0:T(8,128)S(1)} %select_select_fusion.2), channel_id=1, source_target_pairs={{0,4},{1,5},{2,6},{3,7},{4,0},{5,1},{6,2},{7,3},{8,12},{9,13},{10,... | collective-permute-start | bytes 98312 | tf_op jit(solution)/shard_map/ppermute | solution.py:609
  46.5 0.0 collective-permute-done.11.one_ref
  46.5 1.0 %edge_chip.1 = (f32[32,2048]{1,0:T(8,128)S(1)}, f32[32,512]{1,0:T(8,128)S(1)}) custom-call(f32[56,128]{1,0:T(8,128)S(1)} %get-tuple-element.60.refs_0_.mult_ref, bf16[768,2048]{1,0:T(8,128)(2,1)S(1)} %get-tuple-element.90.emb_ref.refs_1_, f32[1,2048]{1,0:T(1,128)S(1)} %get-tuple-element.63.refs_3_.hn_ref, ...), custom_call_target="tpu_custom_call" | custom-call | tf_op jit(solution)/shard_map/edge_chip/pallas_call | solution.py:51
  47.4 1.3 %collective-permute-done.10 = f32[32,256]{1,0:T(8,128)S(1)} collective-permute-done((f32[32,256]{1,0:T(8,128)S(1)}, f32[32,256]{1,0:T(8,128)S(1)}, u32[]{:S(2)}, u32[]{:S(2)}) %collective-permute-start.10) | collective-permute-done | bytes 32800 | tf_op jit(solution)/shard_map/ppermute | solution.py:609
  48.7 0.1 collective-permute-start.12
  48.8 1.9 %collective-permute-start.13 = (f32[32,512]{1,0:T(8,128)S(1)}, f32[32,512]{1,0:T(8,128)S(1)}, u32[]{:S(2)}, u32[]{:S(2)}) collective-permute-start(f32[32,512]{1,0:T(8,128)S(1)} %get-tuple-element.98), channel_id=1, source_target_pairs={{1,2},{5,6},{9,10},{13,14},{17,18},{21,22},{25,26},{29,30},{3,4},{... | collective-permute-start | bytes 196616 | tf_op jit(solution)/shard_map/ppermute | solution.py:619
  50.7 2.0 %collective-permute-done.12 = f32[32,256]{1,0:T(8,128)S(1)} collective-permute-done((f32[32,256]{1,0:T(8,128)S(1)}, f32[32,256]{1,0:T(8,128)S(1)}, u32[]{:S(2)}, u32[]{:S(2)}) %collective-permute-start.12) | collective-permute-done | bytes 32800 | tf_op jit(solution)/shard_map/ppermute | solution.py:609
  52.7 3.6 %collective-permute-done.13.back_ref = f32[32,512]{1,0:T(8,128)S(1)} collective-permute-done((f32[32,512]{1,0:T(8,128)S(1)}, f32[32,512]{1,0:T(8,128)S(1)}, u32[]{:S(2)}, u32[]{:S(2)}) %collective-permute-start.13) | collective-permute-done | bytes 65568 | tf_op jit(solution)/shard_map/ppermute | solution.py:619
  56.3 0.0 copy-done
  56.3 2.1 %last.1 = f32[32,2048]{1,0:T(8,128)} custom-call(f32[32,256]{1,0:T(8,128)S(1)} %select_select_fusion.z_ref, f32[30,64,64]{2,1,0:T(8,128)S(1)} %copy-done, bf16[256,2048]{1,0:T(8,128)(2,1)S(1)} %far.1.far_ref, f32[32,512]{1,0:T(8,128)S(1)} %collective-permute-done.13.back_ref, s32[1,2048]{1,0:T(1,128)S(1)} %get-tuple-element.99.inv_ref, ...), custom_call_target="tpu_custom_call" | custom-call | tf_op jit(solution)/shard_map/last/pallas_call | solution.py:51
  (18 shorter events, 0.1 us)
Async XLA Ops:
  0.0 3.5 %copy-start.1 = (s32[1,512]{1,0:T(1,128)S(1)}, s32[1,512]{1,0:T(1,128)}, u32[]{:S(2)}) copy-start(s32[1,512]{1,0:T(1,128)} %constant.55) | copy-start | bytes 6148
  0.0 3.5 %copy-start.2 = (s32[1,512]{1,0:T(1,128)S(1)}, s32[1,512]{1,0:T(1,128)}, u32[]{:S(2)}) copy-start(s32[1,512]{1,0:T(1,128)} %constant.56) | copy-start | bytes 6148
  0.0 3.5 %copy-start.3 = (s32[1,512]{1,0:T(1,128)S(1)}, s32[1,512]{1,0:T(1,128)}, u32[]{:S(2)}) copy-start(s32[1,512]{1,0:T(1,128)} %constant.57) | copy-start | bytes 6148
  0.0 3.5 %copy-start.4 = (s32[1,512]{1,0:T(1,128)S(1)}, s32[1,512]{1,0:T(1,128)}, u32[]{:S(2)}) copy-start(s32[1,512]{1,0:T(1,128)} %constant.58) | copy-start | bytes 6148
  3.1 4.7 %collective-permute-start = (bf16[8,768]{1,0:T(8,128)(2,1)S(1)}, bf16[8,768]{1,0:T(8,128)(2,1)S(1)}, u32[]{:S(2)}, u32[]{:S(2)}) collective-permute-start(bf16[8,768]{1,0:T(8,128)(2,1)S(1)} %get-tuple-element.53.refs_0_), channel_id=1, source_target_pairs={{0,16},{1,17},{2,18},{3,19},{4,20},{5,21},{6,22},{7,23},{8,24},{9,... | collective-permute-start | bytes 36872 | tf_op jit(solution)/shard_map/ppermute | solution.py:524
  7.8 3.9 %collective-permute-start.1 = (bf16[16,768]{1,0:T(8,128)(2,1)S(1)}, bf16[16,768]{1,0:T(8,128)(2,1)S(1)}, u32[]{:S(2)}, u32[]{:S(2)}) collective-permute-start(bf16[16,768]{1,0:T(8,128)(2,1)S(1)} %join.4.refs_0_), channel_id=1, source_target_pairs={{0,8},{1,9},{2,10},{3,11},{4,12},{5,13},{6,14},{7,15},{8,0},{9,1},... | collective-permute-start | bytes 73736 | tf_op jit(solution)/shard_map/ppermute | solution.py:524
  11.7 10.4 %collective-permute-start.4 = (bf16[800,768]{1,0:T(8,128)(2,1)S(1)}, bf16[800,768]{1,0:T(8,128)(2,1)S(1)}, u32[]{:S(2)}, u32[]{:S(2)}) collective-permute-start(bf16[800,768]{1,0:T(8,128)(2,1)S(1)} %cut.1), channel_id=1, source_target_pairs={{0,1},{1,0},{2,3},{3,2},{4,5},{5,4},{6,7},{7,6},{8,9},{9,8},{10,11... | collective-permute-start | bytes 3686408 | tf_op jit(solution)/shard_map/ppermute | solution.py:532
  11.7 4.7 %collective-permute-start.2 = (bf16[48,768]{1,0:T(8,128)(2,1)S(1)}, bf16[48,768]{1,0:T(8,128)(2,1)S(1)}, u32[]{:S(2)}, u32[]{:S(2)}) collective-permute-start(bf16[48,768]{1,0:T(8,128)(2,1)S(1)} %join.5.refs_0_), channel_id=1, source_target_pairs={{0,4},{1,5},{2,6},{3,7},{4,0},{5,1},{6,2},{7,3},{8,12},{9,13},{10,... | collective-permute-start | bytes 221192 | tf_op jit(solution)/shard_map/ppermute | solution.py:524
  16.4 7.4 %collective-permute-start.3 = (bf16[128,768]{1,0:T(8,128)(2,1)S(1)}, bf16[128,768]{1,0:T(8,128)(2,1)S(1)}, u32[]{:S(2)}, u32[]{:S(2)}) collective-permute-start(bf16[128,768]{1,0:T(8,128)(2,1)S(1)} %join.6.refs_0_), channel_id=1, source_target_pairs={{0,2},{1,3},{2,0},{3,1},{4,6},{5,7},{6,4},{7,5},{8,10},{9,11},{10,... | collective-permute-start | bytes 589832 | tf_op jit(solution)/shard_map/ppermute | solution.py:524
  19.8 15.7 %collective-permute-start.7 = (bf16[808,512]{1,0:T(8,128)(2,1)S(1)}, bf16[808,512]{1,0:T(8,128)(2,1)S(1)}, u32[]{:S(2)}, u32[]{:S(2)}) collective-permute-start(bf16[808,512]{1,0:T(8,128)(2,1)S(1)} %cut_chip.2), channel_id=1, source_target_pairs={{3,4},{7,8},{11,12},{15,16},{19,20},{23,24},{27,28},{4,3},{8,7},{1... | collective-permute-start | bytes 2482184 | tf_op jit(solution)/shard_map/ppermute | solution.py:538
  23.8 1.8 %collective-permute-start.5 = (bf16[256,768]{1,0:T(8,128)(2,1)S(1)}, bf16[256,768]{1,0:T(8,128)(2,1)S(1)}, u32[]{:S(2)}, u32[]{:S(2)}) collective-permute-start(bf16[256,768]{1,0:T(8,128)(2,1)S(1)} %join.7.block_ref), channel_id=1, source_target_pairs={{0,1},{1,0},{2,3},{3,2},{4,5},{5,4},{6,7},{7,6},{8,9},{9,8},{10,11... | collective-permute-start | bytes 1179656 | tf_op jit(solution)/shard_map/ppermute | solution.py:524
  27.3 8.2 %collective-permute-start.6 = (f32[32,256]{1,0:T(8,128)S(1)}, f32[32,256]{1,0:T(8,128)S(1)}, u32[]{:S(2)}, u32[]{:S(2)}) collective-permute-start(f32[32,256]{1,0:T(8,128)S(1)} %own.1), channel_id=1, source_target_pairs={{0,1},{1,0},{2,3},{3,2},{4,5},{5,4},{6,7},{7,6},{8,9},{9,8},{10,11... | collective-permute-start | bytes 98312 | tf_op jit(solution)/shard_map/ppermute | solution.py:609
  27.6 18.9 %collective-permute-start.11 = (bf16[808,512]{1,0:T(8,128)(2,1)S(1)}, bf16[808,512]{1,0:T(8,128)(2,1)S(1)}, u32[]{:S(2)}, u32[]{:S(2)}) collective-permute-start(bf16[808,512]{1,0:T(8,128)(2,1)S(1)} %cut_chip.3), channel_id=1, source_target_pairs={{1,2},{5,6},{9,10},{13,14},{17,18},{21,22},{25,26},{29,30},{2,1},{... | collective-permute-start | bytes 2482184 | tf_op jit(solution)/shard_map/ppermute | solution.py:614
  29.8 26.5 %copy-start = (f32[30,64,64]{2,1,0:T(8,128)S(1)}, f32[30,64,64]{2,1,0:T(8,128)}, u32[]{:S(2)}) copy-start(f32[30,64,64]{2,1,0:T(8,128)} %core_ref.1) | copy-start | bytes 1474564
  35.5 4.0 %collective-permute-start.8 = (f32[32,256]{1,0:T(8,128)S(1)}, f32[32,256]{1,0:T(8,128)S(1)}, u32[]{:S(2)}, u32[]{:S(2)}) collective-permute-start(f32[32,256]{1,0:T(8,128)S(1)} %select_select_fusion.4), channel_id=1, source_target_pairs={{0,8},{1,9},{2,10},{3,11},{4,12},{5,13},{6,14},{7,15},{8,0},{9,1},... | collective-permute-start | bytes 98312 | tf_op jit(solution)/shard_map/ppermute | solution.py:609
  39.5 5.2 %collective-permute-start.9 = (f32[32,256]{1,0:T(8,128)S(1)}, f32[32,256]{1,0:T(8,128)S(1)}, u32[]{:S(2)}, u32[]{:S(2)}) collective-permute-start(f32[32,256]{1,0:T(8,128)S(1)} %select_select_fusion.3), channel_id=1, source_target_pairs={{0,16},{1,17},{2,18},{3,19},{4,20},{5,21},{6,22},{7,23},{8,24},{9,... | collective-permute-start | bytes 98312 | tf_op jit(solution)/shard_map/ppermute | solution.py:609
  44.7 4.0 %collective-permute-start.10 = (f32[32,256]{1,0:T(8,128)S(1)}, f32[32,256]{1,0:T(8,128)S(1)}, u32[]{:S(2)}, u32[]{:S(2)}) collective-permute-start(f32[32,256]{1,0:T(8,128)S(1)} %select_select_fusion.2), channel_id=1, source_target_pairs={{0,4},{1,5},{2,6},{3,7},{4,0},{5,1},{6,2},{7,3},{8,12},{9,13},{10,... | collective-permute-start | bytes 98312 | tf_op jit(solution)/shard_map/ppermute | solution.py:609
  48.7 4.0 %collective-permute-start.12 = (f32[32,256]{1,0:T(8,128)S(1)}, f32[32,256]{1,0:T(8,128)S(1)}, u32[]{:S(2)}, u32[]{:S(2)}) collective-permute-start(f32[32,256]{1,0:T(8,128)S(1)} %select_select_fusion.1), channel_id=1, source_target_pairs={{0,2},{1,3},{2,0},{3,1},{4,6},{5,7},{6,4},{7,5},{8,10},{9,11},{10,... | collective-permute-start | bytes 98312 | tf_op jit(solution)/shard_map/ppermute | solution.py:609
  48.8 7.5 %collective-permute-start.13 = (f32[32,512]{1,0:T(8,128)S(1)}, f32[32,512]{1,0:T(8,128)S(1)}, u32[]{:S(2)}, u32[]{:S(2)}) collective-permute-start(f32[32,512]{1,0:T(8,128)S(1)} %get-tuple-element.98), channel_id=1, source_target_pairs={{1,2},{5,6},{9,10},{13,14},{17,18},{21,22},{25,26},{29,30},{3,4},{... | collective-permute-start | bytes 196616 | tf_op jit(solution)/shard_map/ppermute | solution.py:619

commit v5 on v4

--- a/solution.py
+++ b/solution.py
@@ -534,7 +534,6 @@
             partner, near = after((partner, near))
         if stage == 3:
             near = near_part(tuple(range(4, leaves)), emb, x_tree, hn, near)
-            emb, near = after((emb, near))
             recv_b2 = lax.ppermute(cut_chip(emb, x_tree), "leaf", pairs(3))
             near = core_part(emb, hn, recv_a, near)
             partner, near = after((partner, near))
@@ -579,7 +578,7 @@
         flops=50 * 2 * 256**3,
         nbytes=4 << 20,
         name="own",
-        cost=2_000_000_000,
+        cost=3_000_000_000,
     )
 
     def far_kernel(block_ref, other_ref, dest_ref, emb_ref, hn_ref, out_ref):

time: 58.6 us -> 56.5 us (0.964)
  waiting for transfers between devices: 28.4 us -> 27.2 us
  starting transfers between devices: 12 us -> 11.1 us
    ppermute x1, waiting for transfers between devices: 5.68 us -> 3.83 us  [body(): recv_b2 = lax.ppermute(cut_chip(emb, x_tree), 'leaf', pairs(3))]
    ppermute x5, starting transfers between devices: 2.83 us -> 1.93 us  [body(): heard = lax.ppermute(z, 'leaf', [(i, i ^ 1 << bit) for i in range(n)])]
    ppermute x5, waiting for transfers between devices: 11.6 us -> 12.3 us  [body(): heard = lax.ppermute(z, 'leaf', [(i, i ^ 1 << bit) for i in range(n)])]
  transfers between devices with their start and end apart: 14 -> 14, of which waited for: 10 -> 10; matrix products, arithmetic and copies ran while one was open for 0% -> 0% of each run, Pallas kernels for 21% -> 22%
where the time goes in v5:
time: 56.5 us; the launch traced here: 56.2 us
  waiting for transfers between devices  27.2 us (48%)
  Pallas kernels  17.7 us (31%)
  starting transfers between devices  11.1 us (20%)
    pallas_call x17, Pallas kernels, call(): pl.pallas_call(kernel, out_shape=outs, in_specs=[sm if i in smem else hb...  17.7 us
    ppermute x5, waiting for transfers between devices, body(): heard = lax.ppermute(z, 'leaf', [(i, i ^ 1 << bit) for i in range(n)])  12.3 us
    ppermute x5, waiting for transfers between devices, body(): partner = lax.ppermute(block, 'leaf', [(i, i ^ 1 << bit) for i in range(n)])  7.53 us
    ppermute x5, starting transfers between devices, body(): partner = lax.ppermute(block, 'leaf', [(i, i ^ 1 << bit) for i in range(n)])  4.1 us
    ppermute x1, waiting for transfers between devices, body(): recv_b2 = lax.ppermute(cut_chip(emb, x_tree), 'leaf', pairs(3))  3.83 us
    ppermute x1, waiting for transfers between devices, body(): back = lax.ppermute(back, 'leaf', pairs(1, 3))  3.48 us
    ppermute x1, starting transfers between devices, body(): recv_b2 = lax.ppermute(cut_chip(emb, x_tree), 'leaf', pairs(3))  2.24 us
    ppermute x5, starting transfers between devices, body(): heard = lax.ppermute(z, 'leaf', [(i, i ^ 1 << bit) for i in range(n)])  1.93 us
  transfers between devices with their start and end apart: 14, of which 10 were waited for; matrix products, arithmetic and copies ran while one was open for 0% of the time, Pallas kernels for 22%

profile of v5, /device:TPU:24, one launch (start us, length us, event | category | flops | bytes accessed | tf_op | source)
XLA Modules:
  0.0 56.2 jit_solution(1176591806040670002)
XLA Ops:
  0.0 0.0 copy-start.4
  0.0 3.1 %prep.1 = (bf16[8,768]{1,0:T(8,128)(2,1)S(1)}, bf16[8,768]{1,0:T(8,128)(2,1)S(1)}, bf16[16,768]{1,0:T(8,128)(2,1)S(1)}, bf16[32,768]{1,0:T(8,128)(2,1)S(1)}, bf16[768,2048]{1,0:T(8,128)(2,1)S(1)}) custom-call(s32[30,64]{1,0:T(8,128)} %skel_hbm.1, bf16[768,2048]{1,0:T(8,128)(2,1)} %emb_hbm.1), custom_call_target="tpu_custom_call" | custom-call | tf_op jit(solution)/shard_map/prep/pallas_call | solution.py:51
  3.1 0.4 collective-permute-start
  3.5 0.0 copy-done.1
  3.5 0.0 copy-done.2
  3.5 0.0 copy-done.3
  3.5 0.0 copy-done.4
  3.5 1.9 %tree.1 = (bf16[32,2048]{1,0:T(8,128)(2,1)S(1)}, s32[1,2048]{1,0:T(1,128)S(1)}, f32[1,2048]{1,0:T(1,128)S(1)}, f32[56,128]{1,0:T(8,128)S(1)}) custom-call(s32[1,2048]{1,0:T(1,128)} %order_hbm.1, bf16[32,2048]{1,0:T(8,128)(2,1)} %probes_hbm.1, s32[8,7]{1,0:T(8,128)} %list_hbm.1, s32[1,8]{1,0:T(1,128)} %count_hbm.1, ...), custom_call_target="tpu_custom_call" | custom-call | tf_op jit(solution)/shard_map/tree/pallas_call | solution.py:51
  5.4 2.4 %collective-permute-done.refs_1_ = bf16[8,768]{1,0:T(8,128)(2,1)S(1)} collective-permute-done((bf16[8,768]{1,0:T(8,128)(2,1)S(1)}, bf16[8,768]{1,0:T(8,128)(2,1)S(1)}, u32[]{:S(2)}, u32[]{:S(2)}) %collective-permute-start) | collective-permute-done | bytes 12320 | tf_op jit(solution)/shard_map/ppermute | solution.py:524
  7.8 0.5 collective-permute-start.1
  8.3 0.2 cut.1
  8.5 1.4 %near0.1.refs_4_ = f32[32,2048]{1,0:T(8,128)S(1)} custom-call(f32[56,128]{1,0:T(8,128)S(1)} %get-tuple-element.58.refs_0_.mult_ref, bf16[768,2048]{1,0:T(8,128)(2,1)S(1)} %get-tuple-element.86.emb_ref.refs_1_, bf16[32,2048]{1,0:T(8,128)(2,1)S(1)} %get-tuple-element.79.refs_2_.x_ref, f32[1,2048]{1,0:T(1,128)S(1)} %get-tuple-element.61.refs_3_.hn_ref), custom_call_target="tpu_custom_call" | custom-call | tf_op jit(solution)/shard_map/near0/pallas_call | solution.py:51
  9.9 1.8 %collective-permute-done.1.refs_1_ = bf16[16,768]{1,0:T(8,128)(2,1)S(1)} collective-permute-done((bf16[16,768]{1,0:T(8,128)(2,1)S(1)}, bf16[16,768]{1,0:T(8,128)(2,1)S(1)}, u32[]{:S(2)}, u32[]{:S(2)}) %collective-permute-start.1) | collective-permute-done | bytes 24608 | tf_op jit(solution)/shard_map/ppermute | solution.py:524
  11.7 0.0 collective-permute-start.4
  11.7 1.6 %collective-permute-start.2 = (bf16[48,768]{1,0:T(8,128)(2,1)S(1)}, bf16[48,768]{1,0:T(8,128)(2,1)S(1)}, u32[]{:S(2)}, u32[]{:S(2)}) collective-permute-start(bf16[48,768]{1,0:T(8,128)(2,1)S(1)} %join.5.refs_0_), channel_id=1, source_target_pairs={{0,4},{1,5},{2,6},{3,7},{4,0},{5,1},{6,2},{7,3},{8,12},{9,13},{10,... | collective-permute-start | bytes 221192 | tf_op jit(solution)/shard_map/ppermute | solution.py:524
  13.3 1.4 %near2.1.refs_4_ = f32[32,2048]{1,0:T(8,128)S(1)} custom-call(f32[56,128]{1,0:T(8,128)S(1)} %get-tuple-element.58.refs_0_.mult_ref, bf16[768,2048]{1,0:T(8,128)(2,1)S(1)} %get-tuple-element.86.emb_ref.refs_1_, bf16[32,2048]{1,0:T(8,128)(2,1)S(1)} %get-tuple-element.79.refs_2_.x_ref, f32[1,2048]{1,0:T(1,128)S(1)} %get-tuple-element.61.refs_3_.hn_ref, ...), custom_call_target="tpu_custom_call" | custom-call | tf_op jit(solution)/shard_map/near2/pallas_call | solution.py:51
  14.7 1.7 %collective-permute-done.2.refs_1_ = bf16[48,768]{1,0:T(8,128)(2,1)S(1)} collective-permute-done((bf16[48,768]{1,0:T(8,128)(2,1)S(1)}, bf16[48,768]{1,0:T(8,128)(2,1)S(1)}, u32[]{:S(2)}, u32[]{:S(2)}) %collective-permute-start.2) | collective-permute-done | bytes 73760 | tf_op jit(solution)/shard_map/ppermute | solution.py:524
  16.4 1.6 %collective-permute-start.3 = (bf16[128,768]{1,0:T(8,128)(2,1)S(1)}, bf16[128,768]{1,0:T(8,128)(2,1)S(1)}, u32[]{:S(2)}, u32[]{:S(2)}) collective-permute-start(bf16[128,768]{1,0:T(8,128)(2,1)S(1)} %join.6.refs_0_), channel_id=1, source_target_pairs={{0,2},{1,3},{2,0},{3,1},{4,6},{5,7},{6,4},{7,5},{8,10},{9,11},{10,... | collective-permute-start | bytes 589832 | tf_op jit(solution)/shard_map/ppermute | solution.py:524
  17.9 0.1 cut_chip.2
  18.1 2.2 %collective-permute-start.7 = (bf16[808,512]{1,0:T(8,128)(2,1)S(1)}, bf16[808,512]{1,0:T(8,128)(2,1)S(1)}, u32[]{:S(2)}, u32[]{:S(2)}) collective-permute-start(bf16[808,512]{1,0:T(8,128)(2,1)S(1)} %cut_chip.2), channel_id=1, source_target_pairs={{3,4},{7,8},{11,12},{15,16},{19,20},{23,24},{27,28},{4,3},{8,7},{1... | collective-permute-start | bytes 2482184 | tf_op jit(solution)/shard_map/ppermute | solution.py:537
  20.3 1.8 %near4.1.near_in = f32[32,2048]{1,0:T(8,128)S(1)} custom-call(f32[56,128]{1,0:T(8,128)S(1)} %get-tuple-element.58.refs_0_.mult_ref, bf16[768,2048]{1,0:T(8,128)(2,1)S(1)} %get-tuple-element.86.emb_ref.refs_1_, bf16[32,2048]{1,0:T(8,128)(2,1)S(1)} %get-tuple-element.79.refs_2_.x_ref, f32[1,2048]{1,0:T(1,128)S(1)} %get-tuple-element.61.refs_3_.hn_ref, ...), custom_call_target="tpu_custom_call" | custom-call | tf_op jit(solution)/shard_map/near4/pallas_call | solution.py:51
  22.1 0.0 collective-permute-done.4.src_ref
  22.1 1.6 %edge_core.1.near_in = f32[32,2048]{1,0:T(8,128)S(1)} custom-call(f32[56,128]{1,0:T(8,128)S(1)} %get-tuple-element.58.refs_0_.mult_ref, bf16[768,2048]{1,0:T(8,128)(2,1)S(1)} %get-tuple-element.86.emb_ref.refs_1_, f32[1,2048]{1,0:T(1,128)S(1)} %get-tuple-element.61.refs_3_.hn_ref, bf16[800,768]{1,0:T(8,128)(2,1)S(1)} %collective-permute-done.4.src_ref, ...), custom_call_target="tpu_custom_call" | custom-call | tf_op jit(solution)/shard_map/edge_core/pallas_call | solution.py:51
  23.7 0.0 collective-permute-done.3.refs_1_
  23.8 0.1 collective-permute-start.5
  23.8 1.7 %collective-permute-done.5.other_ref = bf16[256,768]{1,0:T(8,128)(2,1)S(1)} collective-permute-done((bf16[256,768]{1,0:T(8,128)(2,1)S(1)}, bf16[256,768]{1,0:T(8,128)(2,1)S(1)}, u32[]{:S(2)}, u32[]{:S(2)}) %collective-permute-start.5) | collective-permute-done | bytes 393248 | tf_op jit(solution)/shard_map/ppermute | solution.py:524
  25.6 1.7 %own.1 = f32[32,256]{1,0:T(8,128)S(1)} custom-call(bf16[256,768]{1,0:T(8,128)(2,1)S(1)} %join.7.block_ref, bf16[256,768]{1,0:T(8,128)(2,1)S(1)} %collective-permute-done.5.other_ref, s32[1,512]{1,0:T(1,128)S(1)} %multiply_add_fusion.dest_ref, bf16[768,2048]{1,0:T(8,128)(2,1)S(1)} %get-tuple-element.86.emb_ref.refs_1_, ...), custom_call_target="tpu_custom_call" | custom-call | flops 3000000000 | tf_op jit(solution)/shard_map/own/pallas_call | solution.py:51
  27.2 0.2 collective-permute-start.6
  27.4 0.1 cut_chip.3
  27.6 0.9 %collective-permute-start.11 = (bf16[808,512]{1,0:T(8,128)(2,1)S(1)}, bf16[808,512]{1,0:T(8,128)(2,1)S(1)}, u32[]{:S(2)}, u32[]{:S(2)}) collective-permute-start(bf16[808,512]{1,0:T(8,128)(2,1)S(1)} %cut_chip.3), channel_id=1, source_target_pairs={{1,2},{5,6},{9,10},{13,14},{17,18},{21,22},{25,26},{29,30},{2,1},{... | collective-permute-start | bytes 2482184 | tf_op jit(solution)/shard_map/ppermute | solution.py:613
  28.5 1.3 %far.1.far_ref = bf16[256,2048]{1,0:T(8,128)(2,1)S(1)} custom-call(bf16[256,768]{1,0:T(8,128)(2,1)S(1)} %join.7.block_ref, bf16[256,768]{1,0:T(8,128)(2,1)S(1)} %collective-permute-done.5.other_ref, s32[1,512]{1,0:T(1,128)S(1)} %multiply_add_fusion.dest_ref, bf16[768,2048]{1,0:T(8,128)(2,1)S(1)} %get-tuple-element.86.emb_ref.refs_1_, ...), custom_call_target="tpu_custom_call" | custom-call | tf_op jit(solution)/shard_map/far/pallas_call | solution.py:51
  29.8 0.0 copy-start
  29.8 3.8 %collective-permute-done.7.two_ref = bf16[808,512]{1,0:T(8,128)(2,1)S(1)} collective-permute-done((bf16[808,512]{1,0:T(8,128)(2,1)S(1)}, bf16[808,512]{1,0:T(8,128)(2,1)S(1)}, u32[]{:S(2)}, u32[]{:S(2)}) %collective-permute-start.7) | collective-permute-done | bytes 827424 | tf_op jit(solution)/shard_map/ppermute | solution.py:537
  33.6 0.0 collective-permute-done.6
  33.6 0.5 collective-permute-start.8
  34.1 3.5 %collective-permute-done.8 = f32[32,256]{1,0:T(8,128)S(1)} collective-permute-done((f32[32,256]{1,0:T(8,128)S(1)}, f32[32,256]{1,0:T(8,128)S(1)}, u32[]{:S(2)}, u32[]{:S(2)}) %collective-permute-start.8) | collective-permute-done | bytes 32800 | tf_op jit(solution)/shard_map/ppermute | solution.py:608
  37.6 0.4 collective-permute-start.9
  38.0 4.7 %collective-permute-done.9 = f32[32,256]{1,0:T(8,128)S(1)} collective-permute-done((f32[32,256]{1,0:T(8,128)S(1)}, f32[32,256]{1,0:T(8,128)S(1)}, u32[]{:S(2)}, u32[]{:S(2)}) %collective-permute-start.9) | collective-permute-done | bytes 32800 | tf_op jit(solution)/shard_map/ppermute | solution.py:608
  42.7 0.8 %collective-permute-start.10 = (f32[32,256]{1,0:T(8,128)S(1)}, f32[32,256]{1,0:T(8,128)S(1)}, u32[]{:S(2)}, u32[]{:S(2)}) collective-permute-start(f32[32,256]{1,0:T(8,128)S(1)} %select_select_fusion.2), channel_id=1, source_target_pairs={{0,4},{1,5},{2,6},{3,7},{4,0},{5,1},{6,2},{7,3},{8,12},{9,13},{10,... | collective-permute-start | bytes 98312 | tf_op jit(solution)/shard_map/ppermute | solution.py:608
  43.6 0.0 collective-permute-done.11.one_ref
  43.6 1.0 %edge_chip.1 = (f32[32,2048]{1,0:T(8,128)S(1)}, f32[32,512]{1,0:T(8,128)S(1)}) custom-call(f32[56,128]{1,0:T(8,128)S(1)} %get-tuple-element.58.refs_0_.mult_ref, bf16[768,2048]{1,0:T(8,128)(2,1)S(1)} %get-tuple-element.86.emb_ref.refs_1_, f32[1,2048]{1,0:T(1,128)S(1)} %get-tuple-element.61.refs_3_.hn_ref, ...), custom_call_target="tpu_custom_call" | custom-call | tf_op jit(solution)/shard_map/edge_chip/pallas_call | solution.py:51
  44.5 2.2 %collective-permute-done.10 = f32[32,256]{1,0:T(8,128)S(1)} collective-permute-done((f32[32,256]{1,0:T(8,128)S(1)}, f32[32,256]{1,0:T(8,128)S(1)}, u32[]{:S(2)}, u32[]{:S(2)}) %collective-permute-start.10) | collective-permute-done | bytes 32800 | tf_op jit(solution)/shard_map/ppermute | solution.py:608
  46.7 0.1 collective-permute-start.12
  46.8 1.9 %collective-permute-start.13 = (f32[32,512]{1,0:T(8,128)S(1)}, f32[32,512]{1,0:T(8,128)S(1)}, u32[]{:S(2)}, u32[]{:S(2)}) collective-permute-start(f32[32,512]{1,0:T(8,128)S(1)} %get-tuple-element.94), channel_id=1, source_target_pairs={{1,2},{5,6},{9,10},{13,14},{17,18},{21,22},{25,26},{29,30},{3,4},{... | collective-permute-start | bytes 196616 | tf_op jit(solution)/shard_map/ppermute | solution.py:618
  48.7 2.0 %collective-permute-done.12 = f32[32,256]{1,0:T(8,128)S(1)} collective-permute-done((f32[32,256]{1,0:T(8,128)S(1)}, f32[32,256]{1,0:T(8,128)S(1)}, u32[]{:S(2)}, u32[]{:S(2)}) %collective-permute-start.12) | collective-permute-done | bytes 32800 | tf_op jit(solution)/shard_map/ppermute | solution.py:608
  50.7 3.5 %collective-permute-done.13.back_ref = f32[32,512]{1,0:T(8,128)S(1)} collective-permute-done((f32[32,512]{1,0:T(8,128)S(1)}, f32[32,512]{1,0:T(8,128)S(1)}, u32[]{:S(2)}, u32[]{:S(2)}) %collective-permute-start.13) | collective-permute-done | bytes 65568 | tf_op jit(solution)/shard_map/ppermute | solution.py:618
  54.2 0.0 copy-done
  54.2 2.0 %last.1 = f32[32,2048]{1,0:T(8,128)} custom-call(f32[32,256]{1,0:T(8,128)S(1)} %select_select_fusion.z_ref, f32[30,64,64]{2,1,0:T(8,128)S(1)} %copy-done, bf16[256,2048]{1,0:T(8,128)(2,1)S(1)} %far.1.far_ref, f32[32,512]{1,0:T(8,128)S(1)} %collective-permute-done.13.back_ref, s32[1,2048]{1,0:T(1,128)S(1)} %get-tuple-element.95.inv_ref, ...), custom_call_target="tpu_custom_call" | custom-call | tf_op jit(solution)/shard_map/last/pallas_call | solution.py:51
  (18 shorter events, 0.1 us)
Async XLA Ops:
  0.0 3.5 %copy-start.1 = (s32[1,512]{1,0:T(1,128)S(1)}, s32[1,512]{1,0:T(1,128)}, u32[]{:S(2)}) copy-start(s32[1,512]{1,0:T(1,128)} %constant.55) | copy-start | bytes 6148
  0.0 3.5 %copy-start.2 = (s32[1,512]{1,0:T(1,128)S(1)}, s32[1,512]{1,0:T(1,128)}, u32[]{:S(2)}) copy-start(s32[1,512]{1,0:T(1,128)} %constant.56) | copy-start | bytes 6148
  0.0 3.5 %copy-start.3 = (s32[1,512]{1,0:T(1,128)S(1)}, s32[1,512]{1,0:T(1,128)}, u32[]{:S(2)}) copy-start(s32[1,512]{1,0:T(1,128)} %constant.57) | copy-start | bytes 6148
  0.0 3.5 %copy-start.4 = (s32[1,512]{1,0:T(1,128)S(1)}, s32[1,512]{1,0:T(1,128)}, u32[]{:S(2)}) copy-start(s32[1,512]{1,0:T(1,128)} %constant.58) | copy-start | bytes 6148
  3.1 4.7 %collective-permute-start = (bf16[8,768]{1,0:T(8,128)(2,1)S(1)}, bf16[8,768]{1,0:T(8,128)(2,1)S(1)}, u32[]{:S(2)}, u32[]{:S(2)}) collective-permute-start(bf16[8,768]{1,0:T(8,128)(2,1)S(1)} %get-tuple-element.51.refs_0_), channel_id=1, source_target_pairs={{0,16},{1,17},{2,18},{3,19},{4,20},{5,21},{6,22},{7,23},{8,24},{9,... | collective-permute-start | bytes 36872 | tf_op jit(solution)/shard_map/ppermute | solution.py:524
  7.8 3.9 %collective-permute-start.1 = (bf16[16,768]{1,0:T(8,128)(2,1)S(1)}, bf16[16,768]{1,0:T(8,128)(2,1)S(1)}, u32[]{:S(2)}, u32[]{:S(2)}) collective-permute-start(bf16[16,768]{1,0:T(8,128)(2,1)S(1)} %join.4.refs_0_), channel_id=1, source_target_pairs={{0,8},{1,9},{2,10},{3,11},{4,12},{5,13},{6,14},{7,15},{8,0},{9,1},... | collective-permute-start | bytes 73736 | tf_op jit(solution)/shard_map/ppermute | solution.py:524
  11.7 10.4 %collective-permute-start.4 = (bf16[800,768]{1,0:T(8,128)(2,1)S(1)}, bf16[800,768]{1,0:T(8,128)(2,1)S(1)}, u32[]{:S(2)}, u32[]{:S(2)}) collective-permute-start(bf16[800,768]{1,0:T(8,128)(2,1)S(1)} %cut.1), channel_id=1, source_target_pairs={{0,1},{1,0},{2,3},{3,2},{4,5},{5,4},{6,7},{7,6},{8,9},{9,8},{10,11... | collective-permute-start | bytes 3686408 | tf_op jit(solution)/shard_map/ppermute | solution.py:532
  11.7 4.7 %collective-permute-start.2 = (bf16[48,768]{1,0:T(8,128)(2,1)S(1)}, bf16[48,768]{1,0:T(8,128)(2,1)S(1)}, u32[]{:S(2)}, u32[]{:S(2)}) collective-permute-start(bf16[48,768]{1,0:T(8,128)(2,1)S(1)} %join.5.refs_0_), channel_id=1, source_target_pairs={{0,4},{1,5},{2,6},{3,7},{4,0},{5,1},{6,2},{7,3},{8,12},{9,13},{10,... | collective-permute-start | bytes 221192 | tf_op jit(solution)/shard_map/ppermute | solution.py:524
  16.4 7.3 %collective-permute-start.3 = (bf16[128,768]{1,0:T(8,128)(2,1)S(1)}, bf16[128,768]{1,0:T(8,128)(2,1)S(1)}, u32[]{:S(2)}, u32[]{:S(2)}) collective-permute-start(bf16[128,768]{1,0:T(8,128)(2,1)S(1)} %join.6.refs_0_), channel_id=1, source_target_pairs={{0,2},{1,3},{2,0},{3,1},{4,6},{5,7},{6,4},{7,5},{8,10},{9,11},{10,... | collective-permute-start | bytes 589832 | tf_op jit(solution)/shard_map/ppermute | solution.py:524
  18.1 15.5 %collective-permute-start.7 = (bf16[808,512]{1,0:T(8,128)(2,1)S(1)}, bf16[808,512]{1,0:T(8,128)(2,1)S(1)}, u32[]{:S(2)}, u32[]{:S(2)}) collective-permute-start(bf16[808,512]{1,0:T(8,128)(2,1)S(1)} %cut_chip.2), channel_id=1, source_target_pairs={{3,4},{7,8},{11,12},{15,16},{19,20},{23,24},{27,28},{4,3},{8,7},{1... | collective-permute-start | bytes 2482184 | tf_op jit(solution)/shard_map/ppermute | solution.py:537
  23.8 1.8 %collective-permute-start.5 = (bf16[256,768]{1,0:T(8,128)(2,1)S(1)}, bf16[256,768]{1,0:T(8,128)(2,1)S(1)}, u32[]{:S(2)}, u32[]{:S(2)}) collective-permute-start(bf16[256,768]{1,0:T(8,128)(2,1)S(1)} %join.7.block_ref), channel_id=1, source_target_pairs={{0,1},{1,0},{2,3},{3,2},{4,5},{5,4},{6,7},{7,6},{8,9},{9,8},{10,11... | collective-permute-start | bytes 1179656 | tf_op jit(solution)/shard_map/ppermute | solution.py:524
  27.2 6.4 %collective-permute-start.6 = (f32[32,256]{1,0:T(8,128)S(1)}, f32[32,256]{1,0:T(8,128)S(1)}, u32[]{:S(2)}, u32[]{:S(2)}) collective-permute-start(f32[32,256]{1,0:T(8,128)S(1)} %own.1), channel_id=1, source_target_pairs={{0,1},{1,0},{2,3},{3,2},{4,5},{5,4},{6,7},{7,6},{8,9},{9,8},{10,11... | collective-permute-start | bytes 98312 | tf_op jit(solution)/shard_map/ppermute | solution.py:608
  27.6 16.0 %collective-permute-start.11 = (bf16[808,512]{1,0:T(8,128)(2,1)S(1)}, bf16[808,512]{1,0:T(8,128)(2,1)S(1)}, u32[]{:S(2)}, u32[]{:S(2)}) collective-permute-start(bf16[808,512]{1,0:T(8,128)(2,1)S(1)} %cut_chip.3), channel_id=1, source_target_pairs={{1,2},{5,6},{9,10},{13,14},{17,18},{21,22},{25,26},{29,30},{2,1},{... | collective-permute-start | bytes 2482184 | tf_op jit(solution)/shard_map/ppermute | solution.py:613
  29.8 24.4 %copy-start = (f32[30,64,64]{2,1,0:T(8,128)S(1)}, f32[30,64,64]{2,1,0:T(8,128)}, u32[]{:S(2)}) copy-start(f32[30,64,64]{2,1,0:T(8,128)} %core_ref.1) | copy-start | bytes 1474564
  33.6 4.0 %collective-permute-start.8 = (f32[32,256]{1,0:T(8,128)S(1)}, f32[32,256]{1,0:T(8,128)S(1)}, u32[]{:S(2)}, u32[]{:S(2)}) collective-permute-start(f32[32,256]{1,0:T(8,128)S(1)} %select_select_fusion.4), channel_id=1, source_target_pairs={{0,8},{1,9},{2,10},{3,11},{4,12},{5,13},{6,14},{7,15},{8,0},{9,1},... | collective-permute-start | bytes 98312 | tf_op jit(solution)/shard_map/ppermute | solution.py:608
  37.6 5.1 %collective-permute-start.9 = (f32[32,256]{1,0:T(8,128)S(1)}, f32[32,256]{1,0:T(8,128)S(1)}, u32[]{:S(2)}, u32[]{:S(2)}) collective-permute-start(f32[32,256]{1,0:T(8,128)S(1)} %select_select_fusion.3), channel_id=1, source_target_pairs={{0,16},{1,17},{2,18},{3,19},{4,20},{5,21},{6,22},{7,23},{8,24},{9,... | collective-permute-start | bytes 98312 | tf_op jit(solution)/shard_map/ppermute | solution.py:608
  42.7 4.0 %collective-permute-start.10 = (f32[32,256]{1,0:T(8,128)S(1)}, f32[32,256]{1,0:T(8,128)S(1)}, u32[]{:S(2)}, u32[]{:S(2)}) collective-permute-start(f32[32,256]{1,0:T(8,128)S(1)} %select_select_fusion.2), channel_id=1, source_target_pairs={{0,4},{1,5},{2,6},{3,7},{4,0},{5,1},{6,2},{7,3},{8,12},{9,13},{10,... | collective-permute-start | bytes 98312 | tf_op jit(solution)/shard_map/ppermute | solution.py:608
  46.7 4.0 %collective-permute-start.12 = (f32[32,256]{1,0:T(8,128)S(1)}, f32[32,256]{1,0:T(8,128)S(1)}, u32[]{:S(2)}, u32[]{:S(2)}) collective-permute-start(f32[32,256]{1,0:T(8,128)S(1)} %select_select_fusion.1), channel_id=1, source_target_pairs={{0,2},{1,3},{2,0},{3,1},{4,6},{5,7},{6,4},{7,5},{8,10},{9,11},{10,... | collective-permute-start | bytes 98312 | tf_op jit(solution)/shard_map/ppermute | solution.py:608
  46.8 7.4 %collective-permute-start.13 = (f32[32,512]{1,0:T(8,128)S(1)}, f32[32,512]{1,0:T(8,128)S(1)}, u32[]{:S(2)}, u32[]{:S(2)}) collective-permute-start(f32[32,512]{1,0:T(8,128)S(1)} %get-tuple-element.94), channel_id=1, source_target_pairs={{1,2},{5,6},{9,10},{13,14},{17,18},{21,22},{25,26},{29,30},{3,4},{... | collective-permute-start | bytes 196616 | tf_op jit(solution)/shard_map/ppermute | solution.py:618

commit v6 on v5

--- a/solution.py
+++ b/solution.py
@@ -267,7 +267,7 @@
             y = dot(stack, hot[:, sl])
             x = jnp.zeros((cols, LEAF), F32)
             for h in range(groups):
-                x = x + jnp.where(high[:, sl] == h, y[h * cols : (h + 1) * cols], 0.0)
+                x = jnp.where(high[:, sl] == h, y[h * cols : (h + 1) * cols], x)
             x_ref[:, sl] = x.astype(BF16)
 
         k = lax.broadcasted_iota(jnp.int32, (8, points), 1)
@@ -525,13 +525,12 @@
         if stage == 0:
             partner, x_tree, dest = after((partner, x_tree, dest))
         if stage == 1:
+            recv_a = lax.ppermute(cut_core(emb, x_tree), "leaf", pairs_a)
             near = near_part((0, 1), emb, x_tree, hn)
-            send_a = cut_core(emb, x_tree)
-            partner, near, send_a = after((partner, near, send_a))
+            partner, near = after((partner, near))
         if stage == 2:
-            recv_a = lax.ppermute(send_a, "leaf", pairs_a)
             near = near_part((2, 3), emb, x_tree, hn, near)
-            partner, near = after((partner, near))
+            partner, near, recv_a = after((partner, near, recv_a))
         if stage == 3:
             near = near_part(tuple(range(4, leaves)), emb, x_tree, hn, near)
             recv_b2 = lax.ppermute(cut_chip(emb, x_tree), "leaf", pairs(3))
@@ -661,7 +660,7 @@
             y = dot(stack, jnp.concatenate([hot[:, sl]] * 2, axis=0))
             out = jnp.zeros((cols, LEAF), F32)
             for h in range(groups):
-                out = out + jnp.where(high[:, sl] == h, y[h * cols : (h + 1) * cols], 0.0)
+                out = jnp.where(high[:, sl] == h, y[h * cols : (h + 1) * cols], out)
             out_ref[:, sl] = out
 
     return call(

time: 56.5 us -> 56.4 us (level)
  no operation moved by 1% of the time
where the time goes in v6:
time: 56.4 us; the launch traced here: 56.2 us
  waiting for transfers between devices  27.5 us (49%)
  Pallas kernels  17.6 us (31%)
  starting transfers between devices  10.8 us (19%)
    pallas_call x17, Pallas kernels, call(): pl.pallas_call(kernel, out_shape=outs, in_specs=[sm if i in smem else hb...  17.6 us
    ppermute x5, waiting for transfers between devices, body(): heard = lax.ppermute(z, 'leaf', [(i, i ^ 1 << bit) for i in range(n)])  12.3 us
    ppermute x5, waiting for transfers between devices, body(): partner = lax.ppermute(block, 'leaf', [(i, i ^ 1 << bit) for i in range(n)])  7.5 us
    ppermute x1, waiting for transfers between devices, body(): recv_b2 = lax.ppermute(cut_chip(emb, x_tree), 'leaf', pairs(3))  4.15 us
    ppermute x5, starting transfers between devices, body(): partner = lax.ppermute(block, 'leaf', [(i, i ^ 1 << bit) for i in range(n)])  4.04 us
    ppermute x1, waiting for transfers between devices, body(): back = lax.ppermute(back, 'leaf', pairs(1, 3))  3.48 us
    ppermute x5, starting transfers between devices, body(): heard = lax.ppermute(z, 'leaf', [(i, i ^ 1 << bit) for i in range(n)])  1.93 us
    ppermute x1, starting transfers between devices, body(): recv_b2 = lax.ppermute(cut_chip(emb, x_tree), 'leaf', pairs(3))  1.92 us
  transfers between devices with their start and end apart: 14, of which 10 were waited for; matrix products, arithmetic and copies ran while one was open for 0% of the time, Pallas kernels for 22%

profile of v6, /device:TPU:24, one launch (start us, length us, event | category | flops | bytes accessed | tf_op | source)
XLA Modules:
  0.0 56.2 jit_solution(10923732334796442997)
XLA Ops:
  0.0 0.0 copy-start.4
  0.0 3.1 %prep.1 = (bf16[8,768]{1,0:T(8,128)(2,1)S(1)}, bf16[8,768]{1,0:T(8,128)(2,1)S(1)}, bf16[16,768]{1,0:T(8,128)(2,1)S(1)}, bf16[32,768]{1,0:T(8,128)(2,1)S(1)}, bf16[768,2048]{1,0:T(8,128)(2,1)S(1)}) custom-call(s32[30,64]{1,0:T(8,128)} %skel_hbm.1, bf16[768,2048]{1,0:T(8,128)(2,1)} %emb_hbm.1), custom_call_target="tpu_custom_call" | custom-call | tf_op jit(solution)/shard_map/prep/pallas_call | solution.py:51
  3.1 0.4 collective-permute-start
  3.5 0.0 copy-done.1
  3.5 0.0 copy-done.2
  3.5 0.0 copy-done.3
  3.5 0.0 copy-done.4
  3.5 1.9 %tree.1 = (bf16[32,2048]{1,0:T(8,128)(2,1)S(1)}, s32[1,2048]{1,0:T(1,128)S(1)}, f32[1,2048]{1,0:T(1,128)S(1)}, f32[56,128]{1,0:T(8,128)S(1)}) custom-call(s32[1,2048]{1,0:T(1,128)} %order_hbm.1, bf16[32,2048]{1,0:T(8,128)(2,1)} %probes_hbm.1, s32[8,7]{1,0:T(8,128)} %list_hbm.1, s32[1,8]{1,0:T(1,128)} %count_hbm.1, ...), custom_call_target="tpu_custom_call" | custom-call | tf_op jit(solution)/shard_map/tree/pallas_call | solution.py:51
  5.4 2.4 %collective-permute-done.refs_1_ = bf16[8,768]{1,0:T(8,128)(2,1)S(1)} collective-permute-done((bf16[8,768]{1,0:T(8,128)(2,1)S(1)}, bf16[8,768]{1,0:T(8,128)(2,1)S(1)}, u32[]{:S(2)}, u32[]{:S(2)}) %collective-permute-start) | collective-permute-done | bytes 12320 | tf_op jit(solution)/shard_map/ppermute | solution.py:524
  7.8 0.2 cut.1
  8.0 0.1 collective-permute-start.3
  8.1 0.5 collective-permute-start.1
  8.6 1.4 %near0.1.refs_4_ = f32[32,2048]{1,0:T(8,128)S(1)} custom-call(f32[56,128]{1,0:T(8,128)S(1)} %get-tuple-element.58.refs_0_.mult_ref, bf16[768,2048]{1,0:T(8,128)(2,1)S(1)} %get-tuple-element.86.emb_ref.refs_1_, bf16[32,2048]{1,0:T(8,128)(2,1)S(1)} %get-tuple-element.79.refs_2_.x_ref, f32[1,2048]{1,0:T(1,128)S(1)} %get-tuple-element.61.refs_3_.hn_ref), custom_call_target="tpu_custom_call" | custom-call | tf_op jit(solution)/shard_map/near0/pallas_call | solution.py:51
  10.0 2.0 %collective-permute-done.1.refs_1_ = bf16[16,768]{1,0:T(8,128)(2,1)S(1)} collective-permute-done((bf16[16,768]{1,0:T(8,128)(2,1)S(1)}, bf16[16,768]{1,0:T(8,128)(2,1)S(1)}, u32[]{:S(2)}, u32[]{:S(2)}) %collective-permute-start.1) | collective-permute-done | bytes 24608 | tf_op jit(solution)/shard_map/ppermute | solution.py:524
  12.0 1.5 %collective-permute-start.2 = (bf16[48,768]{1,0:T(8,128)(2,1)S(1)}, bf16[48,768]{1,0:T(8,128)(2,1)S(1)}, u32[]{:S(2)}, u32[]{:S(2)}) collective-permute-start(bf16[48,768]{1,0:T(8,128)(2,1)S(1)} %join.5.refs_0_), channel_id=1, source_target_pairs={{0,4},{1,5},{2,6},{3,7},{4,0},{5,1},{6,2},{7,3},{8,12},{9,13},{10,... | collective-permute-start | bytes 221192 | tf_op jit(solution)/shard_map/ppermute | solution.py:524
  13.5 1.4 %near2.1.refs_4_ = f32[32,2048]{1,0:T(8,128)S(1)} custom-call(f32[56,128]{1,0:T(8,128)S(1)} %get-tuple-element.58.refs_0_.mult_ref, bf16[768,2048]{1,0:T(8,128)(2,1)S(1)} %get-tuple-element.86.emb_ref.refs_1_, bf16[32,2048]{1,0:T(8,128)(2,1)S(1)} %get-tuple-element.79.refs_2_.x_ref, f32[1,2048]{1,0:T(1,128)S(1)} %get-tuple-element.61.refs_3_.hn_ref, ...), custom_call_target="tpu_custom_call" | custom-call | tf_op jit(solution)/shard_map/near2/pallas_call | solution.py:51
  14.9 1.4 %collective-permute-done.2.refs_1_ = bf16[48,768]{1,0:T(8,128)(2,1)S(1)} collective-permute-done((bf16[48,768]{1,0:T(8,128)(2,1)S(1)}, bf16[48,768]{1,0:T(8,128)(2,1)S(1)}, u32[]{:S(2)}, u32[]{:S(2)}) %collective-permute-start.2) | collective-permute-done | bytes 73760 | tf_op jit(solution)/shard_map/ppermute | solution.py:524
  16.3 0.0 collective-permute-done.3.src_ref
  16.3 1.6 %collective-permute-start.4 = (bf16[128,768]{1,0:T(8,128)(2,1)S(1)}, bf16[128,768]{1,0:T(8,128)(2,1)S(1)}, u32[]{:S(2)}, u32[]{:S(2)}) collective-permute-start(bf16[128,768]{1,0:T(8,128)(2,1)S(1)} %join.6.refs_0_), channel_id=1, source_target_pairs={{0,2},{1,3},{2,0},{3,1},{4,6},{5,7},{6,4},{7,5},{8,10},{9,11},{10,... | collective-permute-start | bytes 589832 | tf_op jit(solution)/shard_map/ppermute | solution.py:524
  17.9 0.1 cut_chip.2
  18.0 1.9 %collective-permute-start.7 = (bf16[808,512]{1,0:T(8,128)(2,1)S(1)}, bf16[808,512]{1,0:T(8,128)(2,1)S(1)}, u32[]{:S(2)}, u32[]{:S(2)}) collective-permute-start(bf16[808,512]{1,0:T(8,128)(2,1)S(1)} %cut_chip.2), channel_id=1, source_target_pairs={{3,4},{7,8},{11,12},{15,16},{19,20},{23,24},{27,28},{4,3},{8,7},{1... | collective-permute-start | bytes 2482184 | tf_op jit(solution)/shard_map/ppermute | solution.py:536
  20.0 1.8 %near4.1.near_in = f32[32,2048]{1,0:T(8,128)S(1)} custom-call(f32[56,128]{1,0:T(8,128)S(1)} %get-tuple-element.58.refs_0_.mult_ref, bf16[768,2048]{1,0:T(8,128)(2,1)S(1)} %get-tuple-element.86.emb_ref.refs_1_, bf16[32,2048]{1,0:T(8,128)(2,1)S(1)} %get-tuple-element.79.refs_2_.x_ref, f32[1,2048]{1,0:T(1,128)S(1)} %get-tuple-element.61.refs_3_.hn_ref, ...), custom_call_target="tpu_custom_call" | custom-call | tf_op jit(solution)/shard_map/near4/pallas_call | solution.py:51
  21.7 1.6 %edge_core.1.near_in = f32[32,2048]{1,0:T(8,128)S(1)} custom-call(f32[56,128]{1,0:T(8,128)S(1)} %get-tuple-element.58.refs_0_.mult_ref, bf16[768,2048]{1,0:T(8,128)(2,1)S(1)} %get-tuple-element.86.emb_ref.refs_1_, f32[1,2048]{1,0:T(1,128)S(1)} %get-tuple-element.61.refs_3_.hn_ref, bf16[800,768]{1,0:T(8,128)(2,1)S(1)} %collective-permute-done.3.src_ref, ...), custom_call_target="tpu_custom_call" | custom-call | tf_op jit(solution)/shard_map/edge_core/pallas_call | solution.py:51
  23.4 0.0 collective-permute-done.4.refs_1_
  23.4 0.1 collective-permute-start.5
  23.5 1.7 %collective-permute-done.5.other_ref = bf16[256,768]{1,0:T(8,128)(2,1)S(1)} collective-permute-done((bf16[256,768]{1,0:T(8,128)(2,1)S(1)}, bf16[256,768]{1,0:T(8,128)(2,1)S(1)}, u32[]{:S(2)}, u32[]{:S(2)}) %collective-permute-start.5) | collective-permute-done | bytes 393248 | tf_op jit(solution)/shard_map/ppermute | solution.py:524
  25.2 1.7 %own.1 = f32[32,256]{1,0:T(8,128)S(1)} custom-call(bf16[256,768]{1,0:T(8,128)(2,1)S(1)} %join.7.block_ref, bf16[256,768]{1,0:T(8,128)(2,1)S(1)} %collective-permute-done.5.other_ref, s32[1,512]{1,0:T(1,128)S(1)} %multiply_add_fusion.dest_ref, bf16[768,2048]{1,0:T(8,128)(2,1)S(1)} %get-tuple-element.86.emb_ref.refs_1_, ...), custom_call_target="tpu_custom_call" | custom-call | flops 3000000000 | tf_op jit(solution)/shard_map/own/pallas_call | solution.py:51
  26.9 0.2 collective-permute-start.6
  27.0 0.1 cut_chip.3
  27.2 0.9 %collective-permute-start.11 = (bf16[808,512]{1,0:T(8,128)(2,1)S(1)}, bf16[808,512]{1,0:T(8,128)(2,1)S(1)}, u32[]{:S(2)}, u32[]{:S(2)}) collective-permute-start(bf16[808,512]{1,0:T(8,128)(2,1)S(1)} %cut_chip.3), channel_id=1, source_target_pairs={{1,2},{5,6},{9,10},{13,14},{17,18},{21,22},{25,26},{29,30},{2,1},{... | collective-permute-start | bytes 2482184 | tf_op jit(solution)/shard_map/ppermute | solution.py:612
  28.1 1.3 %far.1.far_ref = bf16[256,2048]{1,0:T(8,128)(2,1)S(1)} custom-call(bf16[256,768]{1,0:T(8,128)(2,1)S(1)} %join.7.block_ref, bf16[256,768]{1,0:T(8,128)(2,1)S(1)} %collective-permute-done.5.other_ref, s32[1,512]{1,0:T(1,128)S(1)} %multiply_add_fusion.dest_ref, bf16[768,2048]{1,0:T(8,128)(2,1)S(1)} %get-tuple-element.86.emb_ref.refs_1_, ...), custom_call_target="tpu_custom_call" | custom-call | tf_op jit(solution)/shard_map/far/pallas_call | solution.py:51
  29.4 0.0 copy-start
  29.4 0.0 collective-permute-done.6
  29.4 4.2 %collective-permute-done.7.two_ref = bf16[808,512]{1,0:T(8,128)(2,1)S(1)} collective-permute-done((bf16[808,512]{1,0:T(8,128)(2,1)S(1)}, bf16[808,512]{1,0:T(8,128)(2,1)S(1)}, u32[]{:S(2)}, u32[]{:S(2)}) %collective-permute-start.7) | collective-permute-done | bytes 827424 | tf_op jit(solution)/shard_map/ppermute | solution.py:536
  33.6 0.5 collective-permute-start.8
  34.1 3.5 %collective-permute-done.8 = f32[32,256]{1,0:T(8,128)S(1)} collective-permute-done((f32[32,256]{1,0:T(8,128)S(1)}, f32[32,256]{1,0:T(8,128)S(1)}, u32[]{:S(2)}, u32[]{:S(2)}) %collective-permute-start.8) | collective-permute-done | bytes 32800 | tf_op jit(solution)/shard_map/ppermute | solution.py:607
  37.6 0.4 collective-permute-start.9
  38.0 4.7 %collective-permute-done.9 = f32[32,256]{1,0:T(8,128)S(1)} collective-permute-done((f32[32,256]{1,0:T(8,128)S(1)}, f32[32,256]{1,0:T(8,128)S(1)}, u32[]{:S(2)}, u32[]{:S(2)}) %collective-permute-start.9) | collective-permute-done | bytes 32800 | tf_op jit(solution)/shard_map/ppermute | solution.py:607
  42.7 0.8 %collective-permute-start.10 = (f32[32,256]{1,0:T(8,128)S(1)}, f32[32,256]{1,0:T(8,128)S(1)}, u32[]{:S(2)}, u32[]{:S(2)}) collective-permute-start(f32[32,256]{1,0:T(8,128)S(1)} %select_select_fusion.2), channel_id=1, source_target_pairs={{0,4},{1,5},{2,6},{3,7},{4,0},{5,1},{6,2},{7,3},{8,12},{9,13},{10,... | collective-permute-start | bytes 98312 | tf_op jit(solution)/shard_map/ppermute | solution.py:607
  43.5 0.0 collective-permute-done.11.one_ref
  43.5 1.0 %edge_chip.1 = (f32[32,2048]{1,0:T(8,128)S(1)}, f32[32,512]{1,0:T(8,128)S(1)}) custom-call(f32[56,128]{1,0:T(8,128)S(1)} %get-tuple-element.58.refs_0_.mult_ref, bf16[768,2048]{1,0:T(8,128)(2,1)S(1)} %get-tuple-element.86.emb_ref.refs_1_, f32[1,2048]{1,0:T(1,128)S(1)} %get-tuple-element.61.refs_3_.hn_ref, ...), custom_call_target="tpu_custom_call" | custom-call | tf_op jit(solution)/shard_map/edge_chip/pallas_call | solution.py:51
  44.5 2.2 %collective-permute-done.10 = f32[32,256]{1,0:T(8,128)S(1)} collective-permute-done((f32[32,256]{1,0:T(8,128)S(1)}, f32[32,256]{1,0:T(8,128)S(1)}, u32[]{:S(2)}, u32[]{:S(2)}) %collective-permute-start.10) | collective-permute-done | bytes 32800 | tf_op jit(solution)/shard_map/ppermute | solution.py:607
  46.7 0.1 collective-permute-start.12
  46.8 1.9 %collective-permute-start.13 = (f32[32,512]{1,0:T(8,128)S(1)}, f32[32,512]{1,0:T(8,128)S(1)}, u32[]{:S(2)}, u32[]{:S(2)}) collective-permute-start(f32[32,512]{1,0:T(8,128)S(1)} %get-tuple-element.94), channel_id=1, source_target_pairs={{1,2},{5,6},{9,10},{13,14},{17,18},{21,22},{25,26},{29,30},{3,4},{... | collective-permute-start | bytes 196616 | tf_op jit(solution)/shard_map/ppermute | solution.py:617
  48.7 2.0 %collective-permute-done.12 = f32[32,256]{1,0:T(8,128)S(1)} collective-permute-done((f32[32,256]{1,0:T(8,128)S(1)}, f32[32,256]{1,0:T(8,128)S(1)}, u32[]{:S(2)}, u32[]{:S(2)}) %collective-permute-start.12) | collective-permute-done | bytes 32800 | tf_op jit(solution)/shard_map/ppermute | solution.py:607
  50.7 3.5 %collective-permute-done.13.back_ref = f32[32,512]{1,0:T(8,128)S(1)} collective-permute-done((f32[32,512]{1,0:T(8,128)S(1)}, f32[32,512]{1,0:T(8,128)S(1)}, u32[]{:S(2)}, u32[]{:S(2)}) %collective-permute-start.13) | collective-permute-done | bytes 65568 | tf_op jit(solution)/shard_map/ppermute | solution.py:617
  54.2 0.0 copy-done
  54.2 2.0 %last.1 = f32[32,2048]{1,0:T(8,128)} custom-call(f32[32,256]{1,0:T(8,128)S(1)} %select_select_fusion.z_ref, f32[30,64,64]{2,1,0:T(8,128)S(1)} %copy-done, bf16[256,2048]{1,0:T(8,128)(2,1)S(1)} %far.1.far_ref, f32[32,512]{1,0:T(8,128)S(1)} %collective-permute-done.13.back_ref, s32[1,2048]{1,0:T(1,128)S(1)} %get-tuple-element.95.inv_ref, ...), custom_call_target="tpu_custom_call" | custom-call | tf_op jit(solution)/shard_map/last/pallas_call | solution.py:51
  (18 shorter events, 0.1 us)
Async XLA Ops:
  0.0 3.5 %copy-start.1 = (s32[1,512]{1,0:T(1,128)S(1)}, s32[1,512]{1,0:T(1,128)}, u32[]{:S(2)}) copy-start(s32[1,512]{1,0:T(1,128)} %constant.55) | copy-start | bytes 6148
  0.0 3.5 %copy-start.2 = (s32[1,512]{1,0:T(1,128)S(1)}, s32[1,512]{1,0:T(1,128)}, u32[]{:S(2)}) copy-start(s32[1,512]{1,0:T(1,128)} %constant.56) | copy-start | bytes 6148
  0.0 3.5 %copy-start.3 = (s32[1,512]{1,0:T(1,128)S(1)}, s32[1,512]{1,0:T(1,128)}, u32[]{:S(2)}) copy-start(s32[1,512]{1,0:T(1,128)} %constant.57) | copy-start | bytes 6148
  0.0 3.5 %copy-start.4 = (s32[1,512]{1,0:T(1,128)S(1)}, s32[1,512]{1,0:T(1,128)}, u32[]{:S(2)}) copy-start(s32[1,512]{1,0:T(1,128)} %constant.58) | copy-start | bytes 6148
  3.1 4.7 %collective-permute-start = (bf16[8,768]{1,0:T(8,128)(2,1)S(1)}, bf16[8,768]{1,0:T(8,128)(2,1)S(1)}, u32[]{:S(2)}, u32[]{:S(2)}) collective-permute-start(bf16[8,768]{1,0:T(8,128)(2,1)S(1)} %get-tuple-element.51.refs_0_), channel_id=1, source_target_pairs={{0,16},{1,17},{2,18},{3,19},{4,20},{5,21},{6,22},{7,23},{8,24},{9,... | collective-permute-start | bytes 36872 | tf_op jit(solution)/shard_map/ppermute | solution.py:524
  8.0 8.3 %collective-permute-start.3 = (bf16[800,768]{1,0:T(8,128)(2,1)S(1)}, bf16[800,768]{1,0:T(8,128)(2,1)S(1)}, u32[]{:S(2)}, u32[]{:S(2)}) collective-permute-start(bf16[800,768]{1,0:T(8,128)(2,1)S(1)} %cut.1), channel_id=1, source_target_pairs={{0,1},{1,0},{2,3},{3,2},{4,5},{5,4},{6,7},{7,6},{8,9},{9,8},{10,11... | collective-permute-start | bytes 3686408 | tf_op jit(solution)/shard_map/ppermute | solution.py:528
  8.1 3.9 %collective-permute-start.1 = (bf16[16,768]{1,0:T(8,128)(2,1)S(1)}, bf16[16,768]{1,0:T(8,128)(2,1)S(1)}, u32[]{:S(2)}, u32[]{:S(2)}) collective-permute-start(bf16[16,768]{1,0:T(8,128)(2,1)S(1)} %join.4.refs_0_), channel_id=1, source_target_pairs={{0,8},{1,9},{2,10},{3,11},{4,12},{5,13},{6,14},{7,15},{8,0},{9,1},... | collective-permute-start | bytes 73736 | tf_op jit(solution)/shard_map/ppermute | solution.py:524
  12.0 4.4 %collective-permute-start.2 = (bf16[48,768]{1,0:T(8,128)(2,1)S(1)}, bf16[48,768]{1,0:T(8,128)(2,1)S(1)}, u32[]{:S(2)}, u32[]{:S(2)}) collective-permute-start(bf16[48,768]{1,0:T(8,128)(2,1)S(1)} %join.5.refs_0_), channel_id=1, source_target_pairs={{0,4},{1,5},{2,6},{3,7},{4,0},{5,1},{6,2},{7,3},{8,12},{9,13},{10,... | collective-permute-start | bytes 221192 | tf_op jit(solution)/shard_map/ppermute | solution.py:524
  16.3 7.0 %collective-permute-start.4 = (bf16[128,768]{1,0:T(8,128)(2,1)S(1)}, bf16[128,768]{1,0:T(8,128)(2,1)S(1)}, u32[]{:S(2)}, u32[]{:S(2)}) collective-permute-start(bf16[128,768]{1,0:T(8,128)(2,1)S(1)} %join.6.refs_0_), channel_id=1, source_target_pairs={{0,2},{1,3},{2,0},{3,1},{4,6},{5,7},{6,4},{7,5},{8,10},{9,11},{10,... | collective-permute-start | bytes 589832 | tf_op jit(solution)/shard_map/ppermute | solution.py:524
  18.0 15.5 %collective-permute-start.7 = (bf16[808,512]{1,0:T(8,128)(2,1)S(1)}, bf16[808,512]{1,0:T(8,128)(2,1)S(1)}, u32[]{:S(2)}, u32[]{:S(2)}) collective-permute-start(bf16[808,512]{1,0:T(8,128)(2,1)S(1)} %cut_chip.2), channel_id=1, source_target_pairs={{3,4},{7,8},{11,12},{15,16},{19,20},{23,24},{27,28},{4,3},{8,7},{1... | collective-permute-start | bytes 2482184 | tf_op jit(solution)/shard_map/ppermute | solution.py:536
  23.4 1.8 %collective-permute-start.5 = (bf16[256,768]{1,0:T(8,128)(2,1)S(1)}, bf16[256,768]{1,0:T(8,128)(2,1)S(1)}, u32[]{:S(2)}, u32[]{:S(2)}) collective-permute-start(bf16[256,768]{1,0:T(8,128)(2,1)S(1)} %join.7.block_ref), channel_id=1, source_target_pairs={{0,1},{1,0},{2,3},{3,2},{4,5},{5,4},{6,7},{7,6},{8,9},{9,8},{10,11... | collective-permute-start | bytes 1179656 | tf_op jit(solution)/shard_map/ppermute | solution.py:524
  26.9 2.5 %collective-permute-start.6 = (f32[32,256]{1,0:T(8,128)S(1)}, f32[32,256]{1,0:T(8,128)S(1)}, u32[]{:S(2)}, u32[]{:S(2)}) collective-permute-start(f32[32,256]{1,0:T(8,128)S(1)} %own.1), channel_id=1, source_target_pairs={{0,1},{1,0},{2,3},{3,2},{4,5},{5,4},{6,7},{7,6},{8,9},{9,8},{10,11... | collective-permute-start | bytes 98312 | tf_op jit(solution)/shard_map/ppermute | solution.py:607
  27.2 16.3 %collective-permute-start.11 = (bf16[808,512]{1,0:T(8,128)(2,1)S(1)}, bf16[808,512]{1,0:T(8,128)(2,1)S(1)}, u32[]{:S(2)}, u32[]{:S(2)}) collective-permute-start(bf16[808,512]{1,0:T(8,128)(2,1)S(1)} %cut_chip.3), channel_id=1, source_target_pairs={{1,2},{5,6},{9,10},{13,14},{17,18},{21,22},{25,26},{29,30},{2,1},{... | collective-permute-start | bytes 2482184 | tf_op jit(solution)/shard_map/ppermute | solution.py:612
  29.4 24.8 %copy-start = (f32[30,64,64]{2,1,0:T(8,128)S(1)}, f32[30,64,64]{2,1,0:T(8,128)}, u32[]{:S(2)}) copy-start(f32[30,64,64]{2,1,0:T(8,128)} %core_ref.1) | copy-start | bytes 1474564
  33.6 4.0 %collective-permute-start.8 = (f32[32,256]{1,0:T(8,128)S(1)}, f32[32,256]{1,0:T(8,128)S(1)}, u32[]{:S(2)}, u32[]{:S(2)}) collective-permute-start(f32[32,256]{1,0:T(8,128)S(1)} %select_select_fusion.4), channel_id=1, source_target_pairs={{0,8},{1,9},{2,10},{3,11},{4,12},{5,13},{6,14},{7,15},{8,0},{9,1},... | collective-permute-start | bytes 98312 | tf_op jit(solution)/shard_map/ppermute | solution.py:607
  37.6 5.1 %collective-permute-start.9 = (f32[32,256]{1,0:T(8,128)S(1)}, f32[32,256]{1,0:T(8,128)S(1)}, u32[]{:S(2)}, u32[]{:S(2)}) collective-permute-start(f32[32,256]{1,0:T(8,128)S(1)} %select_select_fusion.3), channel_id=1, source_target_pairs={{0,16},{1,17},{2,18},{3,19},{4,20},{5,21},{6,22},{7,23},{8,24},{9,... | collective-permute-start | bytes 98312 | tf_op jit(solution)/shard_map/ppermute | solution.py:607
  42.7 4.0 %collective-permute-start.10 = (f32[32,256]{1,0:T(8,128)S(1)}, f32[32,256]{1,0:T(8,128)S(1)}, u32[]{:S(2)}, u32[]{:S(2)}) collective-permute-start(f32[32,256]{1,0:T(8,128)S(1)} %select_select_fusion.2), channel_id=1, source_target_pairs={{0,4},{1,5},{2,6},{3,7},{4,0},{5,1},{6,2},{7,3},{8,12},{9,13},{10,... | collective-permute-start | bytes 98312 | tf_op jit(solution)/shard_map/ppermute | solution.py:607
  46.7 4.0 %collective-permute-start.12 = (f32[32,256]{1,0:T(8,128)S(1)}, f32[32,256]{1,0:T(8,128)S(1)}, u32[]{:S(2)}, u32[]{:S(2)}) collective-permute-start(f32[32,256]{1,0:T(8,128)S(1)} %select_select_fusion.1), channel_id=1, source_target_pairs={{0,2},{1,3},{2,0},{3,1},{4,6},{5,7},{6,4},{7,5},{8,10},{9,11},{10,... | collective-permute-start | bytes 98312 | tf_op jit(solution)/shard_map/ppermute | solution.py:607
  46.8 7.4 %collective-permute-start.13 = (f32[32,512]{1,0:T(8,128)S(1)}, f32[32,512]{1,0:T(8,128)S(1)}, u32[]{:S(2)}, u32[]{:S(2)}) collective-permute-start(f32[32,512]{1,0:T(8,128)S(1)} %get-tuple-element.94), channel_id=1, source_target_pairs={{1,2},{5,6},{9,10},{13,14},{17,18},{21,22},{25,26},{29,30},{3,4},{... | collective-permute-start | bytes 196616 | tf_op jit(solution)/shard_map/ppermute | solution.py:617
